TPU v7x, 32 devices: a whole 2x2x4 slice. The times are simulated.
32 devices in a mesh: fsdp: 4 (over z), ctx: 4 (over y, core), tp: 2 (over x).
Axes of the slice: x: 2, y: 2, z: 4, core: 2. Of those that a mesh axis runs over, the one named last changes fastest.
Arguments:
- tokens: bfloat16 [4, 512, 1536], P('fsdp', 'ctx'), may hold values from -6 to 6
- cotangent: bfloat16 [4, 512, 1536], P('fsdp', 'ctx'), may hold values from -6 to 6
- prefix: int32 [4], P('fsdp'), may hold values from 51 to 256
- norm_one: bfloat16 [1536], P(('fsdp', 'ctx')), may hold values from 0.25 to 1.75
- w_query: bfloat16 [1536, 768], P(('fsdp', 'ctx'), 'tp'), may hold values from -0.078125 to 0.078125
- w_key: bfloat16 [1536, 768], P(('fsdp', 'ctx'), 'tp'), may hold values from -0.078125 to 0.078125
- value_projection_weight: bfloat16 [1536, 768], P(('fsdp', 'ctx'), 'tp'), may hold values from -0.15625 to 0.15625
- w_out: bfloat16 [768, 1536], P('tp', ('fsdp', 'ctx')), may hold values from -1.25 to 1.25
- position_bias_matrix: bfloat16 [12, 32], P('tp'), may hold values from -3 to 3
- norm_two: bfloat16 [1536], P(('fsdp', 'ctx')), may hold values from 0.25 to 1.75
- w_gate: bfloat16 [1536, 3968], P(('fsdp', 'ctx'), 'tp'), may hold values from -0.15625 to 0.15625
- w_up: bfloat16 [1536, 3968], P(('fsdp', 'ctx'), 'tp'), may hold values from -0.15625 to 0.15625
- w_down: bfloat16 [3968, 1536], P('tp', ('fsdp', 'ctx')), may hold values from -0.09375 to 0.09375
Outputs:
- mixed: bfloat16 [4, 512, 1536], P('fsdp', 'ctx')
- input_grad: bfloat16 [4, 512, 1536], P('fsdp', 'ctx')
- grad_norm_one: float32 [1536], P(('fsdp', 'ctx'))
- grad_query: float32 [1536, 768], P(('fsdp', 'ctx'), 'tp')
- grad_key: float32 [1536, 768], P(('fsdp', 'ctx'), 'tp')
- grad_value: float32 [1536, 768], P(('fsdp', 'ctx'), 'tp')
- grad_out: float32 [768, 1536], P('tp', ('fsdp', 'ctx'))
- grad_table: float32 [12, 32], P('tp')
- grad_norm_two: float32 [1536], P(('fsdp', 'ctx'))
- grad_gate: float32 [1536, 3968], P(('fsdp', 'ctx'), 'tp')
- grad_up: float32 [1536, 3968], P(('fsdp', 'ctx'), 'tp')
- grad_down: float32 [3968, 1536], P('tp', ('fsdp', 'ctx'))
Inputs may be any that keep to these rules, and one draw needn't show every extreme that they name: `prefix`: each sequence's number of leading bytes that all of its bytes see.
All inputs are finite; a program needn't handle non-finite values.
Results may differ from a plain program's by a relative error of at most 0.019.
Values may be sent and summed in bfloat16 or wider, within the bound.
No kernel may reach another device: no remote copies, remote signals or barrier semaphores. Data moves between devices by JAX's collectives and lax.ppermute only.
A program may use at most 192 MiB of HBM per device.

v0:
```python
import functools

import jax
import jax.numpy as jnp
import numpy as np
from jax import lax
from jax.experimental import pallas as pl
from jax.experimental.pallas import tpu as pltpu
from jax.sharding import Mesh, PartitionSpec as P

epsilon = 1e-06
masked_value = -1e30
far_bounds = (12, 16, 23, 32, 46, 64, 91)
f32 = jnp.float32
bf16 = jnp.bfloat16
lane = 128
ffn_order = (2, 3, 0, 1, 4, 5)
attn_order = (4, 2, 1, 0, 3, 5)
at_k, at_yl, at_zl, at_zh, at_yh, at_prefix, at_lists = range(7)


def bucket_of(relative, buckets):
    offset = jnp.abs(relative)
    far = jnp.full(offset.shape, buckets // 4, jnp.int32)
    for threshold in far_bounds:
        far = far + (offset >= threshold).astype(jnp.int32)
    return jnp.where(offset < buckets // 4, offset, far) + buckets // 2 * (relative > 0).astype(
        jnp.int32
    )


def dot(left, right, dims=((1,), (0,))):
    return lax.dot_general(left, right, (dims, ((), ())), preferred_element_type=f32)


def dot_nt(left, right):
    return dot(left, right, ((1,), (1,)))


def dot_tn(left, right):
    return dot(left, right, ((0,), (0,)))


def fetch(value, axis, step):
    size = lax.axis_size(axis)
    return lax.ppermute(value, axis, [((i + step) % size, i) for i in range(size)])


def swap(value, axis):
    return fetch(value, axis, 1)


def gather(value, axis):
    return [value] + [fetch(value, axis, e) for e in range(1, lax.axis_size(axis))]


def send_sums(sends, axis):
    size = lax.axis_size(axis)
    return [fetch(sends[e - 1], axis, size - e) for e in range(1, size)]


def place(pieces, axis):
    size, here = len(pieces), lax.axis_index(axis)
    if size == 1:
        return pieces[0][None]
    if size == 2:
        first = here == 0
        return jnp.stack(
            [jnp.where(first, pieces[0], pieces[1]), jnp.where(first, pieces[1], pieces[0])]
        )
    stack = jnp.zeros((size, *pieces[0].shape), pieces[0].dtype)
    for e, piece in enumerate(pieces):
        stack = lax.dynamic_update_slice_in_dim(stack, piece[None], (here + e) % size, 0)
    return stack


def both(value, axis):
    return place(gather(value, axis), axis)


class Clock:
    def __init__(self, token):
        self.token = token

    def tick(self, *values):
        self.token, *values = lax.optimization_barrier((self.token, *values))
        return values


def runs_of(dims, order, inverse):
    index = np.arange(int(np.prod(dims))).reshape(dims).transpose(order).reshape(-1)
    if inverse:
        index = np.argsort(index)
    cuts = [0, *(np.flatnonzero(np.diff(index) != 1) + 1).tolist(), len(index)]
    return [(int(index[a]), int(index[a]) + b - a) for a, b in zip(cuts[:-1], cuts[1:])]


def reorder(value, dims, order, inverse=False):
    return jnp.concatenate([value[:, a:b] for a, b in runs_of(dims, order, inverse)], axis=1)


def inv_scale(values):
    return lax.rsqrt(jnp.mean(values * values, axis=-1, keepdims=True) + epsilon)


def norm_back(scale, normed, grad_normed):
    return scale * (grad_normed - normed * jnp.mean(grad_normed * normed, axis=-1, keepdims=True))


def aligned(index, size):
    return pl.ds(pl.multiple_of(index * size, size), size)


def call(body, name, here, arrays, outs, scratch=(), **static):
    space = pl.BlockSpec(memory_space=pltpu.VMEM)
    return pl.pallas_call(
        functools.partial(body, **static),
        out_shape=tuple(jax.ShapeDtypeStruct(shape, kind) for shape, kind in outs),
        in_specs=[pl.BlockSpec(memory_space=pltpu.SMEM)] + [space] * len(arrays),
        out_specs=tuple(space for _ in outs),
        scratch_shapes=scratch,
        name=name,
    )(here, *arrays)


def pack_attn_body(here, wq, wk, wv, wo, own, send):
    half = wq.shape[1] // 2
    mats = [wq[...], wk[...], wv[...], wo[...].astype(f32).T.astype(bf16)]
    low = jnp.concatenate([m[:, :half] for m in mats], axis=1)
    high = jnp.concatenate([m[:, half:] for m in mats], axis=1)

    @pl.when(here[at_yl] == 0)
    def _():
        own[...] = low
        send[...] = high

    @pl.when(here[at_yl] != 0)
    def _():
        own[...] = high
        send[...] = low


def pack_ffn_body(here, wg, wu, wd, own, send, room, *, chunks):
    hidden = wg.shape[1]
    whole = hidden // lane * lane
    room[:, :, whole:] = jnp.zeros((3, wg.shape[0], 4 * chunks * lane - whole), bf16)
    room[0, :, :hidden] = wg[...]
    room[1, :, :hidden] = wu[...]
    room[2, :, :hidden] = wd[...].astype(f32).T.astype(bf16)
    for out, core in ((own, here[at_k]), (send, 1 - here[at_k])):
        for h in range(2):
            for j in range(chunks):
                for m in range(3):
                    out[h, j, :, m * lane : (m + 1) * lane] = room[
                        m, :, aligned((2 * h + core) * chunks + j, lane)
                    ]


def place_ffn_body(here, own, got, near, other, *, chunks):
    k, zl = here[at_k], here[at_zl]
    for j in range(chunks):
        near[j, k] = own[zl, j]
        near[j, 1 - k] = got[zl, j]
        other[j, k] = own[1 - zl, j]
        other[j, 1 - k] = got[1 - zl, j]


def place_zl_body(here, near, got, *outs):
    zl = here[at_zl]
    for j, out in enumerate(outs):
        out[zl] = near[j]
        out[1 - zl] = got[j]


def rows_body(here, gain, cotangent, *refs, dims):
    *blocks, out, low_grad = refs
    rows = cotangent.shape[0]
    low_grad[...] = reorder(cotangent[...].astype(f32), dims, ffn_order).astype(bf16)
    for at, block in enumerate(blocks):
        values = block[...].astype(f32)
        values = values * inv_scale(values) * gain[...]
        out[at * rows : (at + 1) * rows] = reorder(values, dims, attn_order).astype(bf16)


def bias_block(line_ref, head, start, rows):
    line = line_ref[pl.ds(head, 1), pl.ds(pl.multiple_of(start, rows), 2 * rows)]
    spread = jnp.broadcast_to(line, (rows, 2 * rows))
    return pltpu.roll(spread, 0, 1, stride=1, stride_axis=0)[:, rows:]


def attend_body(
    here, inputs, w_own, w_other, lines, qkv, probs_out, attended, keep, send, *, sizes
):
    rows, heads, width, query_blocks, key_blocks, span = sizes
    prefix = here[at_prefix]
    inner = heads * width
    half = w_own.shape[0]
    places = [here[at_lists + i] for i in range(key_blocks)]
    mine, other = aligned(here[at_k], half), aligned(1 - here[at_k], half)
    qkv[...] = (
        dot(inputs[:, mine], w_own[:, : 3 * inner]) + dot(inputs[:, other], w_other[:, : 3 * inner])
    ).astype(bf16)
    for head in range(heads):
        lanes = slice(head * width, (head + 1) * width)
        keys = qkv[:, inner + head * width : inner + (head + 1) * width]
        values = qkv[:, 2 * inner + head * width : 2 * inner + (head + 1) * width]
        for at, block in enumerate(query_blocks):
            query_block = places[block]
            queries = qkv[block * rows : (block + 1) * rows, lanes]
            raw = dot_nt(queries, keys)
            query_pos = query_block * rows + lax.broadcasted_iota(jnp.int32, (rows, rows), 0)
            parts = []
            for key_at, key_block in enumerate(places):
                start = (key_block - query_block) * rows + span - rows
                key_pos = key_block * rows + lax.broadcasted_iota(jnp.int32, (rows, rows), 1)
                allowed = (key_pos <= query_pos) | (key_pos < prefix)
                biased = raw[:, key_at * rows : (key_at + 1) * rows] + bias_block(
                    lines, head, start, rows
                )
                parts.append(jnp.where(allowed, biased, masked_value))
            scores = jnp.concatenate(parts, axis=1)
            top = jnp.max(scores, axis=1, keepdims=True)
            powers = jnp.exp(scores - top)
            probs = powers / jnp.sum(powers, axis=1, keepdims=True)
            probs_out[head, at * rows : (at + 1) * rows, :] = probs
            attended[at * rows : (at + 1) * rows, lanes] = dot(probs.astype(bf16), values).astype(
                bf16
            )
    for lanes, weights in ((mine, w_own), (other, w_other)):
        out = dot_nt(attended[...], weights[:, 3 * inner :])
        keep[:, lanes] = out[:rows]
        send[:, lanes] = out[rows:].astype(bf16)


def norm_body(here, own, got, tokens, gain, residual, low, *, dims):
    total = own[...].astype(f32) + got[...].astype(f32)
    values = tokens[...].astype(f32) + reorder(total, dims, attn_order, True)
    residual[...] = values
    low[...] = reorder(values * inv_scale(values) * gain[...], dims, ffn_order).astype(bf16)


def tall(refs, lanes):
    return jnp.concatenate([ref[:, lanes] for ref in refs], axis=0)


def ffn_body(here, *refs, where):
    rows, grads, weights, (first_out, hidden_out) = refs[:4], refs[4:8], refs[8:-2], refs[-2:]
    size = weights[0].shape[0]
    first, d_hidden = None, None
    for at, w in enumerate(weights):
        lanes = aligned(here[where + at], size)
        first_part = dot(tall(rows, lanes), w[:, : 2 * lane])
        d_part = dot(tall(grads, lanes), w[:, 2 * lane :])
        first = first_part if first is None else first + first_part
        d_hidden = d_part if d_hidden is None else d_hidden + d_part
    gate, up = first[:, :lane], first[:, lane:]
    root = float(np.sqrt(2.0 / np.pi))
    square = gate * gate
    bend = jnp.tanh(root * gate * (1.0 + 0.044715 * square))
    half = 0.5 * (1.0 + bend)
    active = gate * half
    slope = half + 0.5 * gate * (1.0 - bend * bend) * (root * (1.0 + 3.0 * 0.044715 * square))
    hidden_out[...] = (active * up).astype(bf16)
    first_out[:, :lane] = (d_hidden * up * slope).astype(bf16)
    first_out[:, lane:] = (d_hidden * active).astype(bf16)


def back_body(here, *refs, where, chunks, lanes):
    lefts, weights, (keep, send) = refs[:chunks], refs[chunks:-2], refs[-2:]
    blocks = len(weights) // chunks
    size, rows = weights[0].shape[0], keep.shape[1]
    for at in range(blocks):
        total = None
        for j in range(chunks):
            part = dot_nt(lefts[j][...], weights[j * blocks + at][:, lanes])
            total = part if total is None else total + part
        here_lanes = aligned(here[where + at], size)
        for a in range(2):
            keep[a, :, here_lanes] = total[2 * a * rows : (2 * a + 1) * rows]
            send[a, :, here_lanes] = total[(2 * a + 1) * rows : (2 * a + 2) * rows].astype(bf16)


def ffn_grad_body(here, *refs, outer):
    rows, grads, (first, hidden, keep, send) = refs[:4], refs[4:8], refs[8:]
    size = keep.shape[1]
    for e in range(outer):
        yh = here[at_yh] + e
        yh = jnp.where(yh >= outer, yh - outer, yh) * 2
        for out, y in ((keep, yh + here[at_yl]), (send, yh + 1 - here[at_yl])):
            lanes = aligned(y, size)
            out[e, :, : 2 * lane] = dot_tn(tall(rows, lanes), first[...]).astype(out.dtype)
            out[e, :, 2 * lane :] = dot_tn(tall(grads, lanes), hidden[...]).astype(out.dtype)


def split_body(here, own, *refs, which):
    *got, keep, send = refs
    count = own.shape[0]
    for e in range(count):
        at = here[which] + e
        at = jnp.where(at >= count, at - count, at)
        total = own[at]
        for ref in got:
            total = total + ref[at].astype(f32)
        if e:
            send[e - 1] = total.astype(bf16)
        else:
            keep[...] = total


def split(here, which, own, got):
    shape = own.shape[1:]
    return call(
        split_body,
        "split",
        here,
        [own, *(g.reshape(own.shape) for g in got)],
        [(shape, f32), ((own.shape[0] - 1, *shape), bf16)],
        which=which,
    )


def ffn_split_body(here, *refs, chunks):
    done, core, other = refs[-3:]
    each = (len(refs) - 3) // chunks
    zl, k = here[at_zl], here[at_k]
    for j in range(chunks):
        own, *got = refs[j * each : (j + 1) * each]

        def total(depth, slice_):
            value = own[depth, slice_]
            for ref in got:
                value = value + ref[depth, slice_].astype(f32)
            return value

        done[j] = total(zl, k)
        core[j] = total(zl, 1 - k).astype(bf16)
        other[j, 0] = total(1 - zl, 0).astype(bf16)
        other[j, 1] = total(1 - zl, 1).astype(bf16)


def ffn_final_body(here, done, core, other, far, wg, wu, gain, grad_g, grad_u, grad_d, grad_gain, room):
    chunks, part, hidden = done.shape[0], done.shape[1], wg.shape[1]
    zl, k = here[at_zl], here[at_k]
    for j in range(chunks):
        for h, c, value in (
            (zl, k, done[j]),
            (1 - zl, k, other[j, k].astype(f32)),
            (zl, 1 - k, core[j].astype(f32)),
            (1 - zl, 1 - k, far[j, k].astype(f32)),
        ):
            for m in range(3):
                room[m, :, aligned((2 * h + c) * chunks + j, lane)] = value[
                    :, m * lane : (m + 1) * lane
                ]
    gate, up = room[0, :, :hidden], room[1, :, :hidden]
    grad_g[...] = gate
    grad_u[...] = up
    grad_d[...] = room[2].T[:hidden]
    sums = gate * wg[...].astype(f32) + up * wu[...].astype(f32)
    grad_gain[...] = jnp.sum(sums, axis=1, keepdims=True) / gain[...]


def pair_body(here, own, got, keep, send):
    keep[...] = own[0] + got[0].astype(f32)
    send[...] = (own[1] + got[1].astype(f32)).astype(bf16)


def residual_back_body(here, own, got, residual, cotangent, gain, d_residual, d_low, *, dims):
    total = own[...].astype(f32) + got[...].astype(f32)
    grad_normed = reorder(total, dims, ffn_order, True) * gain[...]
    values = residual[...]
    scale = inv_scale(values)
    back = cotangent[...].astype(f32) + norm_back(scale, values * scale, grad_normed)
    d_residual[...] = back
    d_low[...] = reorder(back, dims, attn_order).astype(bf16)


def attend_back_body(
    here, qkv, probs_in, d_own, d_far, w_own, w_other, d_query, d_keep, d_send, lines, d_att, *, sizes
):
    rows, heads, width, query_blocks, key_blocks, span = sizes
    inner = heads * width
    half = w_own.shape[0]
    places = [here[at_lists + i] for i in range(key_blocks)]
    mine, other = aligned(here[at_k], half), aligned(1 - here[at_k], half)
    d_rows = (d_own, d_far)
    d_att[...] = (
        dot(tall(d_rows, mine), w_own[:, 3 * inner :])
        + dot(tall(d_rows, other), w_other[:, 3 * inner :])
    ).astype(bf16)
    lines[...] = jnp.zeros_like(lines)
    up, down = (lax.broadcasted_iota(jnp.int32, (rows, rows), axis) for axis in (0, 1))
    flip = (up + down == rows - 1).astype(bf16)
    for head in range(heads):
        lanes = slice(head * width, (head + 1) * width)
        value_lanes = slice(inner + head * width, inner + (head + 1) * width)
        keys = qkv[:, inner + head * width : inner + (head + 1) * width]
        values = qkv[:, 2 * inner + head * width : 2 * inner + (head + 1) * width]
        d_key, d_value = None, None
        for at, block in enumerate(query_blocks):
            queries = qkv[block * rows : (block + 1) * rows, lanes]
            d_attended = d_att[at * rows : (at + 1) * rows, lanes]
            probs = probs_in[head, at * rows : (at + 1) * rows, :]
            d_probs = dot_nt(d_attended, values)
            delta = jnp.sum(probs * d_probs, axis=1, keepdims=True)
            d_scores = (probs * (d_probs - delta)).astype(bf16)
            d_query[at * rows : (at + 1) * rows, lanes] = dot(d_scores, keys).astype(bf16)
            key_part = dot_tn(d_scores, queries)
            value_part = dot_tn(probs.astype(bf16), d_attended)
            d_key = key_part if d_key is None else d_key + key_part
            d_value = value_part if d_value is None else d_value + value_part
            upward = dot(flip, d_scores)
            for key_at, key_block in enumerate(places):
                start = (key_block - places[block]) * rows + span - rows
                piece = upward[:, key_at * rows : (key_at + 1) * rows]
                padded = jnp.concatenate([piece, jnp.zeros_like(piece)], axis=1)
                turned = pltpu.roll(padded, 1, 1, stride=1, stride_axis=0)
                span_at = pl.ds(pl.multiple_of(start, rows), 2 * rows)
                lines[pl.ds(head, 1), span_at] += jnp.sum(turned, axis=0, keepdims=True)
        for key_at in range(key_blocks):
            from_, to = slice(key_at * rows, (key_at + 1) * rows), key_at // 2
            for out, parity in ((d_keep, 0), (d_send, 1)):
                if key_at % 2 == parity:
                    out[to, :, lanes] = d_key[from_].astype(out.dtype)
                    out[to, :, value_lanes] = d_value[from_].astype(out.dtype)


def attn_grad_body(
    here, inputs, d_query, d_keep, d_got, d_own, d_far, attended, w_own, w_other,
    g_keep, g_send, keep, send, d_qkv, *, sizes
):
    rows, heads, width, query_blocks, key_blocks, span = sizes
    inner = heads * width
    half = w_own.shape[0]
    mine, other = aligned(here[at_k], half), aligned(1 - here[at_k], half)
    d_qkv[:, :inner] = d_query[...]
    for at in range(2):
        d_qkv[at * rows : (at + 1) * rows, inner:] = (d_keep[at] + d_got[at].astype(f32)).astype(bf16)
    for lanes, weights, out in ((mine, w_own, keep), (other, w_other, send)):
        part = dot_nt(d_qkv[...], weights[:, : 3 * inner])
        g_keep[:, lanes] = part[:rows]
        g_send[:, lanes] = part[rows:].astype(bf16)
        two = jnp.concatenate([inputs[b * rows : (b + 1) * rows, lanes] for b in query_blocks], axis=0)
        out[:, : 3 * inner] = dot_tn(two, d_qkv[...]).astype(out.dtype)
        out[:, 3 * inner :] = dot_tn(tall((d_own, d_far), lanes), attended[...]).astype(out.dtype)


def input_grad_body(here, own, got, tokens, gain, d_residual, out, *, dims):
    total = own[...].astype(f32) + got[...].astype(f32)
    grad_normed = reorder(total, dims, attn_order, True) * gain[...]
    values = tokens[...].astype(f32)
    scale = inv_scale(values)
    out[...] = (d_residual[...] + norm_back(scale, values * scale, grad_normed)).astype(bf16)


def mixed_body(here, own, got, residual, out, *, dims):
    total = own[...].astype(f32) + got[...].astype(f32)
    out[...] = (residual[...] + reorder(total, dims, ffn_order, True)).astype(bf16)


def attn_final_body(here, own, got, wq, wk, wv, gain, gq, gk, gv, go, grad_gain):
    inner = own.shape[1] // 4

    def finish(low, high):
        grads = [
            jnp.concatenate([m[:, i * inner : (i + 1) * inner] for m in (low, high)], axis=1)
            for i in range(4)
        ]
        sums = 0.0
        for out, weights, grad in ((gq, wq, grads[0]), (gk, wk, grads[1]), (gv, wv, grads[2])):
            out[...] = grad
            sums = sums + jnp.sum(grad * weights[...].astype(f32), axis=1, keepdims=True)
        go[...] = grads[3].T
        grad_gain[...] = sums / gain[...]

    @pl.when(here[at_yl] == 0)
    def _():
        finish(own[...], got[...].astype(f32))

    @pl.when(here[at_yl] != 0)
    def _():
        finish(got[...].astype(f32), own[...])


def local(
    tokens,
    cotangent,
    prefix,
    norm_one,
    w_query,
    w_key,
    w_value,
    w_out,
    position_bias_matrix,
    norm_two,
    w_gate,
    w_up,
    w_down,
):
    tick = Clock(prefix).tick
    outer, deep = lax.axis_size("yh"), lax.axis_size("zh")
    rows, wide = tokens.shape[1:]
    part = w_query.shape[0]
    heads_dev, buckets = position_bias_matrix.shape
    heads = heads_dev // 2
    width = w_query.shape[1] // heads_dev
    inner = heads * width
    hidden_dev = w_gate.shape[1]
    chunks = -(-hidden_dev // (4 * lane))
    length = rows * outer * 4
    dims = (deep, 2, outer, 2, 2, part)
    half = wide // 2
    key_blocks = 4 * outer
    sizes = (rows, heads, width, (0, 2), key_blocks, length)

    split_deep = deep == 2 and (4 * part) % lane == 0
    deep_blocks = deep if split_deep else 1
    yh, yl, k, zl, zh = (lax.axis_index(a) for a in ("yh", "yl", "k", "zl", "zh"))
    relative = [(e, a) for a in range(2) for e in range(outer)]
    ys = [((yh + e) % outer) * 2 + (yl + a) % 2 for e, a in relative]
    where = at_lists + key_blocks
    here = [k, yl, zl, zh, yh, prefix[0]]
    here += [
        ((yh + e) % outer) * 4 + ((yl + a) % 2) * 2 + (k + b) % 2
        for e in range(outer)
        for a in range(2)
        for b in range(2)
    ]
    here += [y * deep_blocks + (zh + d) % deep_blocks for d in range(deep_blocks) for y in ys]
    here = jnp.stack([jnp.asarray(v, jnp.int32) for v in here])

    own, send = call(
        pack_attn_body,
        "pack_attn",
        here,
        [w_query, w_key, w_value, w_out],
        [((part, 4 * inner), bf16)] * 2,
    )
    own, send, gains, w_gate_in, w_up_in, w_down_in = tick(
        own, send, jnp.stack([norm_one, norm_two]), w_gate, w_up, w_down
    )
    pack = place([own, swap(send, "yl")], "yl")
    gains = both(both(gains, "zl"), "zh")
    pack, gains, w_gate_in, w_up_in, w_down_in, own_tokens = tick(
        pack, gains, w_gate_in, w_up_in, w_down_in, tokens[0]
    )

    own, send = call(
        pack_ffn_body,
        "pack_ffn",
        here,
        [w_gate_in, w_up_in, w_down_in],
        [((2, chunks, part, 3 * lane), bf16)] * 2,
        [pltpu.VMEM((3, part, 4 * chunks * lane), bf16)],
        chunks=chunks,
    )
    gains = both(both(gains, "yl"), "yh")
    far_tokens = swap(own_tokens, "yl")
    near, near_send = call(
        place_ffn_body,
        "place_ffn",
        here,
        [own, swap(send, "k")],
        [((chunks, 2, part, 3 * lane), bf16)] * 2,
        chunks=chunks,
    )
    pack, near, near_send, gains, far_tokens, own_tokens = tick(
        both(pack, "zh"), near, near_send, gains, far_tokens, own_tokens
    )

    gains = both(gains, "k")
    row_blocks = [p for pair in zip(gather(own_tokens, "yh"), gather(far_tokens, "yh")) for p in pair]
    row_blocks = [p for b in row_blocks for p in gather(b, "k")]
    near_got = swap(near_send, "zl")
    gains = gains.transpose(5, 3, 4, 1, 2, 0, 6).reshape(2, wide).astype(f32)
    gain_one, gain_two = gains[:1], gains[1:]
    attn_input, low_grad = call(
        rows_body,
        "rows",
        here,
        [gain_one, cotangent[0], *row_blocks],
        [((length, wide), bf16), ((rows, wide), bf16)],
        dims=dims,
    )
    table = jnp.where(yl == 0, position_bias_matrix[:heads], position_bias_matrix[heads:])
    distance = jnp.arange(2 * length, dtype=jnp.int32) - length
    indicator = (
        bucket_of(distance, buckets)[None] == jnp.arange(buckets, dtype=jnp.int32)[:, None]
    ).astype(f32)
    lines = jnp.einsum("hb,bd->hd", table.astype(f32), indicator, precision="highest")
    lines = jnp.pad(lines, ((0, 8 - heads), (0, 0)))
    nears = call(
        place_zl_body,
        "place_zl",
        here,
        [near, near_got],
        [((2, 2, part, 3 * lane), bf16)] * chunks,
    )
    pack, attn_input, low_grad, lines, *nears = tick(both(pack, "zl"), attn_input, low_grad, lines, *nears)

    def to_blocks(values):
        return [v.reshape(-1, 3 * lane) for v in values]

    def over_zh(near):
        pieces = gather(near, "zh")
        return pieces if split_deep else [None, place(pieces, "zh")]

    def over_y(value):
        return to_blocks([p for b in gather(value, "yl") for p in gather(b, "yh")])

    near_y = [None] * chunks
    far = [None] * chunks
    far_y = [None] * chunks
    early = split_deep
    pack = both(pack, "yh").reshape(half, 4 * inner)
    w_own, w_other = gather(pack, "k")
    far[0] = over_zh(nears[0])[1]
    for j in (0, 1):
        near_y[j] = over_y(nears[j]) if early else []
    qkv, probs, attended, out_keep, out_send = call(
        attend_body,
        "attend",
        here,
        [attn_input, w_own, w_other, lines],
        [
            ((length, 3 * inner), bf16),
            ((heads, 2 * rows, length), f32),
            ((2 * rows, inner), bf16),
            ((rows, wide), f32),
            ((rows, wide), bf16),
        ],
        sizes=sizes,
    )

    out_keep, out_send, nears[1], nears[2], far[0], low_grad, *flat = tick(
        out_keep, out_send, nears[1], nears[2], far[0], low_grad, *near_y[0], *near_y[1]
    )
    near_y[0], near_y[1] = flat[: len(flat) // 2], flat[len(flat) // 2 :]
    out_sum = (out_keep + swap(out_send, "yl").astype(f32)).astype(bf16)
    far[1] = over_zh(nears[1])[1]
    near_y[2] = over_y(nears[2]) if early else []
    far_grad = swap(low_grad, "zl")
    core_grad = swap(low_grad, "k")
    out_sum, nears[2], nears[3], far[0], far[1], far_grad, core_grad = tick(
        out_sum, nears[2], nears[3], far[0], far[1], far_grad, core_grad
    )
    far[2] = over_zh(nears[2])[1]
    near_y[3] = over_y(nears[3]) if early else []
    far_y[0] = over_y(far[0])
    farcore_grad = swap(far_grad, "k")
    residual, low_two = call(
        norm_body,
        "norm",
        here,
        [out_sum, swap(out_sum, "x"), tokens[0], gain_two],
        [((rows, wide), f32), ((rows, wide), bf16)],
        dims=dims,
    )
    low_two, nears[3], far[1], far[2], farcore_grad, *flat = tick(
        low_two, nears[3], far[1], far[2], farcore_grad, *near_y[2], *near_y[3], *far_y[0]
    )
    count = len(near_y[2])
    near_y[2], near_y[3], far_y[0] = flat[:count], flat[count : 2 * count], flat[2 * count :]
    far_two, core_two = swap(low_two, "zl"), swap(low_two, "k")
    far[3] = over_zh(nears[3])[1]
    far_y[1], far_y[2] = over_y(far[1]), over_y(far[2])
    count = len(far_y[1])
    far_two, core_two, far[3], *flat = tick(far_two, core_two, far[3], *far_y[1], *far_y[2])
    far_y[1], far_y[2] = flat[:count], flat[count:]
    far_y[3] = over_y(far[3])

    ffn_rows = [low_two, core_two, far_two, swap(far_two, "k")]
    grad_rows = [low_grad, core_grad, far_grad, farcore_grad]
    firsts, hiddens = [], []
    for j in range(chunks):
        first, hidden = call(
            ffn_body,
            "ffn",
            here,
            [*ffn_rows, *grad_rows, *near_y[j], *far_y[j]],
            [((4 * rows, 2 * lane), bf16), ((4 * rows, lane), bf16)],
            where=where,
        )
        firsts.append(first)
        hiddens.append(hidden)
    weights = [w for j in range(chunks) for w in (*near_y[j], *far_y[j])]

    def back(lefts, lanes):
        return call(
            back_body,
            "back",
            here,
            [*lefts, *weights],
            [((2, rows, wide), f32), ((2, rows, wide), bf16)],
            where=where,
            chunks=chunks,
            lanes=lanes,
        )

    def ffn_grad(j):
        return call(
            ffn_grad_body,
            "ffn_grad",
            here,
            [*ffn_rows, *grad_rows, firsts[j], hiddens[j]],
            [((outer, half // outer, 3 * lane), kind) for kind in (f32, bf16)],
            outer=outer,
        )

    def sum_y(grads):
        keep, send = grads
        got = [swap(send, "yl")]
        if outer > 1:
            total = keep + got[0].astype(f32)
            got = send_sums([total[e].astype(bf16) for e in range(1, outer)], "yh")
            keep = total[0]
        return split(here, at_zh, keep.reshape(deep, 4 * part, 3 * lane), got)

    def sum_zh(pieces):
        keep, send = pieces
        got = send_sums([send[e] for e in range(deep - 1)], "zh")
        return [v.reshape(2, 2, part, 3 * lane) for v in (keep, *got)]

    def pair(keep, got):
        shape = keep.shape[1:]
        return call(pair_body, "pair", here, [keep, got], [(shape, f32), (shape, bf16)])

    grads = [None] * chunks
    keep, send = back(firsts, slice(0, 2 * lane))
    send, keep = tick(send, keep)
    grads[0] = ffn_grad(0)
    core_keep, core_send = pair(keep, swap(send, "k"))
    core_keep, core_send, *grads[0] = tick(core_keep, core_send, *grads[0])
    core = (core_keep + swap(core_send, "zl").astype(f32)).astype(bf16)
    grads[1] = ffn_grad(1)
    sums = [None] * chunks
    sums[0] = sum_y(grads[0])
    core, *flat = tick(core, *sums[0], *grads[1])
    sums[0], grads[1] = flat[:2], flat[2:]
    grads[2] = ffn_grad(2)
    zh_sums = [None] * chunks
    zh_sums[0] = sum_zh(sums[0])
    sums[1] = sum_y(grads[1])
    d_residual, d_low = call(
        residual_back_body,
        "residual_back",
        here,
        [core, swap(core, "x"), residual, cotangent[0], gain_two],
        [((rows, wide), f32), ((rows, wide), bf16)],
        dims=dims,
    )
    d_low, *flat = tick(d_low, *sums[1], *grads[2], *zh_sums[0])
    sums[1], grads[2], zh_sums[0] = flat[:2], flat[2:4], flat[4:]
    d_far = swap(d_low, "yl")
    zh_sums[1] = sum_zh(sums[1])
    grads[3] = ffn_grad(3)
    mixed_keep, mixed_send = back(hiddens, slice(2 * lane, 3 * lane))
    d_low, d_far, mixed_keep, mixed_send, *flat = tick(
        d_low, d_far, mixed_keep, mixed_send, *grads[2], *grads[3], *zh_sums[1]
    )
    grads[2], grads[3], zh_sums[1] = flat[:2], flat[2:4], flat[4:]

    sums[2] = sum_y(grads[2])
    mixed_keep, mixed_send = pair(mixed_keep, swap(mixed_send, "k"))
    d_query, d_keep, d_send, d_lines = call(
        attend_back_body,
        "attend_back",
        here,
        [qkv, probs, d_low, d_far, w_own, w_other],
        [
            ((2 * rows, inner), bf16),
            ((2 * outer, rows, 2 * inner), f32),
            ((2 * outer, rows, 2 * inner), bf16),
            ((8, 2 * length), f32),
        ],
        [pltpu.VMEM((2 * rows, inner), bf16)],
        sizes=sizes,
    )
    d_query, d_keep, d_send, d_lines, mixed_keep, mixed_send, *flat = tick(
        d_query, d_keep, d_send, d_lines, mixed_keep, mixed_send, *sums[2], *grads[3]
    )
    sums[2], grads[3] = flat[:2], flat[2:]
    sums[3] = sum_y(grads[3])
    zh_sums[2] = sum_zh(sums[2])
    d_got = swap(d_send, "k")
    if outer > 1:
        total = (d_keep + d_got.astype(f32)).reshape(outer, 2, rows, 2 * inner)
        arrived = send_sums([total[e].astype(bf16) for e in range(1, outer)], "yh")
        d_keep, d_got = total[0], sum(a.astype(f32) for a in arrived)
    g_keep, g_send, keep, send = call(
        attn_grad_body,
        "attn_grad",
        here,
        [attn_input, d_query, d_keep, d_got, d_low, d_far, attended, w_own, w_other],
        [
            ((rows, wide), f32),
            ((rows, wide), bf16),
            ((half, 4 * inner), f32),
            ((half, 4 * inner), bf16),
        ],
        [pltpu.VMEM((2 * rows, 3 * inner), bf16)],
        sizes=sizes,
    )
    got = [swap(send, "k")]
    if outer > 1:
        total = (keep + got[0].astype(f32)).reshape(outer, -1, 4 * inner)
        pieces = [lax.dynamic_index_in_dim(total, (yh + e) % outer, 0, False) for e in range(outer)]
        keep, got = pieces[0], send_sums([p.astype(bf16) for p in pieces[1:]], "yh")
    keep, send = split(here, at_zl, keep.reshape(2, deep * 2 * part, 4 * inner), got)
    g_keep, g_send, keep, send, *flat = tick(g_keep, g_send, keep, send, *sums[3], *zh_sums[2])
    sums[3], zh_sums[2] = flat[:2], flat[2:]
    g_sum = (g_keep + swap(g_send, "yl").astype(f32)).astype(bf16)
    got = send_sums([send[0]], "zl")
    zh_sums[3] = sum_zh(sums[3])
    keep, send = split(here, at_zh, keep.reshape(deep, 2 * part, 4 * inner), got)
    done, core_send, other_send = call(
        ffn_split_body,
        "ffn_split",
        here,
        [v for each in zh_sums for v in each],
        [
            ((chunks, part, 3 * lane), f32),
            ((chunks, part, 3 * lane), bf16),
            ((chunks, 2, part, 3 * lane), bf16),
        ],
        chunks=chunks,
    )
    keep, send, g_sum, done, core_send, other_send = tick(
        keep, send, g_sum, done, core_send, other_send
    )
    got = send_sums([send[e] for e in range(deep - 1)], "zh")
    other = swap(other_send, "zl")
    core_got = swap(core_send, "k")
    far_got = swap(other, "k")
    mixed_half = (mixed_keep + swap(mixed_send, "zl").astype(f32)).astype(bf16)
    (input_grad,) = call(
        input_grad_body,
        "input_grad",
        here,
        [g_sum, swap(g_sum, "x"), tokens[0], gain_one, d_residual],
        [((rows, wide), bf16)],
        dims=dims,
    )
    keep, send = split(here, at_yl, keep.reshape(2, part, 4 * inner), got)
    keep, send, mixed_half, input_grad = tick(keep, send, mixed_half, input_grad)
    got = swap(send[0], "yl")
    grad_gate, grad_up, grad_down, gain_two_part = call(
        ffn_final_body,
        "ffn_final",
        here,
        [done, core_got, other, far_got, w_gate, w_up, norm_two.astype(f32)[:, None]],
        [
            ((part, hidden_dev), f32),
            ((part, hidden_dev), f32),
            ((hidden_dev, part), f32),
            ((part, 1), f32),
        ],
        [pltpu.VMEM((3, part, 4 * chunks * lane), f32)],
    )
    (mixed,) = call(
        mixed_body,
        "mixed",
        here,
        [mixed_half, swap(mixed_half, "x"), residual],
        [((rows, wide), bf16)],
        dims=dims,
    )
    grad_query, grad_key, grad_value, grad_out, gain_one_part = call(
        attn_final_body,
        "attn_final",
        here,
        [keep, got, w_query, w_key, w_value, norm_one.astype(f32)[:, None]],
        [((part, 2 * inner), f32)] * 3 + [((2 * inner, part), f32), ((part, 1), f32)],
    )
    grad_gains = jnp.concatenate([gain_one_part, gain_two_part], 1).T
    grad_gains = grad_gains + swap(grad_gains, "x")

    grad_table = jnp.einsum("hd,bd->hb", d_lines[:heads], indicator, precision="highest")
    for axis in ("k", "yh", "zl", "zh"):
        grad_table = jnp.sum(both(grad_table, axis), axis=0)
    grad_table = both(grad_table, "yl").reshape(heads_dev, buckets)
    return (
        mixed[None],
        input_grad[None],
        grad_gains[0],
        grad_query,
        grad_key,
        grad_value,
        grad_out,
        grad_table,
        grad_gains[1],
        grad_gate,
        grad_up,
        grad_down,
    )


def solution(mesh):
    depths, lines, halves = (mesh.shape[a] for a in ("fsdp", "ctx", "tp"))
    fine = Mesh(
        mesh.devices.reshape(depths // 2, 2, lines // 4, 2, 2, halves),
        ("zh", "zl", "yh", "yl", "k", "x"),
    )
    depth, line = ("zh", "zl"), ("yh", "yl", "k")
    every = (*depth, *line)
    in_specs = (
        P(depth, line, None),
        P(depth, line, None),
        P(depth),
        P(every),
        P(every, "x"),
        P(every, "x"),
        P(every, "x"),
        P("x", every),
        P("x", None),
        P(every),
        P(every, "x"),
        P(every, "x"),
        P("x", every),
    )
    out_specs = (
        P(depth, line, None),
        P(depth, line, None),
        P(every),
        P(every, "x"),
        P(every, "x"),
        P(every, "x"),
        P("x", every),
        P("x", None),
        P(every),
        P(every, "x"),
        P(every, "x"),
        P("x", every),
    )
    return jax.shard_map(local, mesh=fine, in_specs=in_specs, out_specs=out_specs, check_vma=False)
```

profile of v0, /device:TPU:0, one launch (start us, length us, event | category | flops | bytes accessed | tf_op | source)
XLA Modules:
  0.0 379.5 jit_solution(3918856023416301074)
XLA Ops:
  26.3 8.7 %collective-permute-done.3 = bf16[2,96,768]{2,1,0:T(8,128)(2,1)S(1)} collective-permute-done((bf16[2,96,768]{2,1,0:T(8,128)(2,1)S(1)}, bf16[2,96,768]{2,1,0:T(8,128)(2,1)S(1)}, u32[]{:S(2)}, u32[]{:S(2)}) %collective-permute-start.3) | collective-permute-done | bytes 294944 | tf_op jit(solution)/shard_map/ppermute | solution.py:46
  47.3 7.3 %collective-permute-done.7 = bf16[2,2,96,768]{3,2,1,0:T(8,128)(2,1)S(1)} collective-permute-done((bf16[2,2,96,768]{3,2,1,0:T(8,128)(2,1)S(1)}, bf16[2,2,96,768]{3,2,1,0:T(8,128)(2,1)S(1)}, u32[]{:S(2)}, u32[]{:S(2)}) %collective-permute-start.7) | collective-permute-done | bytes 589856 | tf_op jit(solution)/shard_map/ppermute | solution.py:46
  54.8 10.3 %collective-permute-done.11.got = bf16[4,2,96,384]{3,2,1,0:T(8,128)(2,1)S(1)} collective-permute-done((bf16[4,2,96,384]{3,2,1,0:T(8,128)(2,1)}, bf16[4,2,96,384]{3,2,1,0:T(8,128)(2,1)S(1)}, u32[]{:S(2)}, u32[]{:S(2)}) %collective-permute-start.11) | collective-permute-done | bytes 589856 | tf_op jit(solution)/shard_map/ppermute | solution.py:46
  73.9 7.6 %attend.1 = (bf16[512,576]{1,0:T(8,128)(2,1)}, f32[3,256,512]{2,1,0:T(8,128)}, bf16[256,192]{1,0:T(8,128)(2,1)}, f32[128,1536]{1,0:T(8,128)}, bf16[128,1536]{1,0:T(8,128)(2,1)}) custom-call(s32[14]{0:T(128)} %stack.142.here, bf16[512,1536]{1,0:T(8,128)(2,1)} %get-tuple-element.242.inputs, bf16[768,768]{1,0:T(8,128)(2,1)} %bitcast.119, ...), custom_call_target="tpu_custom_call" | custom-call | tf_op jit(solution)/shard_map/attend/pallas_call | solution.py:116
  89.6 7.4 %collective-permute-done.16 = bf16[128,1536]{1,0:T(8,128)(2,1)S(1)} collective-permute-done((bf16[128,1536]{1,0:T(8,128)(2,1)}, bf16[128,1536]{1,0:T(8,128)(2,1)S(1)}, u32[]{:S(2)}, u32[]{:S(2)}) %collective-permute-start.16) | collective-permute-done | bytes 393248 | tf_op jit(solution)/shard_map/ppermute | solution.py:46
  98.3 7.0 %collective-permute-done.17 = bf16[2,2,96,384]{3,2,1,0:T(8,128)(2,1)S(1)} collective-permute-done((bf16[2,2,96,384]{3,2,1,0:T(8,128)(2,1)S(1)}, bf16[2,2,96,384]{3,2,1,0:T(8,128)(2,1)S(1)}, u32[]{:S(2)}, u32[]{:S(2)}) %collective-permute-start.17) | collective-permute-done | bytes 294944 | tf_op jit(solution)/shard_map/ppermute | solution.py:46
  109.5 6.6 %collective-permute-done.20.got = bf16[128,1536]{1,0:T(8,128)(2,1)S(1)} collective-permute-done((bf16[128,1536]{1,0:T(8,128)(2,1)S(1)}, bf16[128,1536]{1,0:T(8,128)(2,1)S(1)}, u32[]{:S(2)}, u32[]{:S(2)}) %collective-permute-start.20) | collective-permute-done | bytes 393248 | tf_op jit(solution)/shard_map/ppermute | solution.py:46
  124.0 4.9 %collective-permute-done.25 = bf16[2,2,96,384]{3,2,1,0:T(8,128)(2,1)S(1)} collective-permute-done((bf16[2,2,96,384]{3,2,1,0:T(8,128)(2,1)S(1)}, bf16[2,2,96,384]{3,2,1,0:T(8,128)(2,1)S(1)}, u32[]{:S(2)}, u32[]{:S(2)}) %collective-permute-start.25) | collective-permute-done | bytes 294944 | tf_op jit(solution)/shard_map/ppermute | solution.py:46
  132.5 11.6 %collective-permute-done.28 = bf16[2,2,96,384]{3,2,1,0:T(8,128)(2,1)} collective-permute-done((bf16[2,2,96,384]{3,2,1,0:T(8,128)(2,1)S(1)}, bf16[2,2,96,384]{3,2,1,0:T(8,128)(2,1)}, u32[]{:S(2)}, u32[]{:S(2)}) %collective-permute-start.28) | collective-permute-done | bytes 294944 | tf_op jit(solution)/shard_map/ppermute | solution.py:46
  153.1 4.4 %ffn.5 = (bf16[512,256]{1,0:T(8,128)(2,1)}, bf16[512,128]{1,0:T(8,128)(2,1)}) custom-call(s32[14]{0:T(128)} %stack.142.here, bf16[128,1536]{1,0:T(8,128)(2,1)} %get-tuple-element.267.refs_0_, bf16[128,1536]{1,0:T(8,128)(2,1)} %copy-done.5, bf16[128,1536]{1,0:T(8,128)(2,1)} %copy-done.4, bf16[128,1536]{1,0:T(8,128)(2,1)} %copy-done.6, ...), custom_call_target="tpu_custom_call" | custom-call | tf_op jit(solution)/shard_map/ffn/pallas_call | solution.py:116
  157.4 4.2 %ffn.6 = (bf16[512,256]{1,0:T(8,128)(2,1)}, bf16[512,128]{1,0:T(8,128)(2,1)}) custom-call(s32[14]{0:T(128)} %stack.142.here, bf16[128,1536]{1,0:T(8,128)(2,1)} %get-tuple-element.267.refs_0_, bf16[128,1536]{1,0:T(8,128)(2,1)} %copy-done.5, bf16[128,1536]{1,0:T(8,128)(2,1)} %copy-done.4, bf16[128,1536]{1,0:T(8,128)(2,1)} %copy-done.6, ...), custom_call_target="tpu_custom_call" | custom-call | tf_op jit(solution)/shard_map/ffn/pallas_call | solution.py:116
  166.6 6.3 %back.2 = (f32[2,128,1536]{2,1,0:T(8,128)}, bf16[2,128,1536]{2,1,0:T(8,128)(2,1)}) custom-call(s32[14]{0:T(128)} %stack.142.here, bf16[512,256]{1,0:T(8,128)(2,1)} %get-tuple-element.279.refs_0_.refs_8_, bf16[512,256]{1,0:T(8,128)(2,1)} %get-tuple-element.284.refs_1_.refs_8_, bf16[512,256]{1,0:T(8,128)(2,1)} %get-tuple-element.289.refs_2_.refs_8_, ...), custom_call_target="tpu_custom_call" | custom-call | tf_op jit(solution)/shard_map/back/pallas_call | solution.py:116
  186.6 5.4 %collective-permute-done.34 = bf16[128,1536]{1,0:T(8,128)(2,1)S(1)} collective-permute-done((bf16[128,1536]{1,0:T(8,128)(2,1)}, bf16[128,1536]{1,0:T(8,128)(2,1)S(1)}, u32[]{:S(2)}, u32[]{:S(2)}) %collective-permute-start.34) | collective-permute-done | bytes 393248 | tf_op jit(solution)/shard_map/ppermute | solution.py:46
  192.1 5.0 %collective-permute-done.35 = bf16[1,768,384]{2,1,0:T(8,128)(2,1)S(1)} collective-permute-done((bf16[1,768,384]{2,1,0:T(8,128)(2,1)}, bf16[1,768,384]{2,1,0:T(8,128)(2,1)S(1)}, u32[]{:S(2)}, u32[]{:S(2)}) %collective-permute-start.35) | collective-permute-done | bytes 589856 | tf_op jit(solution)/shard_map/ppermute | solution.py:46
  221.8 5.7 %back.3 = (f32[2,128,1536]{2,1,0:T(8,128)}, bf16[2,128,1536]{2,1,0:T(8,128)(2,1)}) custom-call(s32[14]{0:T(128)} %stack.142.here, bf16[512,128]{1,0:T(8,128)(2,1)} %get-tuple-element.300.refs_9_.refs_0_, bf16[512,128]{1,0:T(8,128)(2,1)} %get-tuple-element.309.refs_9_.refs_1_, bf16[512,128]{1,0:T(8,128)(2,1)} %get-tuple-element.319.refs_9_.refs_2_, ...), custom_call_target="tpu_custom_call" | custom-call | tf_op jit(solution)/shard_map/back/pallas_call | solution.py:116
  235.1 7.0 %attend_back.1 = (bf16[256,192]{1,0:T(8,128)(2,1)}, f32[2,128,384]{2,1,0:T(8,128)}, bf16[2,128,384]{2,1,0:T(8,128)(2,1)}, f32[8,1024]{1,0:T(8,128)}) custom-call(s32[14]{0:T(128)} %stack.142.here, bf16[512,576]{1,0:T(8,128)(2,1)} %get-tuple-element.245.qkv, f32[3,256,512]{2,1,0:T(8,128)} %get-tuple-element.246.probs_in, ...), custom_call_target="tpu_custom_call" | custom-call | tf_op jit(solution)/shard_map/attend_back/pallas_call | solution.py:116
  242.1 8.0 %collective-permute-done.42 = bf16[1,768,384]{2,1,0:T(8,128)(2,1)S(1)} collective-permute-done((bf16[1,768,384]{2,1,0:T(8,128)(2,1)}, bf16[1,768,384]{2,1,0:T(8,128)(2,1)S(1)}, u32[]{:S(2)}, u32[]{:S(2)}) %collective-permute-start.42) | collective-permute-done | bytes 589856 | tf_op jit(solution)/shard_map/ppermute | solution.py:46
  259.2 6.2 %attn_grad.1 = (f32[128,1536]{1,0:T(8,128)}, bf16[128,1536]{1,0:T(8,128)(2,1)}, f32[768,768]{1,0:T(8,128)}, bf16[768,768]{1,0:T(8,128)(2,1)}) custom-call(s32[14]{0:T(128)} %stack.142.here, bf16[512,1536]{1,0:T(8,128)(2,1)} %get-tuple-element.242.inputs, bf16[256,192]{1,0:T(8,128)(2,1)} %get-tuple-element.350.d_query, ...), custom_call_target="tpu_custom_call" | custom-call | tf_op jit(solution)/shard_map/attn_grad/pallas_call | solution.py:116
  266.7 14.4 %collective-permute-done.45 = bf16[1,768,384]{2,1,0:T(8,128)(2,1)S(1)} collective-permute-done((bf16[1,768,384]{2,1,0:T(8,128)(2,1)S(1)}, bf16[1,768,384]{2,1,0:T(8,128)(2,1)S(1)}, u32[]{:S(2)}, u32[]{:S(2)}) %collective-permute-start.45) | collective-permute-done | bytes 589856 | tf_op jit(solution)/shard_map/ppermute | solution.py:46
  294.6 10.3 %collective-permute-done.49 = bf16[384,384]{1,0:T(8,128)(2,1)S(1)} collective-permute-done((bf16[384,384]{1,0:T(8,128)(2,1)S(1)}, bf16[384,384]{1,0:T(8,128)(2,1)S(1)}, u32[]{:S(2)}, u32[]{:S(2)}) %collective-permute-start.49) | collective-permute-done | bytes 294944 | tf_op jit(solution)/shard_map/ppermute | solution.py:46
  309.0 11.0 %collective-permute-done.47 = bf16[384,768]{1,0:T(8,128)(2,1)S(1)} collective-permute-done((bf16[384,768]{1,0:T(8,128)(2,1)}, bf16[384,768]{1,0:T(8,128)(2,1)S(1)}, u32[]{:S(2)}, u32[]{:S(2)}) %collective-permute-start.47) | collective-permute-done | bytes 589856 | tf_op jit(solution)/shard_map/ppermute | solution.py:46
  327.0 7.8 %collective-permute-done.61 = f32[3,32]{1,0:T(4,128)S(1)} collective-permute-done((f32[3,32]{1,0:T(4,128)S(1)}, f32[3,32]{1,0:T(4,128)S(1)}, u32[]{:S(2)}, u32[]{:S(2)}) %collective-permute-start.61) | collective-permute-done | bytes 416 | tf_op jit(solution)/shard_map/ppermute | solution.py:46
  340.8 9.3 %collective-permute-done.50 = bf16[192,768]{1,0:T(8,128)(2,1)S(1)} collective-permute-done((bf16[192,768]{1,0:T(8,128)(2,1)}, bf16[192,768]{1,0:T(8,128)(2,1)S(1)}, u32[]{:S(2)}, u32[]{:S(2)}) %collective-permute-start.50) | collective-permute-done | bytes 294944 | tf_op jit(solution)/shard_map/ppermute | solution.py:46
  358.2 4.5 %collective-permute-done.54.got = bf16[96,768]{1,0:T(8,128)(2,1)S(1)} collective-permute-done((bf16[96,768]{1,0:T(8,128)(2,1)S(1)}, bf16[96,768]{1,0:T(8,128)(2,1)S(1)}, u32[]{:S(2)}, u32[]{:S(2)}) %collective-permute-start.54) | collective-permute-done | bytes 147488 | tf_op jit(solution)/shard_map/ppermute | solution.py:46
  (334 shorter events, 196.4 us)
Async XLA Ops:
  38.3 16.3 %collective-permute-start.7 = (bf16[2,2,96,768]{3,2,1,0:T(8,128)(2,1)S(1)}, bf16[2,2,96,768]{3,2,1,0:T(8,128)(2,1)S(1)}, u32[]{:S(2)}, u32[]{:S(2)}) collective-permute-start(bf16[2,2,96,768]{3,2,1,0:T(8,128)(2,1)S(1)} %pad_maximum_fusion.1), channel_id=1, source_target_pairs={{8,0},{0,8},{9,1},{1,9},{10,2},{2,10},{11,3},{3,11},{12,4},{4,12},... | collective-permute-start | bytes 1769480 | tf_op jit(solution)/shard_map/ppermute | solution.py:46
  40.3 24.8 %collective-permute-start.11 = (bf16[4,2,96,384]{3,2,1,0:T(8,128)(2,1)}, bf16[4,2,96,384]{3,2,1,0:T(8,128)(2,1)S(1)}, u32[]{:S(2)}, u32[]{:S(2)}) collective-permute-start(bf16[4,2,96,384]{3,2,1,0:T(8,128)(2,1)} %get-tuple-element.237), channel_id=1, source_target_pairs={{8,0},{0,8},{9,1},{1,9},{10,2},{2,10},{11,3},{3,11},{12,4},{4,12},... | collective-permute-start | bytes 1769480 | tf_op jit(solution)/shard_map/ppermute | solution.py:46
  68.3 16.9 %collective-permute-start.13 = (bf16[2,2,96,384]{3,2,1,0:T(8,128)(2,1)}, bf16[2,2,96,384]{3,2,1,0:T(8,128)(2,1)S(1)}, u32[]{:S(2)}, u32[]{:S(2)}) collective-permute-start(bf16[2,2,96,384]{3,2,1,0:T(8,128)(2,1)} %get-tuple-element.251), channel_id=1, source_target_pairs={{16,0},{0,16},{17,1},{1,17},{18,2},{2,18},{19,3},{3,19},{20,4},{4,... | collective-permute-start | bytes 884744 | tf_op jit(solution)/shard_map/ppermute | solution.py:46
  87.0 18.3 %collective-permute-start.18 = (bf16[128,1536]{1,0:T(8,128)(2,1)S(1)}, bf16[128,1536]{1,0:T(8,128)(2,1)S(1)}, u32[]{:S(2)}, u32[]{:S(2)}) collective-permute-start(bf16[128,1536]{1,0:T(8,128)(2,1)S(1)} %copy-done), channel_id=1, source_target_pairs={{8,0},{0,8},{9,1},{1,9},{10,2},{2,10},{11,3},{3,11},{12,4},{4,12},... | collective-permute-start | bytes 1179656 | tf_op jit(solution)/shard_map/ppermute | solution.py:46
  88.6 16.7 %collective-permute-start.19 = (bf16[128,1536]{1,0:T(8,128)(2,1)S(1)}, bf16[128,1536]{1,0:T(8,128)(2,1)S(1)}, u32[]{:S(2)}, u32[]{:S(2)}) collective-permute-start(bf16[128,1536]{1,0:T(8,128)(2,1)S(1)} %copy-done), channel_id=1, source_target_pairs={{2,0},{0,2},{3,1},{1,3},{6,4},{4,6},{7,5},{5,7},{10,8},{8,10},{11,... | collective-permute-start | bytes 1179656 | tf_op jit(solution)/shard_map/ppermute | solution.py:46
  88.6 16.7 %collective-permute-start.17 = (bf16[2,2,96,384]{3,2,1,0:T(8,128)(2,1)S(1)}, bf16[2,2,96,384]{3,2,1,0:T(8,128)(2,1)S(1)}, u32[]{:S(2)}, u32[]{:S(2)}) collective-permute-start(bf16[2,2,96,384]{3,2,1,0:T(8,128)(2,1)S(1)} %copy-done.10), channel_id=1, source_target_pairs={{16,0},{0,16},{17,1},{1,17},{18,2},{2,18},{19,3},{3,19},{20,4},{4,... | collective-permute-start | bytes 884744 | tf_op jit(solution)/shard_map/ppermute | solution.py:46
  106.9 22.1 %collective-permute-start.22 = (bf16[128,1536]{1,0:T(8,128)(2,1)S(1)}, bf16[128,1536]{1,0:T(8,128)(2,1)S(1)}, u32[]{:S(2)}, u32[]{:S(2)}) collective-permute-start(bf16[128,1536]{1,0:T(8,128)(2,1)S(1)} %collective-permute-done.18.refs_6_), channel_id=1, source_target_pairs={{2,0},{0,2},{3,1},{1,3},{6,4},{4,6},{7,5},{5,7},{10,8},{8,10},{11,... | collective-permute-start | bytes 1179656 | tf_op jit(solution)/shard_map/ppermute | solution.py:46
  129.0 17.3 %collective-permute-start.26 = (bf16[128,1536]{1,0:T(8,128)(2,1)}, bf16[128,1536]{1,0:T(8,128)(2,1)S(1)}, u32[]{:S(2)}, u32[]{:S(2)}) collective-permute-start(bf16[128,1536]{1,0:T(8,128)(2,1)} %get-tuple-element.267.refs_0_), channel_id=1, source_target_pairs={{8,0},{0,8},{9,1},{1,9},{10,2},{2,10},{11,3},{3,11},{12,4},{4,12},... | collective-permute-start | bytes 1179656 | tf_op jit(solution)/shard_map/ppermute | solution.py:46
  129.0 17.3 %collective-permute-start.27 = (bf16[128,1536]{1,0:T(8,128)(2,1)}, bf16[128,1536]{1,0:T(8,128)(2,1)S(1)}, u32[]{:S(2)}, u32[]{:S(2)}) collective-permute-start(bf16[128,1536]{1,0:T(8,128)(2,1)} %get-tuple-element.267.refs_0_), channel_id=1, source_target_pairs={{2,0},{0,2},{3,1},{1,3},{6,4},{4,6},{7,5},{5,7},{10,8},{8,10},{11,... | collective-permute-start | bytes 1179656 | tf_op jit(solution)/shard_map/ppermute | solution.py:46
  202.1 16.5 %collective-permute-start.38 = (bf16[384,384]{1,0:T(8,128)(2,1)}, bf16[384,384]{1,0:T(8,128)(2,1)S(1)}, u32[]{:S(2)}, u32[]{:S(2)}) collective-permute-start(bf16[384,384]{1,0:T(8,128)(2,1)} %bitcast.197), channel_id=1, source_target_pairs={{16,0},{0,16},{17,1},{1,17},{18,2},{2,18},{19,3},{3,19},{20,4},{4,... | collective-permute-start | bytes 884744 | tf_op jit(solution)/shard_map/ppermute | solution.py:46
  234.1 19.4 %collective-permute-start.41 = (bf16[2,128,1536]{2,1,0:T(8,128)(2,1)S(1)}, bf16[2,128,1536]{2,1,0:T(8,128)(2,1)S(1)}, u32[]{:S(2)}, u32[]{:S(2)}) collective-permute-start(bf16[2,128,1536]{2,1,0:T(8,128)(2,1)S(1)} %copy-done.62), channel_id=1, source_target_pairs={{2,0},{0,2},{3,1},{1,3},{6,4},{4,6},{7,5},{5,7},{10,8},{8,10},{11,... | collective-permute-start | bytes 2359304 | tf_op jit(solution)/shard_map/ppermute | solution.py:46
  234.1 16.0 %collective-permute-start.42 = (bf16[1,768,384]{2,1,0:T(8,128)(2,1)}, bf16[1,768,384]{2,1,0:T(8,128)(2,1)S(1)}, u32[]{:S(2)}, u32[]{:S(2)}) collective-permute-start(bf16[1,768,384]{2,1,0:T(8,128)(2,1)} %get-tuple-element.345), channel_id=1, source_target_pairs={{4,0},{0,4},{5,1},{1,5},{6,2},{2,6},{7,3},{3,7},{12,8},{8,12},{13,... | collective-permute-start | bytes 1769480 | tf_op jit(solution)/shard_map/ppermute | solution.py:46
  265.4 19.0 %collective-permute-start.44 = (bf16[768,768]{1,0:T(8,128)(2,1)}, bf16[768,768]{1,0:T(8,128)(2,1)S(1)}, u32[]{:S(2)}, u32[]{:S(2)}) collective-permute-start(bf16[768,768]{1,0:T(8,128)(2,1)} %get-tuple-element.357), channel_id=1, source_target_pairs={{2,0},{0,2},{3,1},{1,3},{6,4},{4,6},{7,5},{5,7},{10,8},{8,10},{11,... | collective-permute-start | bytes 3538952 | tf_op jit(solution)/shard_map/ppermute | solution.py:46
  266.5 22.4 %collective-permute-start.46 = (bf16[384,384]{1,0:T(8,128)(2,1)S(1)}, bf16[384,384]{1,0:T(8,128)(2,1)S(1)}, u32[]{:S(2)}, u32[]{:S(2)}) collective-permute-start(bf16[384,384]{1,0:T(8,128)(2,1)S(1)} %bitcast.193), channel_id=1, source_target_pairs={{16,0},{0,16},{17,1},{1,17},{18,2},{2,18},{19,3},{3,19},{20,4},{4,... | collective-permute-start | bytes 884744 | tf_op jit(solution)/shard_map/ppermute | solution.py:46
  266.6 26.0 %collective-permute-start.59 = (f32[3,32]{1,0:T(4,128)S(1)}, f32[3,32]{1,0:T(4,128)S(1)}, u32[]{:S(2)}, u32[]{:S(2)}) collective-permute-start(f32[3,32]{1,0:T(4,128)S(1)} %fusion), channel_id=1, source_target_pairs={{2,0},{0,2},{3,1},{1,3},{6,4},{4,6},{7,5},{5,7},{10,8},{8,10},{11,... | collective-permute-start | bytes 1160 | tf_op jit(solution)/shard_map/ppermute | solution.py:46
  288.9 20.0 %collective-permute-start.48 = (bf16[128,1536]{1,0:T(8,128)(2,1)S(1)}, bf16[128,1536]{1,0:T(8,128)(2,1)S(1)}, u32[]{:S(2)}, u32[]{:S(2)}) collective-permute-start(bf16[128,1536]{1,0:T(8,128)(2,1)S(1)} %copy-done.66), channel_id=1, source_target_pairs={{4,0},{0,4},{5,1},{1,5},{6,2},{2,6},{7,3},{3,7},{12,8},{8,12},{13,... | collective-permute-start | bytes 1179656 | tf_op jit(solution)/shard_map/ppermute | solution.py:46
  289.9 50.3 %collective-permute-start.51 = (bf16[128,1536]{1,0:T(8,128)(2,1)}, bf16[128,1536]{1,0:T(8,128)(2,1)S(1)}, u32[]{:S(2)}, u32[]{:S(2)}) collective-permute-start(bf16[128,1536]{1,0:T(8,128)(2,1)} %get-tuple-element.388), channel_id=1, source_target_pairs={{8,0},{0,8},{9,1},{1,9},{10,2},{2,10},{11,3},{3,11},{12,4},{4,12},... | collective-permute-start | bytes 1179656 | tf_op jit(solution)/shard_map/ppermute | solution.py:46
  292.5 27.5 %collective-permute-start.47 = (bf16[384,768]{1,0:T(8,128)(2,1)}, bf16[384,768]{1,0:T(8,128)(2,1)S(1)}, u32[]{:S(2)}, u32[]{:S(2)}) collective-permute-start(bf16[384,768]{1,0:T(8,128)(2,1)} %bitcast.192), channel_id=1, source_target_pairs={{8,0},{0,8},{9,1},{1,9},{10,2},{2,10},{11,3},{3,11},{12,4},{4,12},... | collective-permute-start | bytes 1769480 | tf_op jit(solution)/shard_map/ppermute | solution.py:46
  292.6 30.7 %collective-permute-start.60 = (f32[3,32]{1,0:T(4,128)S(1)}, f32[3,32]{1,0:T(4,128)S(1)}, u32[]{:S(2)}, u32[]{:S(2)}) collective-permute-start(f32[3,32]{1,0:T(4,128)S(1)} %select_add_fusion.2), channel_id=1, source_target_pairs={{8,0},{0,8},{9,1},{1,9},{10,2},{2,10},{11,3},{3,11},{12,4},{4,12},... | collective-permute-start | bytes 1160 | tf_op jit(solution)/shard_map/ppermute | solution.py:46
  323.3 16.9 %collective-permute-start.56 = (bf16[4,2,96,384]{3,2,1,0:T(8,128)(2,1)S(1)}, bf16[4,2,96,384]{3,2,1,0:T(8,128)(2,1)S(1)}, u32[]{:S(2)}, u32[]{:S(2)}) collective-permute-start(bf16[4,2,96,384]{3,2,1,0:T(8,128)(2,1)S(1)} %copy-done.64), channel_id=1, source_target_pairs={{8,0},{0,8},{9,1},{1,9},{10,2},{2,10},{11,3},{3,11},{12,4},{4,12},... | collective-permute-start | bytes 1769480 | tf_op jit(solution)/shard_map/ppermute | solution.py:46
  334.8 23.4 %collective-permute-start.62 = (f32[3,32]{1,0:T(4,128)S(1)}, f32[3,32]{1,0:T(4,128)S(1)}, u32[]{:S(2)}, u32[]{:S(2)}) collective-permute-start(f32[3,32]{1,0:T(4,128)S(1)} %select_add_fusion), channel_id=1, source_target_pairs={{4,0},{0,4},{5,1},{1,5},{6,2},{2,6},{7,3},{3,7},{12,8},{8,12},{13,... | collective-permute-start | bytes 1160 | tf_op jit(solution)/shard_map/ppermute | solution.py:46
  340.2 26.3 %collective-permute-start.55 = (bf16[4,96,384]{2,1,0:T(8,128)(2,1)}, bf16[4,96,384]{2,1,0:T(8,128)(2,1)}, u32[]{:S(2)}, u32[]{:S(2)}) collective-permute-start(bf16[4,96,384]{2,1,0:T(8,128)(2,1)} %get-tuple-element.397), channel_id=1, source_target_pairs={{2,0},{0,2},{3,1},{1,3},{6,4},{4,6},{7,5},{5,7},{10,8},{8,10},{11,... | collective-permute-start | bytes 884744 | tf_op jit(solution)/shard_map/ppermute | solution.py:46
  340.2 26.3 %collective-permute-start.57 = (bf16[4,2,96,384]{3,2,1,0:T(8,128)(2,1)S(1)}, bf16[4,2,96,384]{3,2,1,0:T(8,128)(2,1)S(1)}, u32[]{:S(2)}, u32[]{:S(2)}) collective-permute-start(bf16[4,2,96,384]{3,2,1,0:T(8,128)(2,1)S(1)} %collective-permute-done.56.other), channel_id=1, source_target_pairs={{2,0},{0,2},{3,1},{1,3},{6,4},{4,6},{7,5},{5,7},{10,8},{8,10},{11,... | collective-permute-start | bytes 1769480 | tf_op jit(solution)/shard_map/ppermute | solution.py:46
  356.5 18.1 %collective-permute-start.53 = (bf16[128,1536]{1,0:T(8,128)(2,1)S(1)}, bf16[128,1536]{1,0:T(8,128)(2,1)S(1)}, u32[]{:S(2)}, u32[]{:S(2)}) collective-permute-start(bf16[128,1536]{1,0:T(8,128)(2,1)S(1)} %add_convert_fusion.own), channel_id=1, source_target_pairs={{1,0},{0,1},{3,2},{2,3},{5,4},{4,5},{7,6},{6,7},{9,8},{8,9},{11,10... | collective-permute-start | bytes 1179656 | tf_op jit(solution)/shard_map/ppermute | solution.py:46
  (114 other events, 1162.4 us)
where the time goes:
time: 380 us; the launch traced here: 379 us
  waiting for transfers between devices  162 us (43%)
  Pallas kernels  122 us (32%)
  starting transfers between devices  59.5 us (16%)
  local copies, waits for them, and re-layouts  30.1 us (8%)
    ppermute x63, waiting for transfers between devices, fetch(): lax.ppermute(value, axis, [((i + step) % size, i) for i in range(size)])  162 us
    pallas_call x34, Pallas kernels, call(): pl.pallas_call(functools.partial(body, **static), out_shape=tuple((jax.Sh...  122 us
    ppermute x63, starting transfers between devices, fetch(): lax.ppermute(value, axis, [((i + step) % size, i) for i in range(size)])  59.5 us
    unnamed x153, local copies, waits for them, and re-layouts  22.2 us
  transfers between devices with their start and end apart: 63, of which 28 were waited for; matrix products, arithmetic and copies ran while one was open for 3% of the time, Pallas kernels for 25%

commit v1 on v0

v1 whole, which is shorter than its diff:
```python
import functools

import jax
import jax.numpy as jnp
import numpy as np
from jax import lax
from jax.experimental import pallas as pl
from jax.experimental.pallas import tpu as pltpu
from jax.sharding import Mesh, PartitionSpec as P

epsilon = 1e-06
masked_value = -1e30
far_bounds = (12, 16, 23, 32, 46, 64, 91)
f32 = jnp.float32
bf16 = jnp.bfloat16
lane = 128
ffn_order = (2, 3, 0, 1, 4, 5)
attn_order = (4, 2, 1, 0, 3, 5)
at_k, at_yl, at_zl, at_zh, at_yh, at_prefix, at_lists = range(7)


def bucket_of(relative, buckets):
    offset = jnp.abs(relative)
    far = jnp.full(offset.shape, buckets // 4, jnp.int32)
    for threshold in far_bounds:
        far = far + (offset >= threshold).astype(jnp.int32)
    return jnp.where(offset < buckets // 4, offset, far) + buckets // 2 * (relative > 0).astype(
        jnp.int32
    )


def dot(left, right, dims=((1,), (0,))):
    return lax.dot_general(left, right, (dims, ((), ())), preferred_element_type=f32)


def dot_nt(left, right):
    return dot(left, right, ((1,), (1,)))


def dot_tn(left, right):
    return dot(left, right, ((0,), (0,)))


def fetch(value, axis, step):
    size = lax.axis_size(axis)
    return lax.ppermute(value, axis, [((i + step) % size, i) for i in range(size)])


def swap(value, axis):
    return fetch(value, axis, 1)


def gather(value, axis):
    return [value] + [fetch(value, axis, e) for e in range(1, lax.axis_size(axis))]


def send_sums(sends, axis):
    size = lax.axis_size(axis)
    return [fetch(sends[e - 1], axis, size - e) for e in range(1, size)]


class Clock:
    def __init__(self, token):
        self.token = token

    def tick(self, *values):
        self.token, *values = lax.optimization_barrier((self.token, *values))
        return values


def runs_of(dims, order, inverse):
    index = np.arange(int(np.prod(dims))).reshape(dims).transpose(order).reshape(-1)
    if inverse:
        index = np.argsort(index)
    cuts = [0, *(np.flatnonzero(np.diff(index) != 1) + 1).tolist(), len(index)]
    return [(int(index[a]), int(index[a]) + b - a) for a, b in zip(cuts[:-1], cuts[1:])]


def reorder(value, dims, order, inverse=False):
    return jnp.concatenate([value[:, a:b] for a, b in runs_of(dims, order, inverse)], axis=1)


def inv_scale(values):
    return lax.rsqrt(jnp.mean(values * values, axis=-1, keepdims=True) + epsilon)


def norm_back(scale, normed, grad_normed):
    return scale * (grad_normed - normed * jnp.mean(grad_normed * normed, axis=-1, keepdims=True))


def aligned(index, size):
    return pl.ds(pl.multiple_of(index * size, size), size)


def call(body, name, here, arrays, outs, scratch=(), raw=0, **static):
    space = pl.BlockSpec(memory_space=pltpu.VMEM)
    spaces = [pl.BlockSpec(memory_space=pltpu.HBM)] * raw + [space] * (len(arrays) - raw)
    need = sum(int(np.prod(s.shape)) * jnp.dtype(s.dtype).itemsize for s in scratch[: len(scratch) - bool(raw)])
    need += (6 << 20) if static.get("dims", (lane,))[-1] >= 32 else (40 << 20)
    return pl.pallas_call(
        functools.partial(body, **static),
        out_shape=tuple(jax.ShapeDtypeStruct(shape, kind) for shape, kind in outs),
        in_specs=[pl.BlockSpec(memory_space=pltpu.SMEM)] + spaces,
        out_specs=tuple(space for _ in outs),
        scratch_shapes=scratch,
        compiler_params=pltpu.CompilerParams(vmem_limit_bytes=(56 << 20) if raw else need),
        cost_estimate=pl.CostEstimate(flops=2_000_000_000, bytes_accessed=8_000_000, transcendentals=0),
        name=name,
    )(here, *arrays)


def place_body(here, own, got, out, *, which):
    at = here[which]
    out[at] = own[...]
    out[1 - at] = got[...]


def pack_attn_body(here, wq, wk, wv, wo, one, two, own, send, mats, gains, sems):
    part, wide = mats.shape[1:]
    half = wide // 2
    copies = [
        pltpu.make_async_copy(ref, room, sems.at[i])
        for i, (ref, room) in enumerate(
            [*((ref, mats.at[i]) for i, ref in enumerate((wq, wk, wv, wo))), (one, gains.at[0]), (two, gains.at[1])]
        )
    ]
    for copy in copies:
        copy.start()
    for copy in copies:
        copy.wait()
    low = jnp.concatenate([mats[i, :, :half] for i in range(4)], axis=1)
    high = jnp.concatenate([mats[i, :, half:] for i in range(4)], axis=1)
    row = lax.broadcasted_iota(jnp.int32, (8, part), 0)
    first, second = (jnp.broadcast_to(gains[i].astype(f32), (8, part)) for i in range(2))
    head = jnp.where(row == 0, first, jnp.where(row == 1, second, 0.0)).astype(bf16)

    def write(out, mat):
        out[:8] = jnp.zeros((8, out.shape[1]), bf16)
        out[:8, :part] = head
        out[8:] = mat

    @pl.when(here[at_yl] == 0)
    def _():
        write(own, low)
        write(send, high)

    @pl.when(here[at_yl] != 0)
    def _():
        write(own, high)
        write(send, low)


def pack_ffn_body(here, wg, wu, wd, own, send, room, *, chunks):
    hidden = wg.shape[1]
    whole = hidden // lane * lane
    room[:, :, whole:] = jnp.zeros((3, wg.shape[0], 4 * chunks * lane - whole), bf16)
    room[0, :, :hidden] = wg[...]
    room[1, :, :hidden] = wu[...]
    room[2, :, :hidden] = wd[...]
    for out, core in ((own, here[at_k]), (send, 1 - here[at_k])):
        for h in range(2):
            for j in range(chunks):
                for m in range(3):
                    out[h, j, :, m * lane : (m + 1) * lane] = room[
                        m, :, aligned((2 * h + core) * chunks + j, lane)
                    ]


def place_ffn_body(here, own, got, near, first, rest, *, chunks):
    k, zl = here[at_k], here[at_zl]
    for j in range(chunks):
        near[j, k] = own[zl, j]
        near[j, 1 - k] = got[zl, j]
        out, at = (rest, j - 1) if j else (first, 0)
        out[at, k] = own[1 - zl, j]
        out[at, 1 - k] = got[1 - zl, j]


def place_first_body(here, near, got, out):
    zl = here[at_zl]
    out[zl] = near[0]
    out[1 - zl] = got[0]


def place_rest_body(here, near, rest, whole, *outs):
    zl = here[at_zl]
    j = 0
    for group in outs:
        for at in range(group.shape[0]):
            for out in (whole.at[j], group.at[at]):
                out[zl] = near[j + 1]
                out[1 - zl] = rest[j]
            j += 1


def buckets_row(span, buckets):
    return bucket_of(lax.broadcasted_iota(jnp.int32, (1, 2 * span), 1) - span, buckets)


def rows_body(here, table, *refs, dims, heads):
    *blocks, out, grads_out, lines = refs
    grads, blocks = blocks[:4], blocks[4:]
    rows = grads[0].shape[0]
    for at, block in enumerate(blocks):
        values = block[...].astype(f32)
        out[at * rows : (at + 1) * rows] = reorder(values * inv_scale(values), dims, attn_order)
    for at, block in enumerate(grads):
        low = reorder(block[...].astype(f32), dims, ffn_order)
        grads_out[at * rows : (at + 1) * rows] = low.astype(bf16)
    buckets = table.shape[1]
    values = table[...].astype(f32)
    mine = jnp.where(here[at_yl] == 0, values[:heads], values[heads:])
    row = buckets_row(lines.shape[1] // 2, buckets)
    line = jnp.zeros((heads, lines.shape[1]), f32)
    for b in range(buckets):
        line = line + jnp.where(row == b, mine[:, b : b + 1], 0.0)
    lines[...] = jnp.zeros_like(lines)
    lines[:heads] = line


def bias_block(line_ref, head, start, rows):
    line = line_ref[pl.ds(head, 1), pl.ds(pl.multiple_of(start, rows), 2 * rows)]
    spread = jnp.broadcast_to(line, (rows, 2 * rows))
    return pltpu.roll(spread, 0, 1, stride=1, stride_axis=0)[:, rows:]


def attend_body(
    here, normed, pack_own, pack_other, lines,
    qkv, probs_out, attended, keep, send, inputs, w_own, w_other, gains, *, sizes, dims
):
    rows, heads, width, query_blocks, key_blocks, span = sizes
    prefix = here[at_prefix]
    inner = heads * width
    half = w_own.shape[0]
    part = dims[-1]
    gain_parts = []
    for pack, weights in ((pack_own, w_own), (pack_other, w_other)):
        for at in range(half // part):
            weights[at * part : (at + 1) * part] = pack[at, 8:]
        gain_parts.append(
            [
                jnp.concatenate([pack[at, i : i + 1, :part].astype(f32) for at in range(half // part)], axis=1)
                for i in range(2)
            ]
        )
    for i in range(2):
        low, high = gain_parts[0][i], gain_parts[1][i]
        gain = jnp.where(
            here[at_k] == 0,
            jnp.concatenate([low, high], axis=1),
            jnp.concatenate([high, low], axis=1),
        )
        if i == 0:
            inputs[...] = (normed[...] * gain).astype(bf16)
        gains[i : i + 1] = reorder(gain, dims, attn_order, True)
    places = [here[at_lists + i] for i in range(key_blocks)]
    mine, other = aligned(here[at_k], half), aligned(1 - here[at_k], half)
    qkv[...] = (
        dot(inputs[:, mine], w_own[:, : 3 * inner]) + dot(inputs[:, other], w_other[:, : 3 * inner])
    ).astype(bf16)
    for head in range(heads):
        lanes = slice(head * width, (head + 1) * width)
        keys = qkv[:, inner + head * width : inner + (head + 1) * width]
        values = qkv[:, 2 * inner + head * width : 2 * inner + (head + 1) * width]
        for at, block in enumerate(query_blocks):
            query_block = places[block]
            queries = qkv[block * rows : (block + 1) * rows, lanes]
            raw = dot_nt(queries, keys)
            query_pos = query_block * rows + lax.broadcasted_iota(jnp.int32, (rows, rows), 0)
            parts = []
            for key_at, key_block in enumerate(places):
                start = (key_block - query_block) * rows + span - rows
                key_pos = key_block * rows + lax.broadcasted_iota(jnp.int32, (rows, rows), 1)
                allowed = (key_pos <= query_pos) | (key_pos < prefix)
                biased = raw[:, key_at * rows : (key_at + 1) * rows] + bias_block(
                    lines, head, start, rows
                )
                parts.append(jnp.where(allowed, biased, masked_value))
            scores = jnp.concatenate(parts, axis=1)
            top = jnp.max(scores, axis=1, keepdims=True)
            powers = jnp.exp(scores - top)
            probs = powers / jnp.sum(powers, axis=1, keepdims=True)
            probs_out[head, at * rows : (at + 1) * rows, :] = probs
            attended[at * rows : (at + 1) * rows, lanes] = dot(probs.astype(bf16), values).astype(
                bf16
            )
    for lanes, weights in ((mine, w_own), (other, w_other)):
        out = dot_nt(attended[...], weights[:, 3 * inner :])
        keep[:, lanes] = out[:rows]
        send[:, lanes] = out[rows:].astype(bf16)


def norm_body(here, own, got, tokens, gains, residual, low, *, dims):
    total = own[...].astype(f32) + got[...].astype(f32)
    values = tokens[...].astype(f32) + reorder(total, dims, attn_order, True)
    residual[...] = values
    low[...] = reorder(values * inv_scale(values) * gains[1:2], dims, ffn_order).astype(bf16)


def tall(refs, lanes):
    return jnp.concatenate([ref[:, lanes] for ref in refs], axis=0)


def ffn_body(here, *refs, where, picks):
    rows, grads, weights, (first_out, hidden_out) = refs[:4], refs[4], refs[5:-2], refs[-2:]
    weights = [w if at is None else w.at[at] for at, w in zip(picks, weights)]
    size = weights[0].shape[0]
    first, d_hidden = None, None
    for at, w in enumerate(weights):
        lanes = aligned(here[where + at], size)
        first_part = dot(tall(rows, lanes), w[:, : 2 * lane])
        d_part = dot(grads[:, lanes], w[:, 2 * lane :])
        first = first_part if first is None else first + first_part
        d_hidden = d_part if d_hidden is None else d_hidden + d_part
    gate, up = first[:, :lane], first[:, lane:]
    root = float(np.sqrt(2.0 / np.pi))
    square = gate * gate
    bend = jnp.tanh(root * gate * (1.0 + 0.044715 * square))
    half = 0.5 * (1.0 + bend)
    active = gate * half
    slope = half + 0.5 * gate * (1.0 - bend * bend) * (root * (1.0 + 3.0 * 0.044715 * square))
    hidden_out[...] = (active * up).astype(bf16)
    first_out[:, :lane] = (d_hidden * up * slope).astype(bf16)
    first_out[:, lane:] = (d_hidden * active).astype(bf16)


def back_body(here, *refs, where, chunks, picks, lanes):
    lefts, weights, (keep, send) = refs[:chunks], refs[chunks:-2], refs[-2:]
    weights = [w if at is None else w.at[at] for at, w in zip(picks, weights)]
    blocks = len(weights) // chunks
    rows = keep.shape[1]
    for at in range(blocks):
        total = None
        for j in range(chunks):
            w = weights[j * blocks + at]
            part = dot_nt(lefts[j][...], w[:, lanes])
            total = part if total is None else total + part
        here_lanes = aligned(here[where + at], w.shape[0])
        for a in range(2):
            keep[a, :, here_lanes] = total[2 * a * rows : (2 * a + 1) * rows]
            send[a, :, here_lanes] = total[(2 * a + 1) * rows : (2 * a + 2) * rows].astype(bf16)


def ffn_grad_body(here, *refs, outer):
    rows, grads, (first, hidden, keep, send) = refs[:4], refs[4], refs[5:]
    size = keep.shape[1]
    for e in range(outer):
        yh = here[at_yh] + e
        yh = jnp.where(yh >= outer, yh - outer, yh) * 2
        for out, y in ((keep, yh + here[at_yl]), (send, yh + 1 - here[at_yl])):
            lanes = aligned(y, size)
            out[e, :, : 2 * lane] = dot_tn(tall(rows, lanes), first[...]).astype(out.dtype)
            out[e, :, 2 * lane :] = dot_tn(grads[:, lanes], hidden[...]).astype(out.dtype)


def split_body(here, own, *refs, which):
    *got, keep, send = refs
    count = own.shape[0]
    for e in range(count):
        at = here[which] + e
        at = jnp.where(at >= count, at - count, at)
        total = own[at]
        for ref in got:
            total = total + ref[at].astype(f32)
        if e:
            send[e - 1] = total.astype(bf16)
        else:
            keep[...] = total


def split(here, which, own, got):
    shape = own.shape[1:]
    return call(
        split_body,
        "split",
        here,
        [own, *(g.reshape(own.shape) for g in got)],
        [(shape, f32), ((own.shape[0] - 1, *shape), bf16)],
        which=which,
    )


def ffn_split_body(here, *refs, chunks):
    done, core, other = refs[-3:]
    each = (len(refs) - 3) // chunks
    zl, k = here[at_zl], here[at_k]
    for j in range(chunks):
        own, *got = refs[j * each : (j + 1) * each]

        def total(depth, slice_):
            value = own[depth, slice_]
            for ref in got:
                value = value + ref[depth, slice_].astype(f32)
            return value

        done[j] = total(zl, k)
        core[j] = total(zl, 1 - k).astype(bf16)
        other[j, 0] = total(1 - zl, 0).astype(bf16)
        other[j, 1] = total(1 - zl, 1).astype(bf16)


def sum_row(values):
    sums = jnp.sum(values, axis=1, keepdims=True)
    return jnp.broadcast_to(sums, (values.shape[0], lane)).T[0:1]


def ffn_final_body(here, *refs, groups):
    parts, rest = refs[: 4 * groups], refs[4 * groups :]
    wg, wu, gain, first_row, grad_g, grad_u, grad_d, grad_gain, room = rest
    hidden = wg.shape[1]
    chunks = room.shape[2] // (4 * lane)
    zl, k = here[at_zl], here[at_k]
    j = 0
    for group in range(groups):
        done, other, core, far = parts[4 * group : 4 * group + 4]
        for at in range(done.shape[0]):
            for h, c, value in (
                (zl, k, done[at]),
                (1 - zl, k, other[at, k].astype(f32)),
                (zl, 1 - k, core[at].astype(f32)),
                (1 - zl, 1 - k, far[at, k].astype(f32)),
            ):
                for m in range(3):
                    room[m, :, aligned((2 * h + c) * chunks + j, lane)] = value[
                        :, m * lane : (m + 1) * lane
                    ]
            j += 1
    gate, up = room[0, :, :hidden], room[1, :, :hidden]
    grad_g[...] = gate
    grad_u[...] = up
    grad_d[...] = room[2, :, :hidden]
    sums = gate * wg[...].astype(f32) + up * wu[...].astype(f32)
    grad_gain[0:1] = first_row[...]
    grad_gain[1:2] = sum_row(sums) / gain[...].astype(f32)


def pair_body(here, own, got, keep, send):
    keep[...] = own[0] + got[0].astype(f32)
    send[...] = (own[1] + got[1].astype(f32)).astype(bf16)


def residual_back_body(here, own, got, residual, cotangent, gains, d_residual, d_low, *, dims):
    total = own[...].astype(f32) + got[...].astype(f32)
    grad_normed = reorder(total, dims, ffn_order, True) * gains[1:2]
    values = residual[...]
    scale = inv_scale(values)
    back = cotangent[...].astype(f32) + norm_back(scale, values * scale, grad_normed)
    d_residual[...] = back
    d_low[...] = reorder(back, dims, attn_order).astype(bf16)


def attend_back_body(
    here, qkv, probs_in, d_own, d_far, w_own, w_other,
    d_query, d_keep, d_send, table, lines, d_att, *, sizes, buckets
):
    rows, heads, width, query_blocks, key_blocks, span = sizes
    inner = heads * width
    half = w_own.shape[0]
    places = [here[at_lists + i] for i in range(key_blocks)]
    mine, other = aligned(here[at_k], half), aligned(1 - here[at_k], half)
    d_rows = (d_own, d_far)
    d_att[...] = (
        dot(tall(d_rows, mine), w_own[:, 3 * inner :])
        + dot(tall(d_rows, other), w_other[:, 3 * inner :])
    ).astype(bf16)
    lines[...] = jnp.zeros_like(lines)
    up, down = (lax.broadcasted_iota(jnp.int32, (rows, rows), axis) for axis in (0, 1))
    flip = (up + down == rows - 1).astype(bf16)
    for head in range(heads):
        lanes = slice(head * width, (head + 1) * width)
        value_lanes = slice(inner + head * width, inner + (head + 1) * width)
        keys = qkv[:, inner + head * width : inner + (head + 1) * width]
        values = qkv[:, 2 * inner + head * width : 2 * inner + (head + 1) * width]
        d_key, d_value = None, None
        for at, block in enumerate(query_blocks):
            queries = qkv[block * rows : (block + 1) * rows, lanes]
            d_attended = d_att[at * rows : (at + 1) * rows, lanes]
            probs = probs_in[head, at * rows : (at + 1) * rows, :]
            d_probs = dot_nt(d_attended, values)
            delta = jnp.sum(probs * d_probs, axis=1, keepdims=True)
            d_scores = (probs * (d_probs - delta)).astype(bf16)
            d_query[at * rows : (at + 1) * rows, lanes] = dot(d_scores, keys).astype(bf16)
            key_part = dot_tn(d_scores, queries)
            value_part = dot_tn(probs.astype(bf16), d_attended)
            d_key = key_part if d_key is None else d_key + key_part
            d_value = value_part if d_value is None else d_value + value_part
            upward = dot(flip, d_scores)
            for key_at, key_block in enumerate(places):
                start = (key_block - places[block]) * rows + span - rows
                piece = upward[:, key_at * rows : (key_at + 1) * rows]
                padded = jnp.concatenate([piece, jnp.zeros_like(piece)], axis=1)
                turned = pltpu.roll(padded, 1, 1, stride=1, stride_axis=0)
                span_at = pl.ds(pl.multiple_of(start, rows), 2 * rows)
                lines[pl.ds(head, 1), span_at] += jnp.sum(turned, axis=0, keepdims=True)
        for key_at in range(key_blocks):
            from_, to = slice(key_at * rows, (key_at + 1) * rows), key_at // 2
            for out, parity in ((d_keep, 0), (d_send, 1)):
                if key_at % 2 == parity:
                    out[to, :, lanes] = d_key[from_].astype(out.dtype)
                    out[to, :, value_lanes] = d_value[from_].astype(out.dtype)
    row = buckets_row(span, buckets)
    column = lax.broadcasted_iota(jnp.int32, table.shape, 1)
    total = jnp.zeros(table.shape, f32)
    for b in range(buckets):
        one = jnp.sum(jnp.where(row == b, lines[...], 0.0), axis=1, keepdims=True)
        total = jnp.where(column == b, one, total)
    table[...] = total


def attn_grad_body(
    here, inputs, d_query, d_keep, d_got, d_own, d_far, attended, w_own, w_other,
    g_keep, g_send, keep, send, d_qkv, *, sizes
):
    rows, heads, width, query_blocks, key_blocks, span = sizes
    inner = heads * width
    half = w_own.shape[0]
    mine, other = aligned(here[at_k], half), aligned(1 - here[at_k], half)
    d_qkv[:, :inner] = d_query[...]
    for at in range(2):
        d_qkv[at * rows : (at + 1) * rows, inner:] = (d_keep[at] + d_got[at].astype(f32)).astype(bf16)
    for lanes, weights, out in ((mine, w_own, keep), (other, w_other, send)):
        part = dot_nt(d_qkv[...], weights[:, : 3 * inner])
        g_keep[:, lanes] = part[:rows]
        g_send[:, lanes] = part[rows:].astype(bf16)
        two = jnp.concatenate([inputs[b * rows : (b + 1) * rows, lanes] for b in query_blocks], axis=0)
        out[:, : 3 * inner] = dot_tn(two, d_qkv[...]).astype(out.dtype)
        out[:, 3 * inner :] = dot_tn(tall((d_own, d_far), lanes), attended[...]).astype(out.dtype)


def input_grad_body(here, own, got, tokens, gains, d_residual, out, *, dims):
    total = own[...].astype(f32) + got[...].astype(f32)
    grad_normed = reorder(total, dims, attn_order, True) * gains[0:1]
    values = tokens[...].astype(f32)
    scale = inv_scale(values)
    out[...] = (d_residual[...] + norm_back(scale, values * scale, grad_normed)).astype(bf16)


def mixed_body(here, own, got, residual, out, *, dims):
    total = own[...].astype(f32) + got[...].astype(f32)
    out[...] = (residual[...] + reorder(total, dims, ffn_order, True)).astype(bf16)


def attn_final_body(here, own, got, wq, wk, wv, gain, gq, gk, gv, go, grad_gain):
    inner = own.shape[1] // 4

    def finish(low, high):
        grads = [
            jnp.concatenate([m[:, i * inner : (i + 1) * inner] for m in (low, high)], axis=1)
            for i in range(4)
        ]
        sums = 0.0
        for out, weights, grad in ((gq, wq, grads[0]), (gk, wk, grads[1]), (gv, wv, grads[2])):
            out[...] = grad
            sums = sums + grad * weights[...].astype(f32)
        go[...] = grads[3]
        grad_gain[...] = sum_row(sums) / gain[...].astype(f32)

    @pl.when(here[at_yl] == 0)
    def _():
        finish(own[...], got[...].astype(f32))

    @pl.when(here[at_yl] != 0)
    def _():
        finish(got[...].astype(f32), own[...])


def local(
    tokens,
    cotangent,
    prefix,
    norm_one,
    w_query,
    w_key,
    w_value,
    w_out,
    position_bias_matrix,
    norm_two,
    w_gate,
    w_up,
    w_down,
):
    outer, deep = lax.axis_size("yh"), lax.axis_size("zh")
    rows, wide = tokens.shape[1:]
    part = w_query.shape[0]
    heads_dev, buckets = position_bias_matrix.shape
    heads = heads_dev // 2
    width = w_query.shape[1] // heads_dev
    inner = heads * width
    hidden_dev = w_gate.shape[1]
    chunks = -(-hidden_dev // (4 * lane))
    length = rows * outer * 4
    dims = (deep, 2, outer, 2, 2, part)
    half = wide // 2
    key_blocks = 4 * outer
    sizes = (rows, heads, width, (0, 2), key_blocks, length)

    split_deep = deep == 2 and (4 * part) % lane == 0
    deep_blocks = deep if split_deep else 1
    yh, yl, k, zl, zh = (lax.axis_index(a) for a in ("yh", "yl", "k", "zl", "zh"))
    relative = [(e, a) for a in range(2) for e in range(outer)]
    ys = [((yh + e) % outer) * 2 + (yl + a) % 2 for e, a in relative]
    where = at_lists + key_blocks
    here = [k, yl, zl, zh, yh, prefix[0]]
    here += [
        ((yh + e) % outer) * 4 + ((yl + a) % 2) * 2 + (k + b) % 2
        for e in range(outer)
        for a in range(2)
        for b in range(2)
    ]
    here += [y * deep_blocks + (zh + d) % deep_blocks for d in range(deep_blocks) for y in ys]
    here = jnp.stack([jnp.asarray(v, jnp.int32) for v in here])
    tick = Clock(here).tick
    which = {"k": at_k, "yl": at_yl, "zl": at_zl, "zh": at_zh, "yh": at_yh}

    def kernel(body, name, arrays, outs, scratch=(), **static):
        return call(body, name, here, arrays, outs, scratch, **static)

    def place(pieces, axis):
        size, shape = len(pieces), pieces[0].shape
        if size == 1:
            return pieces[0][None]
        if size == 2:
            outs = [((2, *shape), pieces[0].dtype)]
            return kernel(place_body, "place", pieces, outs, which=which[axis])[0]
        stack = jnp.zeros((size, *shape), pieces[0].dtype)
        for e, piece in enumerate(pieces):
            at = (lax.axis_index(axis) + e) % size
            stack = lax.dynamic_update_slice_in_dim(stack, piece[None], at, 0)
        return stack

    def both(value, axis):
        return place(gather(value, axis), axis)

    tall_part = 8 + part
    own, send = kernel(
        pack_attn_body,
        "pack_attn",
        [w_query, w_key, w_value, w_out.T, norm_one[None], norm_two[None]],
        [((tall_part, 4 * inner), bf16)] * 2,
        [
            pltpu.VMEM((4, part, 2 * inner), bf16),
            pltpu.VMEM((2, 1, part), bf16),
            pltpu.SemaphoreType.DMA((6,)),
        ],
        raw=6,
    )
    own, send, own_grad, *ffn_in = tick(own, send, cotangent[0], w_gate, w_up, w_down.T)
    pack_got = swap(send, "yl")
    far_grad = swap(own_grad, "zl")
    ffn_own, ffn_send = kernel(
        pack_ffn_body,
        "pack_ffn",
        ffn_in,
        [((2, chunks, part, 3 * lane), bf16)] * 2,
        [pltpu.VMEM((3, part, 4 * chunks * lane), bf16)],
        chunks=chunks,
    )
    pack = place([own, pack_got], "yl")

    pack, ffn_own, ffn_send, own_tokens = tick(pack, ffn_own, ffn_send, tokens[0])
    pack_all = gather(pack, "zh")
    far_tokens = swap(own_tokens, "yl")
    near, near_first, near_rest = kernel(
        place_ffn_body,
        "place_ffn",
        [ffn_own, swap(ffn_send, "k")],
        [((n, 2, part, 3 * lane), bf16) for n in (chunks, 1, chunks - 1)],
        chunks=chunks,
    )
    pack = place(pack_all, "zh")

    pack, near, near_first, near_rest, far_tokens, own_tokens, far_grad, own_grad = tick(
        pack, near, near_first, near_rest, far_tokens, own_tokens, far_grad, own_grad
    )
    pack_all = gather(pack, "zl")
    first_got = swap(near_first, "zl")
    row_blocks = [p for pair in zip(gather(own_tokens, "yh"), gather(far_tokens, "yh")) for p in pair]
    row_blocks = [p for b in row_blocks for p in gather(b, "k")]
    grad_blocks = [p for b in (own_grad, far_grad) for p in gather(b, "k")]
    normed, grad_rows, lines = kernel(
        rows_body,
        "rows",
        [position_bias_matrix, *grad_blocks, *row_blocks],
        [((length, wide), f32), ((4 * rows, wide), bf16), ((8, 2 * length), f32)],
        dims=dims,
        heads=heads,
    )
    pack = place(pack_all, "zl")
    (near_zero,) = kernel(
        place_first_body, "place_first", [near, first_got], [((2, 2, part, 3 * lane), bf16)]
    )

    pack, near, near_zero, first_got, near_rest, normed, grad_rows, lines = tick(
        pack, near, near_zero, first_got, near_rest, normed, grad_rows, lines
    )
    pack = both(pack, "yh").reshape(half // part, tall_part, 4 * inner)
    pack_own, pack_other = gather(pack, "k")
    rest_got = swap(near_rest, "zl")

    groups = [[0], list(range(1, chunks - 1)), [chunks - 1]]

    def over_zh(value):
        pieces = gather(value, "zh")
        if split_deep:
            return pieces[1]
        return place(pieces, "zh").swapaxes(0, 1)

    def over_y(value):
        value = value.reshape(value.shape[0], -1, 3 * lane)
        return [p for b in gather(value, "yl") for p in gather(b, "yh")]

    far, far_y = [None] * 3, [None] * 3
    near_zero = near_zero[None]
    far[0] = over_zh(near_zero)
    zero_y = over_y(near_zero) if split_deep else []
    qkv, probs, attended, out_keep, out_send, attn_input, w_own, w_other, gains = kernel(
        attend_body,
        "attend",
        [normed, pack_own, pack_other, lines],
        [
            ((length, 3 * inner), bf16),
            ((heads, 2 * rows, length), f32),
            ((2 * rows, inner), bf16),
            ((rows, wide), f32),
            ((rows, wide), bf16),
            ((length, wide), bf16),
            ((half, 4 * inner), bf16),
            ((half, 4 * inner), bf16),
            ((2, wide), f32),
        ],
        sizes=sizes,
        dims=dims,
    )

    out_keep, out_send = tick(out_keep, out_send)
    out_got = swap(out_send, "yl")
    near, rest_got, far[0], *zero_y = tick(near, rest_got, far[0], *zero_y)
    shape = (2, 2, part, 3 * lane)
    whole, *nears = kernel(
        place_rest_body,
        "place_rest",
        [near, rest_got],
        [((chunks - 1, *shape), bf16)] + [((len(g), *shape), bf16) for g in groups[1:]],
    )
    out_keep, whole, *nears = tick(out_keep, whole, *nears)
    far[1] = over_zh(nears[0])
    rest_y = over_y(whole) if split_deep else []
    out_sum = (out_keep + out_got.astype(f32)).astype(bf16)

    out_sum, far[0] = tick(out_sum, far[0])
    out_other = swap(out_sum, "x")
    residual, low_two = kernel(
        norm_body,
        "norm",
        [out_sum, out_other, tokens[0], gains],
        [((rows, wide), f32), ((rows, wide), bf16)],
        dims=dims,
    )

    low_two, far[0], nears[1], *rest_y = tick(low_two, far[0], nears[1], *rest_y)
    far_two, core_two = swap(low_two, "zl"), swap(low_two, "k")
    far_y[0] = over_y(far[0])
    core_two, far[1], nears[1] = tick(core_two, far[1], nears[1])
    far[2] = over_zh(nears[1])
    far_y[1] = over_y(far[1])

    far_two, core_two, *far_y[0] = tick(far_two, core_two, *far_y[0])
    farcore_two = swap(far_two, "k")
    ffn_rows = [low_two, core_two, far_two, farcore_two]

    def weights_of(j):
        g = next(g for g, group in enumerate(groups) if j in group)
        at = j - groups[g][0]
        near_blocks = []
        if split_deep:
            own, others, near_at = (near_zero, zero_y, 0) if j == 0 else (whole, rest_y, j - 1)
            own = own.reshape(own.shape[0], -1, 3 * lane)
            near_blocks = [(v, near_at) for v in (own, *others[1:])]
        return near_blocks + [(v, at) for v in far_y[g]]

    def ffn(j):
        weights = weights_of(j)
        return kernel(
            ffn_body,
            "ffn",
            [*ffn_rows, grad_rows, *(w for w, _ in weights)],
            [((4 * rows, 2 * lane), bf16), ((4 * rows, lane), bf16)],
            where=where,
            picks=tuple(at for _, at in weights),
        )

    def back(lefts, lanes):
        weights = [w for j in range(chunks) for w in weights_of(j)]
        return kernel(
            back_body,
            "back",
            [*lefts, *(w for w, _ in weights)],
            [((2, rows, wide), f32), ((2, rows, wide), bf16)],
            where=where,
            chunks=chunks,
            picks=tuple(at for _, at in weights),
            lanes=lanes,
        )

    def ffn_grad(first, hidden):
        return kernel(
            ffn_grad_body,
            "ffn_grad",
            [*ffn_rows, grad_rows, first, hidden],
            [((outer, half // outer, 3 * lane), kind) for kind in (f32, bf16)],
            outer=outer,
        )

    def sum_y(keep, got):
        got = [got]
        if outer > 1:
            total = keep + got[0].astype(f32)
            got = send_sums([total[e].astype(bf16) for e in range(1, outer)], "yh")
            keep = total[0]
        return split(here, at_zh, keep.reshape(deep, 4 * part, 3 * lane), got)

    def sum_zh(keep, send):
        got = send_sums([send[e] for e in range(deep - 1)], "zh")
        return [v.reshape(2, 2, part, 3 * lane) for v in (keep, *got)]

    def pair(keep, got):
        shape = keep.shape[1:]
        return kernel(pair_body, "pair", [keep, got], [(shape, f32), (shape, bf16)])

    def ffn_split(group):
        count = len(group)
        return kernel(
            ffn_split_body,
            "ffn_split",
            [v for each in group for v in each],
            [
                ((count, part, 3 * lane), f32),
                ((count, part, 3 * lane), bf16),
                ((count, 2, part, 3 * lane), bf16),
            ],
            chunks=count,
        )

    first_0, hidden_0 = ffn(0)

    far[2], first_0, hidden_0 = tick(far[2], first_0, hidden_0)
    far_y[2] = over_y(far[2])
    grads = [None] * chunks
    grad_got, sums, zh_sums = [None] * chunks, [None] * chunks, [None] * chunks
    grads[0] = ffn_grad(first_0, hidden_0)
    firsts, hiddens = [first_0], [hidden_0]
    for j in range(1, chunks):
        first, hidden = ffn(j)
        firsts.append(first)
        hiddens.append(hidden)
    keep, send = back(firsts, slice(0, 2 * lane))

    keep, send, *flat = tick(keep, send, *grads[0], *firsts[1:], *hiddens)
    grads[0], firsts, hiddens = flat[:2], [None, *flat[2:5]], flat[5:]
    core_got = swap(send, "k")
    grad_got[0] = swap(grads[0][1], "yl")
    grads[1] = ffn_grad(firsts[1], hiddens[1])
    core_keep, core_send = pair(keep, core_got)

    core_keep, core_send, *flat = tick(core_keep, core_send, *grads[1], *firsts[2:], *hiddens)
    grads[1], firsts, hiddens = flat[:2], [None, None, *flat[2:4]], flat[4:]
    core_got = swap(core_send, "zl")
    grad_got[1] = swap(grads[1][1], "yl")
    grads[2] = ffn_grad(firsts[2], hiddens[2])
    grads[3] = ffn_grad(firsts[3], hiddens[3])
    mixed_keep, mixed_send = back(hiddens, slice(2 * lane, 3 * lane))
    grad_keep, mixed_keep, *flat = tick(grads[0][0], mixed_keep, mixed_send, *grads[2], *grads[3])
    mixed_send, grads[2], grads[3] = flat[0], flat[1:3], flat[3:]
    sums[0] = sum_y(grad_keep, grad_got[0])
    core = (core_keep + core_got.astype(f32)).astype(bf16)

    core, mixed_keep, mixed_send, *flat = tick(
        core, mixed_keep, mixed_send, *sums[0], *grads[2], *grads[3]
    )
    sums[0], grads[2], grads[3] = flat[:2], flat[2:4], flat[4:]
    core_other = swap(core, "x")
    zh_sums[0] = sum_zh(*sums[0])
    sums[1] = sum_y(grads[1][0], grad_got[1])
    d_residual, d_low = kernel(
        residual_back_body,
        "residual_back",
        [core, core_other, residual, cotangent[0], gains],
        [((rows, wide), f32), ((rows, wide), bf16)],
        dims=dims,
    )

    d_low, mixed_send, *flat = tick(d_low, mixed_send, *sums[1], *grads[2])
    sums[1], grads[2] = flat[:2], flat[2:]
    d_far = swap(d_low, "yl")
    grad_got[2] = swap(grads[2][1], "yl")
    zh_sums[1] = sum_zh(*sums[1])
    mixed_got = swap(mixed_send, "k")
    mixed_keep, mixed_got, *zh_sums[0] = tick(mixed_keep, mixed_got, *zh_sums[0])
    mixed_keep, mixed_send = pair(mixed_keep, mixed_got)

    d_far, mixed_keep, mixed_send = tick(d_far, mixed_keep, mixed_send)
    mixed_got = swap(mixed_send, "zl")
    d_query, d_keep, d_send, grad_table = kernel(
        attend_back_body,
        "attend_back",
        [qkv, probs, d_low, d_far, w_own, w_other],
        [
            ((2 * rows, inner), bf16),
            ((2 * outer, rows, 2 * inner), f32),
            ((2 * outer, rows, 2 * inner), bf16),
            ((8, lane), f32),
        ],
        [pltpu.VMEM((8, 2 * length), f32), pltpu.VMEM((2 * rows, inner), bf16)],
        sizes=sizes,
        buckets=buckets,
    )

    def table_sum(value, axis):
        if lax.axis_size(axis) == 2:
            return value + swap(value, axis)
        return jnp.sum(both(value, axis), axis=0)

    d_query, d_keep, d_send, grad_table, *zh_sums[1] = tick(
        d_query, d_keep, d_send, grad_table, *zh_sums[1]
    )
    done_a = ffn_split(zh_sums[: chunks // 2])
    d_got = swap(d_send, "k")
    grad_table = table_sum(grad_table, "k")
    if outer > 1:
        grad_table = table_sum(grad_table, "yh")
        total = (d_keep + d_got.astype(f32)).reshape(outer, 2, rows, 2 * inner)
        arrived = send_sums([total[e].astype(bf16) for e in range(1, outer)], "yh")
        d_keep, d_got = total[0], sum(a.astype(f32) for a in arrived)
    g_keep, g_send, keep, send = kernel(
        attn_grad_body,
        "attn_grad",
        [attn_input, d_query, d_keep, d_got, d_low, d_far, attended, w_own, w_other],
        [
            ((rows, wide), f32),
            ((rows, wide), bf16),
            ((half, 4 * inner), f32),
            ((half, 4 * inner), bf16),
        ],
        [pltpu.VMEM((2 * rows, 3 * inner), bf16)],
        sizes=sizes,
    )

    g_keep, g_send, keep, send, grad_table, *flat = tick(
        g_keep, g_send, keep, send, grad_table, grad_got[2], *done_a
    )
    grad_got[2], done_a = flat[0], flat[1:]
    got = [swap(send, "k")]
    g_got = swap(g_send, "yl")
    grad_table = table_sum(grad_table, "zl")

    def spread(done):
        other = swap(done[2], "zl")
        return [done[0], other, swap(done[1], "k"), swap(other, "k")]

    if outer > 1:
        total = (keep + got[0].astype(f32)).reshape(outer, -1, 4 * inner)
        pieces = [lax.dynamic_index_in_dim(total, (yh + e) % outer, 0, False) for e in range(outer)]
        keep, got = pieces[0], send_sums([p.astype(bf16) for p in pieces[1:]], "yh")
    sums[2] = sum_y(grads[2][0], grad_got[2])
    keep, send = split(here, at_zl, keep.reshape(2, deep * 2 * part, 4 * inner), got)

    keep, send, mixed_got, grad_table, *flat = tick(
        keep, send, mixed_got, grad_table, *sums[2], *grads[3]
    )
    sums[2], grads[3] = flat[:2], flat[2:4]
    got = send_sums([send[0]], "zl")
    grad_got[3] = swap(grads[3][1], "yl")
    zh_sums[2] = sum_zh(*sums[2])
    grad_table = table_sum(grad_table, "zh")
    mixed_half = (mixed_keep + mixed_got.astype(f32)).astype(bf16)
    g_sum = (g_keep + g_got.astype(f32)).astype(bf16)
    keep, send = split(here, at_zh, keep.reshape(deep, 2 * part, 4 * inner), got)

    keep, send, g_sum, mixed_half, grad_table, *done_a = tick(
        keep, send, g_sum, mixed_half, grad_table, *done_a
    )
    got = send_sums([send[e] for e in range(deep - 1)], "zh")
    g_other = swap(g_sum, "x")
    mixed_other = swap(mixed_half, "x")

    sums[3] = sum_y(grads[3][0], grad_got[3])
    grad_table = both(grad_table, "yl")
    (mixed,) = kernel(
        mixed_body, "mixed", [mixed_half, mixed_other, residual], [((rows, wide), bf16)], dims=dims
    )
    mixed, *flat = tick(mixed, *sums[3], *done_a)
    sums[3], done_a = flat[:2], flat[2:]
    zh_sums[3] = sum_zh(*sums[3])
    group_a = spread(done_a)
    (input_grad,) = kernel(
        input_grad_body,
        "input_grad",
        [g_sum, g_other, tokens[0], gains, d_residual],
        [((rows, wide), bf16)],
        dims=dims,
    )
    keep, send = split(here, at_yl, keep.reshape(2, part, 4 * inner), got)

    keep, send, grad_table = tick(keep, send, grad_table)
    got = swap(send[0], "yl")
    keep, input_grad = tick(keep, input_grad)
    group_b = spread(ffn_split(zh_sums[chunks // 2 :]))
    grad_query, grad_key, grad_value, grad_out, gain_row = kernel(
        attn_final_body,
        "attn_final",
        [keep, got, w_query, w_key, w_value, norm_one[None]],
        [((part, 2 * inner), f32)] * 4 + [((1, part), f32)],
    )
    grad_gate, grad_up, grad_down, grad_gains = kernel(
        ffn_final_body,
        "ffn_final",
        [*group_a, *group_b, w_gate, w_up, norm_two[None], gain_row],
        [((part, hidden_dev), f32)] * 3 + [((2, part), f32)],
        [pltpu.VMEM((3, part, 4 * chunks * lane), f32)],
        groups=2,
    )
    grad_gains = grad_gains + swap(grad_gains, "x")
    return (
        mixed[None],
        input_grad[None],
        grad_gains[0],
        grad_query,
        grad_key,
        grad_value,
        grad_out.T,
        grad_table[:, :heads, :buckets].reshape(heads_dev, buckets),
        grad_gains[1],
        grad_gate,
        grad_up,
        grad_down.T,
    )


def solution(mesh):
    depths, lines, halves = (mesh.shape[a] for a in ("fsdp", "ctx", "tp"))
    fine = Mesh(
        mesh.devices.reshape(depths // 2, 2, lines // 4, 2, 2, halves),
        ("zh", "zl", "yh", "yl", "k", "x"),
    )
    depth, line = ("zh", "zl"), ("yh", "yl", "k")
    every = (*depth, *line)
    in_specs = (
        P(depth, line, None),
        P(depth, line, None),
        P(depth),
        P(every),
        P(every, "x"),
        P(every, "x"),
        P(every, "x"),
        P("x", every),
        P("x", None),
        P(every),
        P(every, "x"),
        P(every, "x"),
        P("x", every),
    )
    out_specs = (
        P(depth, line, None),
        P(depth, line, None),
        P(every),
        P(every, "x"),
        P(every, "x"),
        P(every, "x"),
        P("x", every),
        P("x", None),
        P(every),
        P(every, "x"),
        P(every, "x"),
        P("x", every),
    )
    return jax.shard_map(local, mesh=fine, in_specs=in_specs, out_specs=out_specs, check_vma=False)
```

time: 380 us -> 297 us (0.78)
  Pallas kernels: 122 us -> 58.7 us
  local copies, waits for them, and re-layouts: 30.1 us -> 1.86 us
  waiting for transfers between devices: 162 us -> 179 us
  starting transfers between devices: 59.5 us -> 55.1 us
    pallas_call x34 -> x40, Pallas kernels: 122 us -> 58.7 us  [call(): pl.pallas_call(functools.partial(body, **static), out_shape=tuple((jax.Sh...]
    unnamed x153 -> x26, local copies, waits for them, and re-layouts: 22.2 us -> 0.06 us
    ppermute x63 -> x59, waiting for transfers between devices: 162 us -> 179 us  [fetch(): lax.ppermute(value, axis, [((i + step) % size, i) for i in range(size)])]
    ppermute x63 -> x59, starting transfers between devices: 59.5 us -> 55.1 us  [fetch(): lax.ppermute(value, axis, [((i + step) % size, i) for i in range(size)])]
  transfers between devices with their start and end apart: 63 -> 59, of which waited for: 28 -> 32; matrix products, arithmetic and copies ran while one was open for 3% -> 0% of each run, Pallas kernels for 25% -> 16%
where the time goes in v1:
time: 297 us
  waiting for transfers between devices  179 us (60%)
  Pallas kernels  58.7 us (20%)
  starting transfers between devices  55.1 us (19%)
    ppermute x59, waiting for transfers between devices, fetch(): lax.ppermute(value, axis, [((i + step) % size, i) for i in range(size)])  179 us
    pallas_call x40, Pallas kernels, call(): pl.pallas_call(functools.partial(body, **static), out_shape=tuple((jax.Sh...  58.7 us
    ppermute x59, starting transfers between devices, fetch(): lax.ppermute(value, axis, [((i + step) % size, i) for i in range(size)])  55.1 us
  transfers between devices with their start and end apart: 59, of which 32 were waited for; matrix products, arithmetic and copies ran while one was open for 0% of the time, Pallas kernels for 16%

profile of v1, /device:TPU:0, one launch (start us, length us, event | category | flops | bytes accessed | tf_op | source)
XLA Modules:
  0.0 296.8 jit_solution(10825581120405037601)
XLA Ops:
  4.7 3.0 %collective-permute-start = (bf16[104,768]{1,0:T(8,128)(2,1)}, bf16[104,768]{1,0:T(8,128)(2,1)S(1)}, u32[]{:S(2)}, u32[]{:S(2)}) collective-permute-start(bf16[104,768]{1,0:T(8,128)(2,1)} %get-tuple-element.257), channel_id=1, source_target_pairs={{4,0},{0,4},{5,1},{1,5},{6,2},{2,6},{7,3},{3,7},{12,8},{8,12},{13,... | collective-permute-start | bytes 479240 | tf_op jit(solution)/shard_map/ppermute | solution.py:46
  8.8 3.3 %collective-permute-done.got = bf16[104,768]{1,0:T(8,128)(2,1)S(1)} collective-permute-done((bf16[104,768]{1,0:T(8,128)(2,1)}, bf16[104,768]{1,0:T(8,128)(2,1)S(1)}, u32[]{:S(2)}, u32[]{:S(2)}) %collective-permute-start) | collective-permute-done | bytes 159776 | tf_op jit(solution)/shard_map/ppermute | solution.py:46
  18.7 12.0 %collective-permute-done.1.got = bf16[2,104,768]{2,1,0:T(8,128)(2,1)S(1)} collective-permute-done((bf16[2,104,768]{2,1,0:T(8,128)(2,1)S(1)}, bf16[2,104,768]{2,1,0:T(8,128)(2,1)S(1)}, u32[]{:S(2)}, u32[]{:S(2)}) %collective-permute-start.1) | collective-permute-done | bytes 319520 | tf_op jit(solution)/shard_map/ppermute | solution.py:46
  35.0 4.2 %collective-permute-done.6.got = bf16[1,2,96,384]{3,2,1,0:T(8,128)(2,1)S(1)} collective-permute-done((bf16[1,2,96,384]{3,2,1,0:T(8,128)(2,1)S(1)}, bf16[1,2,96,384]{3,2,1,0:T(8,128)(2,1)S(1)}, u32[]{:S(2)}, u32[]{:S(2)}) %collective-permute-start.6) | collective-permute-done | bytes 147488 | tf_op jit(solution)/shard_map/ppermute | solution.py:46
  43.6 7.8 %collective-permute-done.5.got = bf16[2,2,104,768]{3,2,1,0:T(8,128)(2,1)S(1)} collective-permute-done((bf16[2,2,104,768]{3,2,1,0:T(8,128)(2,1)S(1)}, bf16[2,2,104,768]{3,2,1,0:T(8,128)(2,1)S(1)}, u32[]{:S(2)}, u32[]{:S(2)}) %collective-permute-start.5) | collective-permute-done | bytes 639008 | tf_op jit(solution)/shard_map/ppermute | solution.py:46
  57.9 5.4 %attend.1 = (bf16[512,576]{1,0:T(8,128)(2,1)S(1)}, f32[3,256,512]{2,1,0:T(8,128)S(1)}, bf16[256,192]{1,0:T(8,128)(2,1)S(1)}, f32[128,1536]{1,0:T(8,128)S(1)}, bf...) custom-call(s32[14]{0:T(128)S(1)} %copy-done, ...), custom_call_target="tpu_custom_call" | custom-call | flops 2000000000 | bytes 8000000 | tf_op jit(solution)/shard_map/attend/pallas_call | solution.py:100
  63.9 6.4 %collective-permute-done.13 = bf16[1,2,2,96,384]{4,3,2,1,0:T(8,128)(2,1)S(1)} collective-permute-done((bf16[1,2,2,96,384]{4,3,2,1,0:T(8,128)(2,1)S(1)}, bf16[1,2,2,96,384]{4,3,2,1,0:T(8,128)(2,1)S(1)}, u32[]{:S(2)}, u32[]{:S(2)}) %collective-permute-start.13) | collective-permute-done | bytes 294944 | tf_op jit(solution)/shard_map/ppermute | solution.py:46
  77.6 6.4 %collective-permute-done.16.got = bf16[128,1536]{1,0:T(8,128)(2,1)S(1)} collective-permute-done((bf16[128,1536]{1,0:T(8,128)(2,1)S(1)}, bf16[128,1536]{1,0:T(8,128)(2,1)S(1)}, u32[]{:S(2)}, u32[]{:S(2)}) %collective-permute-start.16) | collective-permute-done | bytes 393248 | tf_op jit(solution)/shard_map/ppermute | solution.py:46
  85.1 7.9 %collective-permute-done.17.refs_6_.refs_9_.refs_13_.refs_17_ = bf16[3,384,384]{2,1,0:T(8,128)(2,1)S(1)} collective-permute-done((bf16[3,384,384]{2,1,0:T(8,128)(2,1)S(1)}, bf16[3,384,384]{2,1,0:T(8,128)(2,1)S(1)}, u32[]{:S(2)}, u32[]{:S(2)}) %collective-permute-start.17) | collective-permute-done | bytes 884768 | tf_op jit(solution)/shard_map/ppermute | solution.py:46
  97.0 6.0 %collective-permute-done.19 = bf16[2,2,2,96,384]{4,3,2,1,0:T(8,128)(2,1)S(1)} collective-permute-done((bf16[2,2,2,96,384]{4,3,2,1,0:T(8,128)(2,1)S(1)}, bf16[2,2,2,96,384]{4,3,2,1,0:T(8,128)(2,1)S(1)}, u32[]{:S(2)}, u32[]{:S(2)}) %collective-permute-start.19) | collective-permute-done | bytes 589856 | tf_op jit(solution)/shard_map/ppermute | solution.py:46
  104.7 6.7 %collective-permute-done.20.refs_2_ = bf16[128,1536]{1,0:T(8,128)(2,1)S(1)} collective-permute-done((bf16[128,1536]{1,0:T(8,128)(2,1)S(1)}, bf16[128,1536]{1,0:T(8,128)(2,1)S(1)}, u32[]{:S(2)}, u32[]{:S(2)}) %collective-permute-start.20) | collective-permute-done | bytes 393248 | tf_op jit(solution)/shard_map/ppermute | solution.py:46
  115.2 13.8 %collective-permute-done.22 = bf16[1,2,2,96,384]{4,3,2,1,0:T(8,128)(2,1)S(1)} collective-permute-done((bf16[1,2,2,96,384]{4,3,2,1,0:T(8,128)(2,1)S(1)}, bf16[1,2,2,96,384]{4,3,2,1,0:T(8,128)(2,1)S(1)}, u32[]{:S(2)}, u32[]{:S(2)}) %collective-permute-start.22) | collective-permute-done | bytes 294944 | tf_op jit(solution)/shard_map/ppermute | solution.py:46
  152.8 6.1 %collective-permute-done.28 = bf16[1,768,384]{2,1,0:T(8,128)(2,1)S(1)} collective-permute-done((bf16[1,768,384]{2,1,0:T(8,128)(2,1)S(1)}, bf16[1,768,384]{2,1,0:T(8,128)(2,1)S(1)}, u32[]{:S(2)}, u32[]{:S(2)}) %collective-permute-start.28) | collective-permute-done | bytes 589856 | tf_op jit(solution)/shard_map/ppermute | solution.py:46
  160.3 10.8 %collective-permute-done.30 = bf16[1,768,384]{2,1,0:T(8,128)(2,1)S(1)} collective-permute-done((bf16[1,768,384]{2,1,0:T(8,128)(2,1)S(1)}, bf16[1,768,384]{2,1,0:T(8,128)(2,1)S(1)}, u32[]{:S(2)}, u32[]{:S(2)}) %collective-permute-start.30) | collective-permute-done | bytes 589856 | tf_op jit(solution)/shard_map/ppermute | solution.py:46
  178.1 17.0 %collective-permute-done.33 = bf16[384,384]{1,0:T(8,128)(2,1)S(1)} collective-permute-done((bf16[384,384]{1,0:T(8,128)(2,1)S(1)}, bf16[384,384]{1,0:T(8,128)(2,1)S(1)}, u32[]{:S(2)}, u32[]{:S(2)}) %collective-permute-start.33) | collective-permute-done | bytes 294944 | tf_op jit(solution)/shard_map/ppermute | solution.py:46
  195.8 4.5 %attend_back.1 = (bf16[256,192]{1,0:T(8,128)(2,1)S(1)}, f32[2,128,384]{2,1,0:T(8,128)S(1)}, bf16[2,128,384]{2,1,0:T(8,128)(2,1)S(1)}, f32[8,128]{1,0:T(8,128)S(1)}) custom-call(s32[14]{0:T(128)S(1)} %copy-done, bf16[512,576]{1,0:T(8,128)(2,1)S(1)} %get-tuple-element.288.qkv, f32[3,256,512]{2,1,0:T(8,128)S(1)} %get-tuple-element.289.probs_in, ...), custom_call_target="tpu_custom_call" | custom-call | flops 2000000000 | bytes 8000000 | tf_op jit(solution)/shard_map/attend_back/pallas_call | solution.py:100
  209.4 7.4 %collective-permute-done.40 = f32[8,128]{1,0:T(8,128)S(1)} collective-permute-done((f32[8,128]{1,0:T(8,128)S(1)}, f32[8,128]{1,0:T(8,128)S(1)}, u32[]{:S(2)}, u32[]{:S(2)}) %collective-permute-start.40) | collective-permute-done | bytes 4128 | tf_op jit(solution)/shard_map/ppermute | solution.py:46
  220.9 9.7 %collective-permute-done.43 = f32[8,128]{1,0:T(8,128)S(1)} collective-permute-done((f32[8,128]{1,0:T(8,128)S(1)}, f32[8,128]{1,0:T(8,128)S(1)}, u32[]{:S(2)}, u32[]{:S(2)}) %collective-permute-start.43) | collective-permute-done | bytes 4128 | tf_op jit(solution)/shard_map/ppermute | solution.py:46
  235.9 6.9 %collective-permute-done.44.got = bf16[128,1536]{1,0:T(8,128)(2,1)S(1)} collective-permute-done((bf16[128,1536]{1,0:T(8,128)(2,1)S(1)}, bf16[128,1536]{1,0:T(8,128)(2,1)S(1)}, u32[]{:S(2)}, u32[]{:S(2)}) %collective-permute-start.44) | collective-permute-done | bytes 393248 | tf_op jit(solution)/shard_map/ppermute | solution.py:46
  249.0 12.7 %collective-permute-done.52 = bf16[384,384]{1,0:T(8,128)(2,1)S(1)} collective-permute-done((bf16[384,384]{1,0:T(8,128)(2,1)S(1)}, bf16[384,384]{1,0:T(8,128)(2,1)S(1)}, u32[]{:S(2)}, u32[]{:S(2)}) %collective-permute-start.52) | collective-permute-done | bytes 294944 | tf_op jit(solution)/shard_map/ppermute | solution.py:46
  261.7 6.4 %collective-permute-done.53 = bf16[384,384]{1,0:T(8,128)(2,1)S(1)} collective-permute-done((bf16[384,384]{1,0:T(8,128)(2,1)S(1)}, bf16[384,384]{1,0:T(8,128)(2,1)S(1)}, u32[]{:S(2)}, u32[]{:S(2)}) %collective-permute-start.53) | collective-permute-done | bytes 294944 | tf_op jit(solution)/shard_map/ppermute | solution.py:46
  269.5 4.1 %collective-permute-done.46 = bf16[192,768]{1,0:T(8,128)(2,1)S(1)} collective-permute-done((bf16[192,768]{1,0:T(8,128)(2,1)S(1)}, bf16[192,768]{1,0:T(8,128)(2,1)S(1)}, u32[]{:S(2)}, u32[]{:S(2)}) %collective-permute-start.46) | collective-permute-done | bytes 294944 | tf_op jit(solution)/shard_map/ppermute | solution.py:46
  275.5 4.4 %collective-permute-done.49.refs_1_ = bf16[2,2,96,384]{3,2,1,0:T(8,128)(2,1)S(1)} collective-permute-done((bf16[2,2,96,384]{3,2,1,0:T(8,128)(2,1)S(1)}, bf16[2,2,96,384]{3,2,1,0:T(8,128)(2,1)S(1)}, u32[]{:S(2)}, u32[]{:S(2)}) %collective-permute-start.49) | collective-permute-done | bytes 294944 | tf_op jit(solution)/shard_map/ppermute | solution.py:46
  279.9 6.2 %collective-permute-done.54.refs_5_ = bf16[2,2,96,384]{3,2,1,0:T(8,128)(2,1)S(1)} collective-permute-done((bf16[2,2,96,384]{3,2,1,0:T(8,128)(2,1)S(1)}, bf16[2,2,96,384]{3,2,1,0:T(8,128)(2,1)S(1)}, u32[]{:S(2)}, u32[]{:S(2)}) %collective-permute-start.54) | collective-permute-done | bytes 294944 | tf_op jit(solution)/shard_map/ppermute | solution.py:46
  (172 shorter events, 115.9 us)
Async XLA Ops:
  12.7 18.6 %collective-permute-start.2 = (bf16[2,4,96,384]{3,2,1,0:T(8,128)(2,1)S(1)}, bf16[2,4,96,384]{3,2,1,0:T(8,128)(2,1)S(1)}, u32[]{:S(2)}, u32[]{:S(2)}) collective-permute-start(bf16[2,4,96,384]{3,2,1,0:T(8,128)(2,1)S(1)} %get-tuple-element.266), channel_id=1, source_target_pairs={{2,0},{0,2},{3,1},{1,3},{6,4},{4,6},{7,5},{5,7},{10,8},{8,10},{11,... | collective-permute-start | bytes 1769480 | tf_op jit(solution)/shard_map/ppermute | solution.py:46
  12.8 18.0 %collective-permute-start.1 = (bf16[2,104,768]{2,1,0:T(8,128)(2,1)S(1)}, bf16[2,104,768]{2,1,0:T(8,128)(2,1)S(1)}, u32[]{:S(2)}, u32[]{:S(2)}) collective-permute-start(bf16[2,104,768]{2,1,0:T(8,128)(2,1)S(1)} %place.4.own), channel_id=1, source_target_pairs={{16,0},{0,16},{17,1},{1,17},{18,2},{2,18},{19,3},{3,19},{20,4},{4,... | collective-permute-start | bytes 958472 | tf_op jit(solution)/shard_map/ppermute | solution.py:46
  15.6 16.9 %collective-permute-start.4 = (bf16[128,1536]{1,0:T(8,128)(2,1)S(1)}, bf16[128,1536]{1,0:T(8,128)(2,1)S(1)}, u32[]{:S(2)}, u32[]{:S(2)}) collective-permute-start(bf16[128,1536]{1,0:T(8,128)(2,1)S(1)} %bitcast.102), channel_id=1, source_target_pairs={{8,0},{0,8},{9,1},{1,9},{10,2},{2,10},{11,3},{3,11},{12,4},{4,12},... | collective-permute-start | bytes 1179656 | tf_op jit(solution)/shard_map/ppermute | solution.py:46
  34.0 17.4 %collective-permute-start.5 = (bf16[2,2,104,768]{3,2,1,0:T(8,128)(2,1)S(1)}, bf16[2,2,104,768]{3,2,1,0:T(8,128)(2,1)S(1)}, u32[]{:S(2)}, u32[]{:S(2)}) collective-permute-start(bf16[2,2,104,768]{3,2,1,0:T(8,128)(2,1)S(1)} %place.5.own), channel_id=1, source_target_pairs={{8,0},{0,8},{9,1},{1,9},{10,2},{2,10},{11,3},{3,11},{12,4},{4,12},... | collective-permute-start | bytes 1916936 | tf_op jit(solution)/shard_map/ppermute | solution.py:46
  52.1 18.9 %collective-permute-start.12 = (bf16[3,2,96,384]{3,2,1,0:T(8,128)(2,1)S(1)}, bf16[3,2,96,384]{3,2,1,0:T(8,128)(2,1)S(1)}, u32[]{:S(2)}, u32[]{:S(2)}) collective-permute-start(bf16[3,2,96,384]{3,2,1,0:T(8,128)(2,1)S(1)} %get-tuple-element.295), channel_id=1, source_target_pairs={{8,0},{0,8},{9,1},{1,9},{10,2},{2,10},{11,3},{3,11},{12,4},{4,12},... | collective-permute-start | bytes 1327112 | tf_op jit(solution)/shard_map/ppermute | solution.py:46
  53.9 16.4 %collective-permute-start.13 = (bf16[1,2,2,96,384]{4,3,2,1,0:T(8,128)(2,1)S(1)}, bf16[1,2,2,96,384]{4,3,2,1,0:T(8,128)(2,1)S(1)}, u32[]{:S(2)}, u32[]{:S(2)}) collective-permute-start(bf16[1,2,2,96,384]{4,3,2,1,0:T(8,128)(2,1)S(1)} %bitcast.79), channel_id=1, source_target_pairs={{16,0},{0,16},{17,1},{1,17},{18,2},{2,18},{19,3},{3,19},{20,4},{4,... | collective-permute-start | bytes 884744 | tf_op jit(solution)/shard_map/ppermute | solution.py:46
  71.7 21.3 %collective-permute-start.17 = (bf16[3,384,384]{2,1,0:T(8,128)(2,1)S(1)}, bf16[3,384,384]{2,1,0:T(8,128)(2,1)S(1)}, u32[]{:S(2)}, u32[]{:S(2)}) collective-permute-start(bf16[3,384,384]{2,1,0:T(8,128)(2,1)S(1)} %bitcast.62), channel_id=1, source_target_pairs={{4,0},{0,4},{5,1},{1,5},{6,2},{2,6},{7,3},{3,7},{12,8},{8,12},{13,... | collective-permute-start | bytes 2654216 | tf_op jit(solution)/shard_map/ppermute | solution.py:46
  75.7 27.3 %collective-permute-start.19 = (bf16[2,2,2,96,384]{4,3,2,1,0:T(8,128)(2,1)S(1)}, bf16[2,2,2,96,384]{4,3,2,1,0:T(8,128)(2,1)S(1)}, u32[]{:S(2)}, u32[]{:S(2)}) collective-permute-start(bf16[2,2,2,96,384]{4,3,2,1,0:T(8,128)(2,1)S(1)} %get-tuple-element.317), channel_id=1, source_target_pairs={{16,0},{0,16},{17,1},{1,17},{18,2},{2,18},{19,3},{3,19},{20,4},{4,... | collective-permute-start | bytes 1769480 | tf_op jit(solution)/shard_map/ppermute | solution.py:46
  93.0 18.4 %collective-permute-start.20 = (bf16[128,1536]{1,0:T(8,128)(2,1)S(1)}, bf16[128,1536]{1,0:T(8,128)(2,1)S(1)}, u32[]{:S(2)}, u32[]{:S(2)}) collective-permute-start(bf16[128,1536]{1,0:T(8,128)(2,1)S(1)} %get-tuple-element.316.refs_0_), channel_id=1, source_target_pairs={{8,0},{0,8},{9,1},{1,9},{10,2},{2,10},{11,3},{3,11},{12,4},{4,12},... | collective-permute-start | bytes 1179656 | tf_op jit(solution)/shard_map/ppermute | solution.py:46
  111.4 19.9 %collective-permute-start.24 = (bf16[2,384,384]{2,1,0:T(8,128)(2,1)S(1)}, bf16[2,384,384]{2,1,0:T(8,128)(2,1)S(1)}, u32[]{:S(2)}, u32[]{:S(2)}) collective-permute-start(bf16[2,384,384]{2,1,0:T(8,128)(2,1)S(1)} %bitcast.72), channel_id=1, source_target_pairs={{4,0},{0,4},{5,1},{1,5},{6,2},{2,6},{7,3},{3,7},{12,8},{8,12},{13,... | collective-permute-start | bytes 1769480 | tf_op jit(solution)/shard_map/ppermute | solution.py:46
  142.7 16.2 %collective-permute-start.28 = (bf16[1,768,384]{2,1,0:T(8,128)(2,1)S(1)}, bf16[1,768,384]{2,1,0:T(8,128)(2,1)S(1)}, u32[]{:S(2)}, u32[]{:S(2)}) collective-permute-start(bf16[1,768,384]{2,1,0:T(8,128)(2,1)S(1)} %get-tuple-element.378), channel_id=1, source_target_pairs={{4,0},{0,4},{5,1},{1,5},{6,2},{2,6},{7,3},{3,7},{12,8},{8,12},{13,... | collective-permute-start | bytes 1769480 | tf_op jit(solution)/shard_map/ppermute | solution.py:46
  151.3 19.8 %collective-permute-start.30 = (bf16[1,768,384]{2,1,0:T(8,128)(2,1)S(1)}, bf16[1,768,384]{2,1,0:T(8,128)(2,1)S(1)}, u32[]{:S(2)}, u32[]{:S(2)}) collective-permute-start(bf16[1,768,384]{2,1,0:T(8,128)(2,1)S(1)} %get-tuple-element.390), channel_id=1, source_target_pairs={{4,0},{0,4},{5,1},{1,5},{6,2},{2,6},{7,3},{3,7},{12,8},{8,12},{13,... | collective-permute-start | bytes 1769480 | tf_op jit(solution)/shard_map/ppermute | solution.py:46
  173.0 22.1 %collective-permute-start.32 = (bf16[2,128,1536]{2,1,0:T(8,128)(2,1)S(1)}, bf16[2,128,1536]{2,1,0:T(8,128)(2,1)S(1)}, u32[]{:S(2)}, u32[]{:S(2)}) collective-permute-start(bf16[2,128,1536]{2,1,0:T(8,128)(2,1)S(1)} %get-tuple-element.397), channel_id=1, source_target_pairs={{2,0},{0,2},{3,1},{1,3},{6,4},{4,6},{7,5},{5,7},{10,8},{8,10},{11,... | collective-permute-start | bytes 2359304 | tf_op jit(solution)/shard_map/ppermute | solution.py:46
  173.1 22.0 %collective-permute-start.33 = (bf16[384,384]{1,0:T(8,128)(2,1)S(1)}, bf16[384,384]{1,0:T(8,128)(2,1)S(1)}, u32[]{:S(2)}, u32[]{:S(2)}) collective-permute-start(bf16[384,384]{1,0:T(8,128)(2,1)S(1)} %bitcast.115), channel_id=1, source_target_pairs={{16,0},{0,16},{17,1},{1,17},{18,2},{2,18},{19,3},{3,19},{20,4},{4,... | collective-permute-start | bytes 884744 | tf_op jit(solution)/shard_map/ppermute | solution.py:46
  173.1 22.7 %collective-permute-start.31 = (bf16[128,1536]{1,0:T(8,128)(2,1)S(1)}, bf16[128,1536]{1,0:T(8,128)(2,1)S(1)}, u32[]{:S(2)}, u32[]{:S(2)}) collective-permute-start(bf16[128,1536]{1,0:T(8,128)(2,1)S(1)} %get-tuple-element.395.d_own), channel_id=1, source_target_pairs={{4,0},{0,4},{5,1},{1,5},{6,2},{2,6},{7,3},{3,7},{12,8},{8,12},{13,... | collective-permute-start | bytes 1179656 | tf_op jit(solution)/shard_map/ppermute | solution.py:46
  173.5 27.9 %collective-permute-start.34 = (bf16[384,384]{1,0:T(8,128)(2,1)S(1)}, bf16[384,384]{1,0:T(8,128)(2,1)S(1)}, u32[]{:S(2)}, u32[]{:S(2)}) collective-permute-start(bf16[384,384]{1,0:T(8,128)(2,1)S(1)} %bitcast.113), channel_id=1, source_target_pairs={{16,0},{0,16},{17,1},{1,17},{18,2},{2,18},{19,3},{3,19},{20,4},{4,... | collective-permute-start | bytes 884744 | tf_op jit(solution)/shard_map/ppermute | solution.py:46
  176.3 28.8 %collective-permute-start.37 = (bf16[1,768,384]{2,1,0:T(8,128)(2,1)S(1)}, bf16[1,768,384]{2,1,0:T(8,128)(2,1)S(1)}, u32[]{:S(2)}, u32[]{:S(2)}) collective-permute-start(bf16[1,768,384]{2,1,0:T(8,128)(2,1)S(1)} %get-tuple-element.422), channel_id=1, source_target_pairs={{4,0},{0,4},{5,1},{1,5},{6,2},{2,6},{7,3},{3,7},{12,8},{8,12},{13,... | collective-permute-start | bytes 1769480 | tf_op jit(solution)/shard_map/ppermute | solution.py:46
  233.7 28.0 %collective-permute-start.52 = (bf16[384,384]{1,0:T(8,128)(2,1)S(1)}, bf16[384,384]{1,0:T(8,128)(2,1)S(1)}, u32[]{:S(2)}, u32[]{:S(2)}) collective-permute-start(bf16[384,384]{1,0:T(8,128)(2,1)S(1)} %bitcast.111), channel_id=1, source_target_pairs={{16,0},{0,16},{17,1},{1,17},{18,2},{2,18},{19,3},{3,19},{20,4},{4,... | collective-permute-start | bytes 884744 | tf_op jit(solution)/shard_map/ppermute | solution.py:46
  244.3 23.9 %collective-permute-start.53 = (bf16[384,384]{1,0:T(8,128)(2,1)S(1)}, bf16[384,384]{1,0:T(8,128)(2,1)S(1)}, u32[]{:S(2)}, u32[]{:S(2)}) collective-permute-start(bf16[384,384]{1,0:T(8,128)(2,1)S(1)} %bitcast.119), channel_id=1, source_target_pairs={{16,0},{0,16},{17,1},{1,17},{18,2},{2,18},{19,3},{3,19},{20,4},{4,... | collective-permute-start | bytes 884744 | tf_op jit(solution)/shard_map/ppermute | solution.py:46
  245.9 27.7 %collective-permute-start.46 = (bf16[192,768]{1,0:T(8,128)(2,1)S(1)}, bf16[192,768]{1,0:T(8,128)(2,1)S(1)}, u32[]{:S(2)}, u32[]{:S(2)}) collective-permute-start(bf16[192,768]{1,0:T(8,128)(2,1)S(1)} %bitcast.112), channel_id=1, source_target_pairs={{16,0},{0,16},{17,1},{1,17},{18,2},{2,18},{19,3},{3,19},{20,4},{4,... | collective-permute-start | bytes 884744 | tf_op jit(solution)/shard_map/ppermute | solution.py:46
  247.2 21.7 %collective-permute-start.47 = (f32[8,128]{1,0:T(8,128)S(1)}, f32[8,128]{1,0:T(8,128)S(1)}, u32[]{:S(2)}, u32[]{:S(2)}) collective-permute-start(f32[8,128]{1,0:T(8,128)S(1)} %add.123.own), channel_id=1, source_target_pairs={{4,0},{0,4},{5,1},{1,5},{6,2},{2,6},{7,3},{3,7},{12,8},{8,12},{13,... | collective-permute-start | bytes 12296 | tf_op jit(solution)/shard_map/ppermute | solution.py:46
  248.5 37.6 %collective-permute-start.48 = (bf16[128,1536]{1,0:T(8,128)(2,1)S(1)}, bf16[128,1536]{1,0:T(8,128)(2,1)S(1)}, u32[]{:S(2)}, u32[]{:S(2)}) collective-permute-start(bf16[128,1536]{1,0:T(8,128)(2,1)S(1)} %add_convert_fusion.1.own), channel_id=1, source_target_pairs={{1,0},{0,1},{3,2},{2,3},{5,4},{4,5},{7,6},{6,7},{9,8},{8,9},{11,10... | collective-permute-start | bytes 1179656 | tf_op jit(solution)/shard_map/ppermute | solution.py:46
  261.7 18.1 %collective-permute-start.49 = (bf16[2,2,96,384]{3,2,1,0:T(8,128)(2,1)S(1)}, bf16[2,2,96,384]{3,2,1,0:T(8,128)(2,1)S(1)}, u32[]{:S(2)}, u32[]{:S(2)}) collective-permute-start(bf16[2,2,96,384]{3,2,1,0:T(8,128)(2,1)S(1)} %get-tuple-element.473), channel_id=1, source_target_pairs={{8,0},{0,8},{9,1},{1,9},{10,2},{2,10},{11,3},{3,11},{12,4},{4,12},... | collective-permute-start | bytes 884744 | tf_op jit(solution)/shard_map/ppermute | solution.py:46
  268.8 17.3 %collective-permute-start.54 = (bf16[2,2,96,384]{3,2,1,0:T(8,128)(2,1)S(1)}, bf16[2,2,96,384]{3,2,1,0:T(8,128)(2,1)S(1)}, u32[]{:S(2)}, u32[]{:S(2)}) collective-permute-start(bf16[2,2,96,384]{3,2,1,0:T(8,128)(2,1)S(1)} %get-tuple-element.480), channel_id=1, source_target_pairs={{8,0},{0,8},{9,1},{1,9},{10,2},{2,10},{11,3},{3,11},{12,4},{4,12},... | collective-permute-start | bytes 884744 | tf_op jit(solution)/shard_map/ppermute | solution.py:46
  (48 other events, 365.0 us)

commit v2 on v1

--- a/solution.py
+++ b/solution.py
@@ -353,30 +353,59 @@
             out[e, :, 2 * lane :] = dot_tn(grads[:, lanes], hidden[...]).astype(out.dtype)
 
 
-def split_body(here, own, *refs, which):
+def table_parts(values):
+    high = values.astype(bf16)
+    return jnp.concatenate([high, (values - high.astype(f32)).astype(bf16)], axis=0)
+
+
+def table_value(parts):
+    half = parts.shape[0] // 2
+    return parts[:half].astype(f32) + parts[half:].astype(f32)
+
+
+def split_body(here, own, *refs, which, count, tail):
     *got, keep, send = refs
-    count = own.shape[0]
+    size = keep.shape[0] - tail
+
+    def piece(ref, at):
+        if size % 8 == 0:
+            return ref[aligned(at, size)]
+        value = ref[:size]
+        for i in range(1, count):
+            value = jnp.where(at == i, ref[i * size : (i + 1) * size], value)
+        return value
+
     for e in range(count):
         at = here[which] + e
         at = jnp.where(at >= count, at - count, at)
-        total = own[at]
+        total = piece(own, at)
         for ref in got:
-            total = total + ref[at].astype(f32)
+            total = total + piece(ref, at).astype(f32)
         if e:
-            send[e - 1] = total.astype(bf16)
+            send[e - 1, :size] = total.astype(bf16)
         else:
-            keep[...] = total
-
-
-def split(here, which, own, got):
-    shape = own.shape[1:]
+            keep[:size] = total
+    if tail:
+        total = own[count * size :]
+        for ref in got:
+            total = total + table_value(ref[count * size :])
+        parts = table_parts(total)
+        keep[size:] = table_value(parts)
+        for e in range(count - 1):
+            send[e, size:] = parts
+
+
+def split(here, which, count, own, got, tail=0):
+    size = (own.shape[0] - tail // 2) // count
     return call(
         split_body,
         "split",
         here,
-        [own, *(g.reshape(own.shape) for g in got)],
-        [(shape, f32), ((own.shape[0] - 1, *shape), bf16)],
+        [own, *got],
+        [((size + tail // 2, own.shape[1]), f32), ((count - 1, size + tail, own.shape[1]), bf16)],
         which=which,
+        count=count,
+        tail=tail // 2,
     )
 
 
@@ -508,7 +537,7 @@
 
 
 def attn_grad_body(
-    here, inputs, d_query, d_keep, d_got, d_own, d_far, attended, w_own, w_other,
+    here, inputs, d_query, d_keep, d_got, d_own, d_far, attended, w_own, w_other, table,
     g_keep, g_send, keep, send, d_qkv, *, sizes
 ):
     rows, heads, width, query_blocks, key_blocks, span = sizes
@@ -523,8 +552,13 @@
         g_keep[:, lanes] = part[:rows]
         g_send[:, lanes] = part[rows:].astype(bf16)
         two = jnp.concatenate([inputs[b * rows : (b + 1) * rows, lanes] for b in query_blocks], axis=0)
-        out[:, : 3 * inner] = dot_tn(two, d_qkv[...]).astype(out.dtype)
-        out[:, 3 * inner :] = dot_tn(tall((d_own, d_far), lanes), attended[...]).astype(out.dtype)
+        out[:half, : 3 * inner] = dot_tn(two, d_qkv[...]).astype(out.dtype)
+        out[:half, 3 * inner :] = dot_tn(tall((d_own, d_far), lanes), attended[...]).astype(out.dtype)
+    parts = table_parts(table[...])
+    keep[half:] = jnp.zeros((keep.shape[0] - half, keep.shape[1]), f32)
+    send[half:] = jnp.zeros((send.shape[0] - half, send.shape[1]), bf16)
+    keep[half:, :lane] = table_value(parts)
+    send[half:, :lane] = parts
 
 
 def input_grad_body(here, own, got, tokens, gains, d_residual, out, *, dims):
@@ -540,10 +574,10 @@
     out[...] = (residual[...] + reorder(total, dims, ffn_order, True)).astype(bf16)
 
 
-def attn_final_body(here, own, got, wq, wk, wv, gain, gq, gk, gv, go, grad_gain):
-    inner = own.shape[1] // 4
-
-    def finish(low, high):
+def attn_final_body(here, own, got, wq, wk, wv, gain, gq, gk, gv, go, grad_gain, table, *, heads):
+    part, inner = gq.shape[0], own.shape[1] // 4
+
+    def finish(low, high, low_table, high_table):
         grads = [
             jnp.concatenate([m[:, i * inner : (i + 1) * inner] for m in (low, high)], axis=1)
             for i in range(4)
@@ -554,14 +588,18 @@
             sums = sums + grad * weights[...].astype(f32)
         go[...] = grads[3]
         grad_gain[...] = sum_row(sums) / gain[...].astype(f32)
+        table[...] = jnp.concatenate([low_table[:heads], high_table[:heads]], axis=0)
+
+    values = own[:part], got[:part].astype(f32)
+    tables = own[part:, :lane], table_value(got[part:, :lane])
 
     @pl.when(here[at_yl] == 0)
     def _():
-        finish(own[...], got[...].astype(f32))
+        finish(*values, *tables)
 
     @pl.when(here[at_yl] != 0)
     def _():
-        finish(got[...].astype(f32), own[...])
+        finish(*values[::-1], *tables[::-1])
 
 
 def local(
@@ -594,6 +632,7 @@
     key_blocks = 4 * outer
     sizes = (rows, heads, width, (0, 2), key_blocks, length)
 
+    tail = 16
     split_deep = deep == 2 and (4 * part) % lane == 0
     deep_blocks = deep if split_deep else 1
     yh, yl, k, zl, zh = (lax.axis_index(a) for a in ("yh", "yl", "k", "zl", "zh"))
@@ -757,16 +796,13 @@
         dims=dims,
     )
 
-    low_two, far[0], nears[1], *rest_y = tick(low_two, far[0], nears[1], *rest_y)
+    low_two, far[0], nears[1] = tick(low_two, far[0], nears[1])
     far_two, core_two = swap(low_two, "zl"), swap(low_two, "k")
     far_y[0] = over_y(far[0])
-    core_two, far[1], nears[1] = tick(core_two, far[1], nears[1])
+    core_two, far[1], nears[1], *rest_y = tick(core_two, far[1], nears[1], *rest_y)
     far[2] = over_zh(nears[1])
     far_y[1] = over_y(far[1])
 
-    far_two, core_two, *far_y[0] = tick(far_two, core_two, *far_y[0])
-    farcore_two = swap(far_two, "k")
-    ffn_rows = [low_two, core_two, far_two, farcore_two]
 
     def weights_of(j):
         g = next(g for g, group in enumerate(groups) if j in group)
@@ -817,7 +853,8 @@
             total = keep + got[0].astype(f32)
             got = send_sums([total[e].astype(bf16) for e in range(1, outer)], "yh")
             keep = total[0]
-        return split(here, at_zh, keep.reshape(deep, 4 * part, 3 * lane), got)
+        flat = [v.reshape(deep * 4 * part, 3 * lane) for v in (keep, *got)]
+        return split(here, at_zh, deep, flat[0], flat[1:])
 
     def sum_zh(keep, send):
         got = send_sums([send[e] for e in range(deep - 1)], "zh")
@@ -841,15 +878,23 @@
             chunks=count,
         )
 
+    far[2], far_two, core_two, *far_y[0] = tick(far[2], far_two, core_two, *far_y[0])
+    far_y[2] = over_y(far[2])
+    farcore_two = swap(far_two, "k")
+    ffn_rows = [low_two, core_two, far_two, farcore_two]
     first_0, hidden_0 = ffn(0)
-
-    far[2], first_0, hidden_0 = tick(far[2], first_0, hidden_0)
-    far_y[2] = over_y(far[2])
     grads = [None] * chunks
     grad_got, sums, zh_sums = [None] * chunks, [None] * chunks, [None] * chunks
-    grads[0] = ffn_grad(first_0, hidden_0)
     firsts, hiddens = [first_0], [hidden_0]
     for j in range(1, chunks):
+        if j == chunks - 1:
+            grads[0] = ffn_grad(firsts[0], hiddens[0])
+            low_two, *flat = tick(low_two, *firsts, *hiddens, *grads[0])
+            firsts, hiddens, grads[0] = flat[:j], flat[j : 2 * j], flat[2 * j :]
+        elif j == 1:
+            low_two, *flat = tick(low_two, *firsts, *hiddens)
+            firsts, hiddens = flat[:1], flat[1:]
+        ffn_rows[0] = low_two
         first, hidden = ffn(j)
         firsts.append(first)
         hiddens.append(hidden)
@@ -866,21 +911,26 @@
     grads[1], firsts, hiddens = flat[:2], [None, None, *flat[2:4]], flat[4:]
     core_got = swap(core_send, "zl")
     grad_got[1] = swap(grads[1][1], "yl")
+    mixed_keep, mixed_send = back(hiddens, slice(2 * lane, 3 * lane))
+    mixed_keep, mixed_send, *flat = tick(mixed_keep, mixed_send, *firsts[2:], *hiddens)
+    firsts, hiddens = [None, None, *flat[:2]], flat[2:]
+    mixed_got = swap(mixed_send, "k")
     grads[2] = ffn_grad(firsts[2], hiddens[2])
     grads[3] = ffn_grad(firsts[3], hiddens[3])
-    mixed_keep, mixed_send = back(hiddens, slice(2 * lane, 3 * lane))
-    grad_keep, mixed_keep, *flat = tick(grads[0][0], mixed_keep, mixed_send, *grads[2], *grads[3])
-    mixed_send, grads[2], grads[3] = flat[0], flat[1:3], flat[3:]
+    mixed_keep, mixed_got, *flat = tick(mixed_keep, mixed_got, grads[0][0], *grads[2], *grads[3])
+    grad_keep, grads[2], grads[3] = flat[0], flat[1:3], flat[3:]
+    mixed_keep, mixed_send = pair(mixed_keep, mixed_got)
     sums[0] = sum_y(grad_keep, grad_got[0])
     core = (core_keep + core_got.astype(f32)).astype(bf16)
 
-    core, mixed_keep, mixed_send, *flat = tick(
-        core, mixed_keep, mixed_send, *sums[0], *grads[2], *grads[3]
+    core, mixed_keep, mixed_send, grad_keep, *flat = tick(
+        core, mixed_keep, mixed_send, grads[1][0], *sums[0], *grads[2], *grads[3]
     )
     sums[0], grads[2], grads[3] = flat[:2], flat[2:4], flat[4:]
     core_other = swap(core, "x")
     zh_sums[0] = sum_zh(*sums[0])
-    sums[1] = sum_y(grads[1][0], grad_got[1])
+    mixed_got = swap(mixed_send, "zl")
+    sums[1] = sum_y(grad_keep, grad_got[1])
     d_residual, d_low = kernel(
         residual_back_body,
         "residual_back",
@@ -889,17 +939,15 @@
         dims=dims,
     )
 
-    d_low, mixed_send, *flat = tick(d_low, mixed_send, *sums[1], *grads[2])
-    sums[1], grads[2] = flat[:2], flat[2:]
+    d_low, *flat = tick(d_low, *sums[1], *grads[2], *zh_sums[0])
+    sums[1], grads[2], zh_sums[0] = flat[:2], flat[2:4], flat[4:]
     d_far = swap(d_low, "yl")
     grad_got[2] = swap(grads[2][1], "yl")
     zh_sums[1] = sum_zh(*sums[1])
-    mixed_got = swap(mixed_send, "k")
-    mixed_keep, mixed_got, *zh_sums[0] = tick(mixed_keep, mixed_got, *zh_sums[0])
-    mixed_keep, mixed_send = pair(mixed_keep, mixed_got)
-
-    d_far, mixed_keep, mixed_send = tick(d_far, mixed_keep, mixed_send)
-    mixed_got = swap(mixed_send, "zl")
+
+    d_far, mixed_keep, mixed_got = tick(d_far, mixed_keep, mixed_got)
+    mixed_half = (mixed_keep + mixed_got.astype(f32)).astype(bf16)
+    mixed_other = swap(mixed_half, "x")
     d_query, d_keep, d_send, grad_table = kernel(
         attend_back_body,
         "attend_back",
@@ -915,83 +963,84 @@
         buckets=buckets,
     )
 
-    def table_sum(value, axis):
-        if lax.axis_size(axis) == 2:
-            return value + swap(value, axis)
-        return jnp.sum(both(value, axis), axis=0)
-
     d_query, d_keep, d_send, grad_table, *zh_sums[1] = tick(
         d_query, d_keep, d_send, grad_table, *zh_sums[1]
     )
-    done_a = ffn_split(zh_sums[: chunks // 2])
     d_got = swap(d_send, "k")
-    grad_table = table_sum(grad_table, "k")
     if outer > 1:
-        grad_table = table_sum(grad_table, "yh")
         total = (d_keep + d_got.astype(f32)).reshape(outer, 2, rows, 2 * inner)
         arrived = send_sums([total[e].astype(bf16) for e in range(1, outer)], "yh")
         d_keep, d_got = total[0], sum(a.astype(f32) for a in arrived)
     g_keep, g_send, keep, send = kernel(
         attn_grad_body,
         "attn_grad",
-        [attn_input, d_query, d_keep, d_got, d_low, d_far, attended, w_own, w_other],
+        [attn_input, d_query, d_keep, d_got, d_low, d_far, attended, w_own, w_other, grad_table],
         [
             ((rows, wide), f32),
             ((rows, wide), bf16),
-            ((half, 4 * inner), f32),
-            ((half, 4 * inner), bf16),
+            ((half + tail // 2, 4 * inner), f32),
+            ((half + tail, 4 * inner), bf16),
         ],
         [pltpu.VMEM((2 * rows, 3 * inner), bf16)],
         sizes=sizes,
     )
 
-    g_keep, g_send, keep, send, grad_table, *flat = tick(
-        g_keep, g_send, keep, send, grad_table, grad_got[2], *done_a
-    )
-    grad_got[2], done_a = flat[0], flat[1:]
+    g_keep, g_send, keep, send, grad_got[2], *grads[3] = tick(
+        g_keep, g_send, keep, send, grad_got[2], *grads[3]
+    )
     got = [swap(send, "k")]
-    g_got = swap(g_send, "yl")
-    grad_table = table_sum(grad_table, "zl")
+    grad_got[3] = swap(grads[3][1], "yl")
+    done_a = ffn_split(zh_sums[: chunks // 2])
+    keep, grad_keep = tick(keep, grads[2][0])
+    if outer > 1:
+        keep, send = split(here, at_yh, outer, keep, got, tail)
+        got = send_sums([send[e] for e in range(outer - 1)], "yh")
+    sums[2] = sum_y(grad_keep, grad_got[2])
+    keep, send = split(here, at_zl, 2, keep, got, tail)
 
     def spread(done):
         other = swap(done[2], "zl")
-        return [done[0], other, swap(done[1], "k"), swap(other, "k")]
-
-    if outer > 1:
-        total = (keep + got[0].astype(f32)).reshape(outer, -1, 4 * inner)
-        pieces = [lax.dynamic_index_in_dim(total, (yh + e) % outer, 0, False) for e in range(outer)]
-        keep, got = pieces[0], send_sums([p.astype(bf16) for p in pieces[1:]], "yh")
-    sums[2] = sum_y(grads[2][0], grad_got[2])
-    keep, send = split(here, at_zl, keep.reshape(2, deep * 2 * part, 4 * inner), got)
-
-    keep, send, mixed_got, grad_table, *flat = tick(
-        keep, send, mixed_got, grad_table, *sums[2], *grads[3]
-    )
-    sums[2], grads[3] = flat[:2], flat[2:4]
+        return [done[0], other, swap(done[1], "k")]
+
+    def over_cores(group):
+        return [*group, swap(group[1], "k")]
+
+    keep, send, g_keep, g_send, residual, *flat = tick(
+        keep, send, g_keep, g_send, residual, *sums[2], *done_a
+    )
+    sums[2], done_a = flat[:2], flat[2:]
     got = send_sums([send[0]], "zl")
-    grad_got[3] = swap(grads[3][1], "yl")
     zh_sums[2] = sum_zh(*sums[2])
-    grad_table = table_sum(grad_table, "zh")
-    mixed_half = (mixed_keep + mixed_got.astype(f32)).astype(bf16)
-    g_sum = (g_keep + g_got.astype(f32)).astype(bf16)
-    keep, send = split(here, at_zh, keep.reshape(deep, 2 * part, 4 * inner), got)
-
-    keep, send, g_sum, mixed_half, grad_table, *done_a = tick(
-        keep, send, g_sum, mixed_half, grad_table, *done_a
-    )
-    got = send_sums([send[e] for e in range(deep - 1)], "zh")
-    g_other = swap(g_sum, "x")
-    mixed_other = swap(mixed_half, "x")
-
-    sums[3] = sum_y(grads[3][0], grad_got[3])
-    grad_table = both(grad_table, "yl")
+    group_a = spread(done_a)
+    g_got = swap(g_send, "yl")
     (mixed,) = kernel(
         mixed_body, "mixed", [mixed_half, mixed_other, residual], [((rows, wide), bf16)], dims=dims
     )
-    mixed, *flat = tick(mixed, *sums[3], *done_a)
-    sums[3], done_a = flat[:2], flat[2:]
+    keep, send = split(here, at_zh, deep, keep, got, tail)
+
+    keep, send, mixed, grad_keep, *flat = tick(
+        keep, send, mixed, grads[3][0], *zh_sums[2], *group_a[:2]
+    )
+    zh_sums[2], group_a[:2] = flat[:deep], flat[deep:]
+    got = send_sums([send[e] for e in range(deep - 1)], "zh")
+    sums[3] = sum_y(grad_keep, grad_got[3])
     zh_sums[3] = sum_zh(*sums[3])
-    group_a = spread(done_a)
+    keep, send = split(here, at_yl, 2, keep, got, tail)
+
+    keep, send, g_keep, g_got = tick(keep, send, g_keep, g_got)
+    got = swap(send[0], "yl")
+    got, zh_sums[3][0] = tick(got, zh_sums[3][0])
+    g_sum = (g_keep + g_got.astype(f32)).astype(bf16)
+    g_other = swap(g_sum, "x")
+    group_a = over_cores(group_a)
+    group_b = over_cores(spread(ffn_split(zh_sums[chunks // 2 :])))
+    grad_query, grad_key, grad_value, grad_out, gain_row, grad_table = kernel(
+        attn_final_body,
+        "attn_final",
+        [keep, got, w_query, w_key, w_value, norm_one[None]],
+        [((part, 2 * inner), f32)] * 4 + [((1, part), f32), ((heads_dev, lane), f32)],
+        heads=heads,
+    )
     (input_grad,) = kernel(
         input_grad_body,
         "input_grad",
@@ -999,18 +1048,7 @@
         [((rows, wide), bf16)],
         dims=dims,
     )
-    keep, send = split(here, at_yl, keep.reshape(2, part, 4 * inner), got)
-
-    keep, send, grad_table = tick(keep, send, grad_table)
-    got = swap(send[0], "yl")
-    keep, input_grad = tick(keep, input_grad)
-    group_b = spread(ffn_split(zh_sums[chunks // 2 :]))
-    grad_query, grad_key, grad_value, grad_out, gain_row = kernel(
-        attn_final_body,
-        "attn_final",
-        [keep, got, w_query, w_key, w_value, norm_one[None]],
-        [((part, 2 * inner), f32)] * 4 + [((1, part), f32)],
-    )
+    gain_row, input_grad = tick(gain_row, input_grad)
     grad_gate, grad_up, grad_down, grad_gains = kernel(
         ffn_final_body,
         "ffn_final",
@@ -1028,7 +1066,7 @@
         grad_key,
         grad_value,
         grad_out.T,
-        grad_table[:, :heads, :buckets].reshape(heads_dev, buckets),
+        grad_table[:, :buckets],
         grad_gains[1],
         grad_gate,
         grad_up,

time: 297 us -> 271 us (0.912)
  waiting for transfers between devices: 179 us -> 163 us
  starting transfers between devices: 55.1 us -> 46.7 us
    ppermute x59 -> x55, waiting for transfers between devices: 179 us -> 163 us  [fetch(): lax.ppermute(value, axis, [((i + step) % size, i) for i in range(size)])]
    ppermute x59 -> x55, starting transfers between devices: 55.1 us -> 46.7 us  [fetch(): lax.ppermute(value, axis, [((i + step) % size, i) for i in range(size)])]
    pallas_call x40 -> x39, Pallas kernels: 58.7 us -> 58.3 us  [call(): pl.pallas_call(functools.partial(body, **static), out_shape=tuple((jax.Sh...]
  transfers between devices with their start and end apart: 59 -> 55, of which waited for: 32 -> 33; matrix products, arithmetic and copies ran while one was open for 0% -> 0% of each run, Pallas kernels for 16% -> 17%
where the time goes in v2:
time: 271 us
  waiting for transfers between devices  163 us (60%)
  Pallas kernels  58.3 us (22%)
  starting transfers between devices  46.7 us (17%)
    ppermute x55, waiting for transfers between devices, fetch(): lax.ppermute(value, axis, [((i + step) % size, i) for i in range(size)])  163 us
    pallas_call x39, Pallas kernels, call(): pl.pallas_call(functools.partial(body, **static), out_shape=tuple((jax.Sh...  58.3 us
    ppermute x55, starting transfers between devices, fetch(): lax.ppermute(value, axis, [((i + step) % size, i) for i in range(size)])  46.7 us
  transfers between devices with their start and end apart: 55, of which 33 were waited for; matrix products, arithmetic and copies ran while one was open for 0% of the time, Pallas kernels for 17%

profile of v2, /device:TPU:0, one launch (start us, length us, event | category | flops | bytes accessed | tf_op | source)
XLA Modules:
  0.0 271.1 jit_solution(12032686968807994300)
XLA Ops:
  4.7 3.0 %collective-permute-start = (bf16[104,768]{1,0:T(8,128)(2,1)}, bf16[104,768]{1,0:T(8,128)(2,1)S(1)}, u32[]{:S(2)}, u32[]{:S(2)}) collective-permute-start(bf16[104,768]{1,0:T(8,128)(2,1)} %get-tuple-element.273), channel_id=1, source_target_pairs={{4,0},{0,4},{5,1},{1,5},{6,2},{2,6},{7,3},{3,7},{12,8},{8,12},{13,... | collective-permute-start | bytes 479240 | tf_op jit(solution)/shard_map/ppermute | solution.py:46
  8.7 3.3 %collective-permute-done.got = bf16[104,768]{1,0:T(8,128)(2,1)S(1)} collective-permute-done((bf16[104,768]{1,0:T(8,128)(2,1)}, bf16[104,768]{1,0:T(8,128)(2,1)S(1)}, u32[]{:S(2)}, u32[]{:S(2)}) %collective-permute-start) | collective-permute-done | bytes 159776 | tf_op jit(solution)/shard_map/ppermute | solution.py:46
  12.7 2.9 %collective-permute-start.1 = (bf16[2,104,768]{2,1,0:T(8,128)(2,1)S(1)}, bf16[2,104,768]{2,1,0:T(8,128)(2,1)S(1)}, u32[]{:S(2)}, u32[]{:S(2)}) collective-permute-start(bf16[2,104,768]{2,1,0:T(8,128)(2,1)S(1)} %place.3.own), channel_id=1, source_target_pairs={{16,0},{0,16},{17,1},{1,17},{18,2},{2,18},{19,3},{3,19},{20,4},{4,... | collective-permute-start | bytes 958472 | tf_op jit(solution)/shard_map/ppermute | solution.py:46
  18.7 12.0 %collective-permute-done.1.got = bf16[2,104,768]{2,1,0:T(8,128)(2,1)S(1)} collective-permute-done((bf16[2,104,768]{2,1,0:T(8,128)(2,1)S(1)}, bf16[2,104,768]{2,1,0:T(8,128)(2,1)S(1)}, u32[]{:S(2)}, u32[]{:S(2)}) %collective-permute-start.1) | collective-permute-done | bytes 319520 | tf_op jit(solution)/shard_map/ppermute | solution.py:46
  35.0 4.2 %collective-permute-done.6.got = bf16[1,2,96,384]{3,2,1,0:T(8,128)(2,1)S(1)} collective-permute-done((bf16[1,2,96,384]{3,2,1,0:T(8,128)(2,1)S(1)}, bf16[1,2,96,384]{3,2,1,0:T(8,128)(2,1)S(1)}, u32[]{:S(2)}, u32[]{:S(2)}) %collective-permute-start.6) | collective-permute-done | bytes 147488 | tf_op jit(solution)/shard_map/ppermute | solution.py:46
  43.5 7.8 %collective-permute-done.5.got = bf16[2,2,104,768]{3,2,1,0:T(8,128)(2,1)S(1)} collective-permute-done((bf16[2,2,104,768]{3,2,1,0:T(8,128)(2,1)S(1)}, bf16[2,2,104,768]{3,2,1,0:T(8,128)(2,1)S(1)}, u32[]{:S(2)}, u32[]{:S(2)}) %collective-permute-start.5) | collective-permute-done | bytes 639008 | tf_op jit(solution)/shard_map/ppermute | solution.py:46
  57.9 5.4 %attend.1 = (bf16[512,576]{1,0:T(8,128)(2,1)S(1)}, f32[3,256,512]{2,1,0:T(8,128)S(1)}, bf16[256,192]{1,0:T(8,128)(2,1)S(1)}, f32[128,1536]{1,0:T(8,128)S(1)}, bf...) custom-call(s32[14]{0:T(128)S(1)} %copy-done, ...), custom_call_target="tpu_custom_call" | custom-call | flops 2000000000 | bytes 8000000 | tf_op jit(solution)/shard_map/attend/pallas_call | solution.py:100
  63.8 6.4 %collective-permute-done.13 = bf16[1,2,2,96,384]{4,3,2,1,0:T(8,128)(2,1)S(1)} collective-permute-done((bf16[1,2,2,96,384]{4,3,2,1,0:T(8,128)(2,1)S(1)}, bf16[1,2,2,96,384]{4,3,2,1,0:T(8,128)(2,1)S(1)}, u32[]{:S(2)}, u32[]{:S(2)}) %collective-permute-start.13) | collective-permute-done | bytes 294944 | tf_op jit(solution)/shard_map/ppermute | solution.py:46
  77.5 6.4 %collective-permute-done.16.got = bf16[128,1536]{1,0:T(8,128)(2,1)S(1)} collective-permute-done((bf16[128,1536]{1,0:T(8,128)(2,1)S(1)}, bf16[128,1536]{1,0:T(8,128)(2,1)S(1)}, u32[]{:S(2)}, u32[]{:S(2)}) %collective-permute-start.16) | collective-permute-done | bytes 393248 | tf_op jit(solution)/shard_map/ppermute | solution.py:46
  87.9 16.6 %collective-permute-done.18 = bf16[2,2,2,96,384]{4,3,2,1,0:T(8,128)(2,1)S(1)} collective-permute-done((bf16[2,2,2,96,384]{4,3,2,1,0:T(8,128)(2,1)S(1)}, bf16[2,2,2,96,384]{4,3,2,1,0:T(8,128)(2,1)S(1)}, u32[]{:S(2)}, u32[]{:S(2)}) %collective-permute-start.18) | collective-permute-done | bytes 589856 | tf_op jit(solution)/shard_map/ppermute | solution.py:46
  104.8 4.2 %collective-permute-done.21.refs_2_ = bf16[128,1536]{1,0:T(8,128)(2,1)S(1)} collective-permute-done((bf16[128,1536]{1,0:T(8,128)(2,1)S(1)}, bf16[128,1536]{1,0:T(8,128)(2,1)S(1)}, u32[]{:S(2)}, u32[]{:S(2)}) %collective-permute-start.21) | collective-permute-done | bytes 393248 | tf_op jit(solution)/shard_map/ppermute | solution.py:46
  109.0 10.8 %collective-permute-done.20 = bf16[1,2,2,96,384]{4,3,2,1,0:T(8,128)(2,1)S(1)} collective-permute-done((bf16[1,2,2,96,384]{4,3,2,1,0:T(8,128)(2,1)S(1)}, bf16[1,2,2,96,384]{4,3,2,1,0:T(8,128)(2,1)S(1)}, u32[]{:S(2)}, u32[]{:S(2)}) %collective-permute-start.20) | collective-permute-done | bytes 294944 | tf_op jit(solution)/shard_map/ppermute | solution.py:46
  131.0 2.9 %back.2 = (f32[2,128,1536]{2,1,0:T(8,128)S(1)}, bf16[2,128,1536]{2,1,0:T(8,128)(2,1)S(1)}) custom-call(s32[14]{0:T(128)S(1)} %copy-done, bf16[512,256]{1,0:T(8,128)(2,1)S(1)} %get-tuple-element.361.refs_5_.refs_0_, bf16[512,256]{1,0:T(8,128)(2,1)S(1)} %get-tuple-element.379.refs_1_.refs_5_, bf16[512,256]{1,0:T(8,128)(2,1)S(1)} %get-tuple-element.401.refs_2_.refs_5_, ...), custom_call_target="tpu_custom_call" | custom-call | flops 2000000000 | bytes 8000000 | tf_op jit(solution)/shard_map/back/pallas_call | solution.py:100
  144.2 4.0 %collective-permute-done.27 = bf16[128,1536]{1,0:T(8,128)(2,1)S(1)} collective-permute-done((bf16[128,1536]{1,0:T(8,128)(2,1)S(1)}, bf16[128,1536]{1,0:T(8,128)(2,1)S(1)}, u32[]{:S(2)}, u32[]{:S(2)}) %collective-permute-start.27) | collective-permute-done | bytes 393248 | tf_op jit(solution)/shard_map/ppermute | solution.py:46
  153.6 8.8 %collective-permute-done.31 = bf16[1,768,384]{2,1,0:T(8,128)(2,1)S(1)} collective-permute-done((bf16[1,768,384]{2,1,0:T(8,128)(2,1)S(1)}, bf16[1,768,384]{2,1,0:T(8,128)(2,1)S(1)}, u32[]{:S(2)}, u32[]{:S(2)}) %collective-permute-start.31) | collective-permute-done | bytes 589856 | tf_op jit(solution)/shard_map/ppermute | solution.py:46
  167.8 9.8 %collective-permute-done.33.d_far = bf16[128,1536]{1,0:T(8,128)(2,1)S(1)} collective-permute-done((bf16[128,1536]{1,0:T(8,128)(2,1)S(1)}, bf16[128,1536]{1,0:T(8,128)(2,1)S(1)}, u32[]{:S(2)}, u32[]{:S(2)}) %collective-permute-start.33) | collective-permute-done | bytes 393248 | tf_op jit(solution)/shard_map/ppermute | solution.py:46
  177.6 4.4 %attend_back.1 = (bf16[256,192]{1,0:T(8,128)(2,1)S(1)}, f32[2,128,384]{2,1,0:T(8,128)S(1)}, bf16[2,128,384]{2,1,0:T(8,128)(2,1)S(1)}, f32[8,128]{1,0:T(8,128)S(1)}) custom-call(s32[14]{0:T(128)S(1)} %copy-done, bf16[512,576]{1,0:T(8,128)(2,1)S(1)} %get-tuple-element.304.qkv, f32[3,256,512]{2,1,0:T(8,128)S(1)} %get-tuple-element.305.probs_in, ...), custom_call_target="tpu_custom_call" | custom-call | flops 2000000000 | bytes 8000000 | tf_op jit(solution)/shard_map/attend_back/pallas_call | solution.py:100
  185.9 3.3 %collective-permute-done.37 = bf16[1,768,384]{2,1,0:T(8,128)(2,1)S(1)} collective-permute-done((bf16[1,768,384]{2,1,0:T(8,128)(2,1)S(1)}, bf16[1,768,384]{2,1,0:T(8,128)(2,1)S(1)}, u32[]{:S(2)}, u32[]{:S(2)}) %collective-permute-start.37) | collective-permute-done | bytes 589856 | tf_op jit(solution)/shard_map/ppermute | solution.py:46
  198.1 6.2 %collective-permute-done.40.got = bf16[128,1536]{1,0:T(8,128)(2,1)S(1)} collective-permute-done((bf16[128,1536]{1,0:T(8,128)(2,1)S(1)}, bf16[128,1536]{1,0:T(8,128)(2,1)S(1)}, u32[]{:S(2)}, u32[]{:S(2)}) %collective-permute-start.40) | collective-permute-done | bytes 393248 | tf_op jit(solution)/shard_map/ppermute | solution.py:46
  205.8 10.2 %collective-permute-done.39.refs_0_ = bf16[400,768]{1,0:T(8,128)(2,1)S(1)} collective-permute-done((bf16[400,768]{1,0:T(8,128)(2,1)S(1)}, bf16[400,768]{1,0:T(8,128)(2,1)S(1)}, u32[]{:S(2)}, u32[]{:S(2)}) %collective-permute-start.39) | collective-permute-done | bytes 614432 | tf_op jit(solution)/shard_map/ppermute | solution.py:46
  216.7 4.8 %collective-permute-done.42.refs_1_ = bf16[2,2,96,384]{3,2,1,0:T(8,128)(2,1)S(1)} collective-permute-done((bf16[2,2,96,384]{3,2,1,0:T(8,128)(2,1)S(1)}, bf16[2,2,96,384]{3,2,1,0:T(8,128)(2,1)S(1)}, u32[]{:S(2)}, u32[]{:S(2)}) %collective-permute-start.42) | collective-permute-done | bytes 294944 | tf_op jit(solution)/shard_map/ppermute | solution.py:46
  226.6 17.9 %collective-permute-done.43.refs_0_ = bf16[208,768]{1,0:T(8,128)(2,1)S(1)} collective-permute-done((bf16[208,768]{1,0:T(8,128)(2,1)S(1)}, bf16[208,768]{1,0:T(8,128)(2,1)S(1)}, u32[]{:S(2)}, u32[]{:S(2)}) %collective-permute-start.43) | collective-permute-done | bytes 319520 | tf_op jit(solution)/shard_map/ppermute | solution.py:46
  246.6 4.7 %collective-permute-done.45.got = bf16[112,768]{1,0:T(8,128)(2,1)S(1)} collective-permute-done((bf16[112,768]{1,0:T(8,128)(2,1)S(1)}, bf16[112,768]{1,0:T(8,128)(2,1)S(1)}, u32[]{:S(2)}, u32[]{:S(2)}) %collective-permute-start.45) | collective-permute-done | bytes 172064 | tf_op jit(solution)/shard_map/ppermute | solution.py:46
  254.2 6.1 %collective-permute-done.51.refs_5_ = bf16[2,2,96,384]{3,2,1,0:T(8,128)(2,1)S(1)} collective-permute-done((bf16[2,2,96,384]{3,2,1,0:T(8,128)(2,1)S(1)}, bf16[2,2,96,384]{3,2,1,0:T(8,128)(2,1)S(1)}, u32[]{:S(2)}, u32[]{:S(2)}) %collective-permute-start.51) | collective-permute-done | bytes 294944 | tf_op jit(solution)/shard_map/ppermute | solution.py:46
  (158 shorter events, 103.1 us)
Async XLA Ops:
  12.6 18.6 %collective-permute-start.2 = (bf16[2,4,96,384]{3,2,1,0:T(8,128)(2,1)S(1)}, bf16[2,4,96,384]{3,2,1,0:T(8,128)(2,1)S(1)}, u32[]{:S(2)}, u32[]{:S(2)}) collective-permute-start(bf16[2,4,96,384]{3,2,1,0:T(8,128)(2,1)S(1)} %get-tuple-element.282), channel_id=1, source_target_pairs={{2,0},{0,2},{3,1},{1,3},{6,4},{4,6},{7,5},{5,7},{10,8},{8,10},{11,... | collective-permute-start | bytes 1769480 | tf_op jit(solution)/shard_map/ppermute | solution.py:46
  12.7 18.0 %collective-permute-start.1 = (bf16[2,104,768]{2,1,0:T(8,128)(2,1)S(1)}, bf16[2,104,768]{2,1,0:T(8,128)(2,1)S(1)}, u32[]{:S(2)}, u32[]{:S(2)}) collective-permute-start(bf16[2,104,768]{2,1,0:T(8,128)(2,1)S(1)} %place.3.own), channel_id=1, source_target_pairs={{16,0},{0,16},{17,1},{1,17},{18,2},{2,18},{19,3},{3,19},{20,4},{4,... | collective-permute-start | bytes 958472 | tf_op jit(solution)/shard_map/ppermute | solution.py:46
  15.6 16.9 %collective-permute-start.4 = (bf16[128,1536]{1,0:T(8,128)(2,1)S(1)}, bf16[128,1536]{1,0:T(8,128)(2,1)S(1)}, u32[]{:S(2)}, u32[]{:S(2)}) collective-permute-start(bf16[128,1536]{1,0:T(8,128)(2,1)S(1)} %bitcast.95), channel_id=1, source_target_pairs={{8,0},{0,8},{9,1},{1,9},{10,2},{2,10},{11,3},{3,11},{12,4},{4,12},... | collective-permute-start | bytes 1179656 | tf_op jit(solution)/shard_map/ppermute | solution.py:46
  33.9 17.4 %collective-permute-start.5 = (bf16[2,2,104,768]{3,2,1,0:T(8,128)(2,1)S(1)}, bf16[2,2,104,768]{3,2,1,0:T(8,128)(2,1)S(1)}, u32[]{:S(2)}, u32[]{:S(2)}) collective-permute-start(bf16[2,2,104,768]{3,2,1,0:T(8,128)(2,1)S(1)} %place.4.own), channel_id=1, source_target_pairs={{8,0},{0,8},{9,1},{1,9},{10,2},{2,10},{11,3},{3,11},{12,4},{4,12},... | collective-permute-start | bytes 1916936 | tf_op jit(solution)/shard_map/ppermute | solution.py:46
  52.0 18.9 %collective-permute-start.12 = (bf16[3,2,96,384]{3,2,1,0:T(8,128)(2,1)S(1)}, bf16[3,2,96,384]{3,2,1,0:T(8,128)(2,1)S(1)}, u32[]{:S(2)}, u32[]{:S(2)}) collective-permute-start(bf16[3,2,96,384]{3,2,1,0:T(8,128)(2,1)S(1)} %get-tuple-element.311), channel_id=1, source_target_pairs={{8,0},{0,8},{9,1},{1,9},{10,2},{2,10},{11,3},{3,11},{12,4},{4,12},... | collective-permute-start | bytes 1327112 | tf_op jit(solution)/shard_map/ppermute | solution.py:46
  53.8 16.4 %collective-permute-start.13 = (bf16[1,2,2,96,384]{4,3,2,1,0:T(8,128)(2,1)S(1)}, bf16[1,2,2,96,384]{4,3,2,1,0:T(8,128)(2,1)S(1)}, u32[]{:S(2)}, u32[]{:S(2)}) collective-permute-start(bf16[1,2,2,96,384]{4,3,2,1,0:T(8,128)(2,1)S(1)} %bitcast.74), channel_id=1, source_target_pairs={{16,0},{0,16},{17,1},{1,17},{18,2},{2,18},{19,3},{3,19},{20,4},{4,... | collective-permute-start | bytes 884744 | tf_op jit(solution)/shard_map/ppermute | solution.py:46
  75.6 28.8 %collective-permute-start.19 = (bf16[3,384,384]{2,1,0:T(8,128)(2,1)S(1)}, bf16[3,384,384]{2,1,0:T(8,128)(2,1)S(1)}, u32[]{:S(2)}, u32[]{:S(2)}) collective-permute-start(bf16[3,384,384]{2,1,0:T(8,128)(2,1)S(1)} %bitcast.57), channel_id=1, source_target_pairs={{4,0},{0,4},{5,1},{1,5},{6,2},{2,6},{7,3},{3,7},{12,8},{8,12},{13,... | collective-permute-start | bytes 2654216 | tf_op jit(solution)/shard_map/ppermute | solution.py:46
  76.8 27.7 %collective-permute-start.18 = (bf16[2,2,2,96,384]{4,3,2,1,0:T(8,128)(2,1)S(1)}, bf16[2,2,2,96,384]{4,3,2,1,0:T(8,128)(2,1)S(1)}, u32[]{:S(2)}, u32[]{:S(2)}) collective-permute-start(bf16[2,2,2,96,384]{4,3,2,1,0:T(8,128)(2,1)S(1)} %get-tuple-element.332), channel_id=1, source_target_pairs={{16,0},{0,16},{17,1},{1,17},{18,2},{2,18},{19,3},{3,19},{20,4},{4,... | collective-permute-start | bytes 1769480 | tf_op jit(solution)/shard_map/ppermute | solution.py:46
  85.1 19.4 %collective-permute-start.17 = (bf16[128,1536]{1,0:T(8,128)(2,1)S(1)}, bf16[128,1536]{1,0:T(8,128)(2,1)S(1)}, u32[]{:S(2)}, u32[]{:S(2)}) collective-permute-start(bf16[128,1536]{1,0:T(8,128)(2,1)S(1)} %get-tuple-element.364.refs_0_), channel_id=1, source_target_pairs={{2,0},{0,2},{3,1},{1,3},{6,4},{4,6},{7,5},{5,7},{10,8},{8,10},{11,... | collective-permute-start | bytes 1179656 | tf_op jit(solution)/shard_map/ppermute | solution.py:46
  85.2 23.8 %collective-permute-start.21 = (bf16[128,1536]{1,0:T(8,128)(2,1)S(1)}, bf16[128,1536]{1,0:T(8,128)(2,1)S(1)}, u32[]{:S(2)}, u32[]{:S(2)}) collective-permute-start(bf16[128,1536]{1,0:T(8,128)(2,1)S(1)} %get-tuple-element.364.refs_0_), channel_id=1, source_target_pairs={{8,0},{0,8},{9,1},{1,9},{10,2},{2,10},{11,3},{3,11},{12,4},{4,12},... | collective-permute-start | bytes 1179656 | tf_op jit(solution)/shard_map/ppermute | solution.py:46
  86.4 18.5 %collective-permute-start.22 = (bf16[1,384,384]{2,1,0:T(8,128)(2,1)S(1)}, bf16[1,384,384]{2,1,0:T(8,128)(2,1)S(1)}, u32[]{:S(2)}, u32[]{:S(2)}) collective-permute-start(bf16[1,384,384]{2,1,0:T(8,128)(2,1)S(1)} %bitcast.79), channel_id=1, source_target_pairs={{4,0},{0,4},{5,1},{1,5},{6,2},{2,6},{7,3},{3,7},{12,8},{8,12},{13,... | collective-permute-start | bytes 884744 | tf_op jit(solution)/shard_map/ppermute | solution.py:46
  104.5 15.3 %collective-permute-start.20 = (bf16[1,2,2,96,384]{4,3,2,1,0:T(8,128)(2,1)S(1)}, bf16[1,2,2,96,384]{4,3,2,1,0:T(8,128)(2,1)S(1)}, u32[]{:S(2)}, u32[]{:S(2)}) collective-permute-start(bf16[1,2,2,96,384]{4,3,2,1,0:T(8,128)(2,1)S(1)} %get-tuple-element.336), channel_id=1, source_target_pairs={{16,0},{0,16},{17,1},{1,17},{18,2},{2,18},{19,3},{3,19},{20,4},{4,... | collective-permute-start | bytes 884744 | tf_op jit(solution)/shard_map/ppermute | solution.py:46
  104.5 18.8 %collective-permute-start.24 = (bf16[2,384,384]{2,1,0:T(8,128)(2,1)S(1)}, bf16[2,384,384]{2,1,0:T(8,128)(2,1)S(1)}, u32[]{:S(2)}, u32[]{:S(2)}) collective-permute-start(bf16[2,384,384]{2,1,0:T(8,128)(2,1)S(1)} %bitcast.67), channel_id=1, source_target_pairs={{4,0},{0,4},{5,1},{1,5},{6,2},{2,6},{7,3},{3,7},{12,8},{8,12},{13,... | collective-permute-start | bytes 1769480 | tf_op jit(solution)/shard_map/ppermute | solution.py:46
  134.0 16.2 %collective-permute-start.29 = (bf16[1,768,384]{2,1,0:T(8,128)(2,1)S(1)}, bf16[1,768,384]{2,1,0:T(8,128)(2,1)S(1)}, u32[]{:S(2)}, u32[]{:S(2)}) collective-permute-start(bf16[1,768,384]{2,1,0:T(8,128)(2,1)S(1)} %get-tuple-element.415), channel_id=1, source_target_pairs={{4,0},{0,4},{5,1},{1,5},{6,2},{2,6},{7,3},{3,7},{12,8},{8,12},{13,... | collective-permute-start | bytes 1769480 | tf_op jit(solution)/shard_map/ppermute | solution.py:46
  139.7 22.7 %collective-permute-start.31 = (bf16[1,768,384]{2,1,0:T(8,128)(2,1)S(1)}, bf16[1,768,384]{2,1,0:T(8,128)(2,1)S(1)}, u32[]{:S(2)}, u32[]{:S(2)}) collective-permute-start(bf16[1,768,384]{2,1,0:T(8,128)(2,1)S(1)} %get-tuple-element.426), channel_id=1, source_target_pairs={{4,0},{0,4},{5,1},{1,5},{6,2},{2,6},{7,3},{3,7},{12,8},{8,12},{13,... | collective-permute-start | bytes 1769480 | tf_op jit(solution)/shard_map/ppermute | solution.py:46
  151.5 16.4 %collective-permute-start.34 = (bf16[128,1536]{1,0:T(8,128)(2,1)S(1)}, bf16[128,1536]{1,0:T(8,128)(2,1)S(1)}, u32[]{:S(2)}, u32[]{:S(2)}) collective-permute-start(bf16[128,1536]{1,0:T(8,128)(2,1)S(1)} %get-tuple-element.435), channel_id=1, source_target_pairs={{8,0},{0,8},{9,1},{1,9},{10,2},{2,10},{11,3},{3,11},{12,4},{4,12},... | collective-permute-start | bytes 1179656 | tf_op jit(solution)/shard_map/ppermute | solution.py:46
  167.0 22.2 %collective-permute-start.37 = (bf16[1,768,384]{2,1,0:T(8,128)(2,1)S(1)}, bf16[1,768,384]{2,1,0:T(8,128)(2,1)S(1)}, u32[]{:S(2)}, u32[]{:S(2)}) collective-permute-start(bf16[1,768,384]{2,1,0:T(8,128)(2,1)S(1)} %get-tuple-element.454), channel_id=1, source_target_pairs={{4,0},{0,4},{5,1},{1,5},{6,2},{2,6},{7,3},{3,7},{12,8},{8,12},{13,... | collective-permute-start | bytes 1769480 | tf_op jit(solution)/shard_map/ppermute | solution.py:46
  192.9 23.1 %collective-permute-start.39 = (bf16[400,768]{1,0:T(8,128)(2,1)S(1)}, bf16[400,768]{1,0:T(8,128)(2,1)S(1)}, u32[]{:S(2)}, u32[]{:S(2)}) collective-permute-start(bf16[400,768]{1,0:T(8,128)(2,1)S(1)} %bitcast.89), channel_id=1, source_target_pairs={{8,0},{0,8},{9,1},{1,9},{10,2},{2,10},{11,3},{3,11},{12,4},{4,12},... | collective-permute-start | bytes 1843208 | tf_op jit(solution)/shard_map/ppermute | solution.py:46
  194.7 28.6 %collective-permute-start.46 = (bf16[1,768,384]{2,1,0:T(8,128)(2,1)S(1)}, bf16[1,768,384]{2,1,0:T(8,128)(2,1)S(1)}, u32[]{:S(2)}, u32[]{:S(2)}) collective-permute-start(bf16[1,768,384]{2,1,0:T(8,128)(2,1)S(1)} %get-tuple-element.498), channel_id=1, source_target_pairs={{4,0},{0,4},{5,1},{1,5},{6,2},{2,6},{7,3},{3,7},{12,8},{8,12},{13,... | collective-permute-start | bytes 1769480 | tf_op jit(solution)/shard_map/ppermute | solution.py:46
  196.0 20.7 %collective-permute-start.41 = (bf16[384,384]{1,0:T(8,128)(2,1)S(1)}, bf16[384,384]{1,0:T(8,128)(2,1)S(1)}, u32[]{:S(2)}, u32[]{:S(2)}) collective-permute-start(bf16[384,384]{1,0:T(8,128)(2,1)S(1)} %bitcast.108), channel_id=1, source_target_pairs={{16,0},{0,16},{17,1},{1,17},{18,2},{2,18},{19,3},{3,19},{20,4},{4,... | collective-permute-start | bytes 884744 | tf_op jit(solution)/shard_map/ppermute | solution.py:46
  198.1 23.4 %collective-permute-start.42 = (bf16[2,2,96,384]{3,2,1,0:T(8,128)(2,1)S(1)}, bf16[2,2,96,384]{3,2,1,0:T(8,128)(2,1)S(1)}, u32[]{:S(2)}, u32[]{:S(2)}) collective-permute-start(bf16[2,2,96,384]{3,2,1,0:T(8,128)(2,1)S(1)} %get-tuple-element.487), channel_id=1, source_target_pairs={{8,0},{0,8},{9,1},{1,9},{10,2},{2,10},{11,3},{3,11},{12,4},{4,12},... | collective-permute-start | bytes 884744 | tf_op jit(solution)/shard_map/ppermute | solution.py:46
  221.5 23.0 %collective-permute-start.43 = (bf16[208,768]{1,0:T(8,128)(2,1)S(1)}, bf16[208,768]{1,0:T(8,128)(2,1)S(1)}, u32[]{:S(2)}, u32[]{:S(2)}) collective-permute-start(bf16[208,768]{1,0:T(8,128)(2,1)S(1)} %bitcast.104), channel_id=1, source_target_pairs={{16,0},{0,16},{17,1},{1,17},{18,2},{2,18},{19,3},{3,19},{20,4},{4,... | collective-permute-start | bytes 958472 | tf_op jit(solution)/shard_map/ppermute | solution.py:46
  222.6 22.5 %collective-permute-start.44 = (bf16[128,1536]{1,0:T(8,128)(2,1)S(1)}, bf16[128,1536]{1,0:T(8,128)(2,1)S(1)}, u32[]{:S(2)}, u32[]{:S(2)}) collective-permute-start(bf16[128,1536]{1,0:T(8,128)(2,1)S(1)} %get-tuple-element.494), channel_id=1, source_target_pairs={{4,0},{0,4},{5,1},{1,5},{6,2},{2,6},{7,3},{3,7},{12,8},{8,12},{13,... | collective-permute-start | bytes 1179656 | tf_op jit(solution)/shard_map/ppermute | solution.py:46
  223.9 27.4 %collective-permute-start.50 = (bf16[384,384]{1,0:T(8,128)(2,1)S(1)}, bf16[384,384]{1,0:T(8,128)(2,1)S(1)}, u32[]{:S(2)}, u32[]{:S(2)}) collective-permute-start(bf16[384,384]{1,0:T(8,128)(2,1)S(1)} %bitcast.112), channel_id=1, source_target_pairs={{16,0},{0,16},{17,1},{1,17},{18,2},{2,18},{19,3},{3,19},{20,4},{4,... | collective-permute-start | bytes 884744 | tf_op jit(solution)/shard_map/ppermute | solution.py:46
  (44 other events, 344.1 us)

commit v3 on v2

--- a/solution.py
+++ b/solution.py
@@ -402,7 +402,7 @@
         "split",
         here,
         [own, *got],
-        [((size + tail // 2, own.shape[1]), f32), ((count - 1, size + tail, own.shape[1]), bf16)],
+        [((size + tail // 2, own.shape[1]), f32), ((max(count - 1, 1), size + tail, own.shape[1]), bf16)],
         which=which,
         count=count,
         tail=tail // 2,
@@ -426,6 +426,41 @@
         core[j] = total(zl, 1 - k).astype(bf16)
         other[j, 0] = total(1 - zl, 0).astype(bf16)
         other[j, 1] = total(1 - zl, 1).astype(bf16)
+
+
+def last_y_body(here, own, got, keep, send):
+    zl = here[at_zl]
+    for h in range(keep.shape[0]):
+        keep[h] = own[h, zl] + got[h, zl].astype(f32)
+        send[h] = (own[h, 1 - zl] + got[h, 1 - zl].astype(f32)).astype(bf16)
+
+
+def ahead(here, which, count, e):
+    at = here[which] + e
+    return jnp.where(at >= count, at - count, at)
+
+
+def last_z_body(here, own, got, send):
+    count = own.shape[0]
+    for e in range(1, count):
+        at = ahead(here, at_zh, count, e)
+        send[e - 1, 0] = own[at].astype(bf16)
+        send[e - 1, 1] = got[at]
+
+
+def last_body(here, own, got, *refs):
+    *arrived, done, core, other = refs
+    part = done.shape[1]
+    zh, k = here[at_zh], here[at_k]
+    mine, theirs = own[zh], got[zh].astype(f32)
+    for ref in arrived:
+        mine = mine + ref[0].astype(f32)
+        theirs = theirs + ref[1].astype(f32)
+    low, high = mine[:part], mine[part:]
+    done[0] = jnp.where(k == 0, low, high)
+    core[0] = jnp.where(k == 0, high, low).astype(bf16)
+    other[0, 0] = theirs[:part].astype(bf16)
+    other[0, 1] = theirs[part:].astype(bf16)
 
 
 def sum_row(values):
@@ -847,14 +882,26 @@
             outer=outer,
         )
 
+    def sum_yh(keep, got):
+        if outer == 1:
+            return keep, [got]
+        total = keep + got.astype(f32)
+        return total[0], send_sums([total[e].astype(bf16) for e in range(1, outer)], "yh")
+
     def sum_y(keep, got):
-        got = [got]
-        if outer > 1:
-            total = keep + got[0].astype(f32)
-            got = send_sums([total[e].astype(bf16) for e in range(1, outer)], "yh")
-            keep = total[0]
+        keep, got = sum_yh(keep, got)
         flat = [v.reshape(deep * 4 * part, 3 * lane) for v in (keep, *got)]
         return split(here, at_zh, deep, flat[0], flat[1:])
+
+    def sum_y_last(keep, got):
+        keep, got = sum_yh(keep, got)
+        shape = (deep, 2, 2 * part, 3 * lane)
+        return kernel(
+            last_y_body,
+            "last_y",
+            [keep.reshape(shape), sum(g.astype(f32) for g in got).reshape(shape) if outer > 1 else got[0].reshape(shape)],
+            [((deep, *shape[2:]), f32), ((deep, *shape[2:]), bf16)],
+        )
 
     def sum_zh(keep, send):
         got = send_sums([send[e] for e in range(deep - 1)], "zh")
@@ -990,7 +1037,6 @@
     )
     got = [swap(send, "k")]
     grad_got[3] = swap(grads[3][1], "yl")
-    done_a = ffn_split(zh_sums[: chunks // 2])
     keep, grad_keep = tick(keep, grads[2][0])
     if outer > 1:
         keep, send = split(here, at_yh, outer, keep, got, tail)
@@ -998,42 +1044,39 @@
     sums[2] = sum_y(grad_keep, grad_got[2])
     keep, send = split(here, at_zl, 2, keep, got, tail)
 
-    def spread(done):
-        other = swap(done[2], "zl")
-        return [done[0], other, swap(done[1], "k")]
-
-    def over_cores(group):
-        return [*group, swap(group[1], "k")]
-
-    keep, send, g_keep, g_send, residual, *flat = tick(
-        keep, send, g_keep, g_send, residual, *sums[2], *done_a
-    )
-    sums[2], done_a = flat[:2], flat[2:]
+    keep, send, g_keep, g_send, residual, grad_keep, *sums[2] = tick(
+        keep, send, g_keep, g_send, residual, grads[3][0], *sums[2]
+    )
     got = send_sums([send[0]], "zl")
     zh_sums[2] = sum_zh(*sums[2])
-    group_a = spread(done_a)
     g_got = swap(g_send, "yl")
+    last_keep, last_send = sum_y_last(grad_keep, grad_got[3])
+    last_got = swap(last_send, "zl")
+    residual, *zh_sums[2] = tick(residual, *zh_sums[2])
     (mixed,) = kernel(
         mixed_body, "mixed", [mixed_half, mixed_other, residual], [((rows, wide), bf16)], dims=dims
     )
     keep, send = split(here, at_zh, deep, keep, got, tail)
 
-    keep, send, mixed, grad_keep, *flat = tick(
-        keep, send, mixed, grads[3][0], *zh_sums[2], *group_a[:2]
-    )
-    zh_sums[2], group_a[:2] = flat[:deep], flat[deep:]
+    keep, send, mixed, last_keep, *zh_sums[2] = tick(keep, send, mixed, last_keep, *zh_sums[2])
     got = send_sums([send[e] for e in range(deep - 1)], "zh")
-    sums[3] = sum_y(grad_keep, grad_got[3])
-    zh_sums[3] = sum_zh(*sums[3])
+    (last_send,) = kernel(
+        last_z_body,
+        "last_z",
+        [last_keep, last_got],
+        [((max(deep - 1, 1), 2, 2 * part, 3 * lane), bf16)],
+    )
+    last_sums = send_sums([last_send[e] for e in range(deep - 1)], "zh")
+    done = ffn_split(zh_sums[:-1])
+    other = swap(done[2], "zl")
+    group_a = [done[0], other, swap(done[1], "k")]
     keep, send = split(here, at_yl, 2, keep, got, tail)
 
-    keep, send, g_keep, g_got = tick(keep, send, g_keep, g_got)
+    keep, send, g_keep, g_got, last_keep = tick(keep, send, g_keep, g_got, last_keep)
     got = swap(send[0], "yl")
-    got, zh_sums[3][0] = tick(got, zh_sums[3][0])
+    group_a.append(swap(other, "k"))
     g_sum = (g_keep + g_got.astype(f32)).astype(bf16)
     g_other = swap(g_sum, "x")
-    group_a = over_cores(group_a)
-    group_b = over_cores(spread(ffn_split(zh_sums[chunks // 2 :])))
     grad_query, grad_key, grad_value, grad_out, gain_row, grad_table = kernel(
         attn_final_body,
         "attn_final",
@@ -1041,14 +1084,18 @@
         [((part, 2 * inner), f32)] * 4 + [((1, part), f32), ((heads_dev, lane), f32)],
         heads=heads,
     )
-    (input_grad,) = kernel(
-        input_grad_body,
-        "input_grad",
-        [g_sum, g_other, tokens[0], gains, d_residual],
-        [((rows, wide), bf16)],
-        dims=dims,
-    )
-    gain_row, input_grad = tick(gain_row, input_grad)
+    gain_row, last_keep = tick(gain_row, last_keep)
+    done = kernel(
+        last_body,
+        "last",
+        [last_keep, last_got, *last_sums],
+        [
+            ((1, part, 3 * lane), f32),
+            ((1, part, 3 * lane), bf16),
+            ((1, 2, part, 3 * lane), bf16),
+        ],
+    )
+    group_b = [done[0], done[2], swap(done[1], "k"), swap(done[2], "k")]
     grad_gate, grad_up, grad_down, grad_gains = kernel(
         ffn_final_body,
         "ffn_final",
@@ -1057,7 +1104,16 @@
         [pltpu.VMEM((3, part, 4 * chunks * lane), f32)],
         groups=2,
     )
-    grad_gains = grad_gains + swap(grad_gains, "x")
+    grad_gains, d_residual = tick(grad_gains, d_residual)
+    gains_got = swap(grad_gains, "x")
+    (input_grad,) = kernel(
+        input_grad_body,
+        "input_grad",
+        [g_sum, g_other, tokens[0], gains, d_residual],
+        [((rows, wide), bf16)],
+        dims=dims,
+    )
+    grad_gains = grad_gains + gains_got
     return (
         mixed[None],
         input_grad[None],

time: 271 us -> 254 us (0.937)
  waiting for transfers between devices: 163 us -> 145 us
    ppermute x55, waiting for transfers between devices: 163 us -> 145 us  [fetch(): lax.ppermute(value, axis, [((i + step) % size, i) for i in range(size)])]
    pallas_call x39 -> x40, Pallas kernels: 58.3 us -> 58.9 us  [call(): pl.pallas_call(functools.partial(body, **static), out_shape=tuple((jax.Sh...]
  transfers between devices with their start and end apart: 55 -> 55, of which waited for: 33 -> 34; matrix products, arithmetic and copies ran while one was open for 0% -> 0% of each run, Pallas kernels for 17% -> 20%
where the time goes in v3:
time: 254 us
  waiting for transfers between devices  145 us (57%)
  Pallas kernels  58.9 us (23%)
  starting transfers between devices  46.5 us (18%)
    ppermute x55, waiting for transfers between devices, fetch(): lax.ppermute(value, axis, [((i + step) % size, i) for i in range(size)])  145 us
    pallas_call x40, Pallas kernels, call(): pl.pallas_call(functools.partial(body, **static), out_shape=tuple((jax.Sh...  58.9 us
    ppermute x55, starting transfers between devices, fetch(): lax.ppermute(value, axis, [((i + step) % size, i) for i in range(size)])  46.5 us
  transfers between devices with their start and end apart: 55, of which 34 were waited for; matrix products, arithmetic and copies ran while one was open for 0% of the time, Pallas kernels for 20%

profile of v3, /device:TPU:0, one launch (start us, length us, event | category | flops | bytes accessed | tf_op | source)
XLA Modules:
  0.0 254.3 jit_solution(5325978555960412575)
XLA Ops:
  4.7 3.0 %collective-permute-start = (bf16[104,768]{1,0:T(8,128)(2,1)}, bf16[104,768]{1,0:T(8,128)(2,1)S(1)}, u32[]{:S(2)}, u32[]{:S(2)}) collective-permute-start(bf16[104,768]{1,0:T(8,128)(2,1)} %get-tuple-element.274), channel_id=1, source_target_pairs={{4,0},{0,4},{5,1},{1,5},{6,2},{2,6},{7,3},{3,7},{12,8},{8,12},{13,... | collective-permute-start | bytes 479240 | tf_op jit(solution)/shard_map/ppermute | solution.py:46
  8.7 3.3 %collective-permute-done.got = bf16[104,768]{1,0:T(8,128)(2,1)S(1)} collective-permute-done((bf16[104,768]{1,0:T(8,128)(2,1)}, bf16[104,768]{1,0:T(8,128)(2,1)S(1)}, u32[]{:S(2)}, u32[]{:S(2)}) %collective-permute-start) | collective-permute-done | bytes 159776 | tf_op jit(solution)/shard_map/ppermute | solution.py:46
  12.7 2.9 %collective-permute-start.1 = (bf16[2,104,768]{2,1,0:T(8,128)(2,1)S(1)}, bf16[2,104,768]{2,1,0:T(8,128)(2,1)S(1)}, u32[]{:S(2)}, u32[]{:S(2)}) collective-permute-start(bf16[2,104,768]{2,1,0:T(8,128)(2,1)S(1)} %place.3.own), channel_id=1, source_target_pairs={{16,0},{0,16},{17,1},{1,17},{18,2},{2,18},{19,3},{3,19},{20,4},{4,... | collective-permute-start | bytes 958472 | tf_op jit(solution)/shard_map/ppermute | solution.py:46
  18.7 12.0 %collective-permute-done.1.got = bf16[2,104,768]{2,1,0:T(8,128)(2,1)S(1)} collective-permute-done((bf16[2,104,768]{2,1,0:T(8,128)(2,1)S(1)}, bf16[2,104,768]{2,1,0:T(8,128)(2,1)S(1)}, u32[]{:S(2)}, u32[]{:S(2)}) %collective-permute-start.1) | collective-permute-done | bytes 319520 | tf_op jit(solution)/shard_map/ppermute | solution.py:46
  35.0 4.2 %collective-permute-done.6.got = bf16[1,2,96,384]{3,2,1,0:T(8,128)(2,1)S(1)} collective-permute-done((bf16[1,2,96,384]{3,2,1,0:T(8,128)(2,1)S(1)}, bf16[1,2,96,384]{3,2,1,0:T(8,128)(2,1)S(1)}, u32[]{:S(2)}, u32[]{:S(2)}) %collective-permute-start.6) | collective-permute-done | bytes 147488 | tf_op jit(solution)/shard_map/ppermute | solution.py:46
  43.5 7.8 %collective-permute-done.5.got = bf16[2,2,104,768]{3,2,1,0:T(8,128)(2,1)S(1)} collective-permute-done((bf16[2,2,104,768]{3,2,1,0:T(8,128)(2,1)S(1)}, bf16[2,2,104,768]{3,2,1,0:T(8,128)(2,1)S(1)}, u32[]{:S(2)}, u32[]{:S(2)}) %collective-permute-start.5) | collective-permute-done | bytes 639008 | tf_op jit(solution)/shard_map/ppermute | solution.py:46
  57.9 5.4 %attend.1 = (bf16[512,576]{1,0:T(8,128)(2,1)S(1)}, f32[3,256,512]{2,1,0:T(8,128)S(1)}, bf16[256,192]{1,0:T(8,128)(2,1)S(1)}, f32[128,1536]{1,0:T(8,128)S(1)}, bf...) custom-call(s32[14]{0:T(128)S(1)} %copy-done, ...), custom_call_target="tpu_custom_call" | custom-call | flops 2000000000 | bytes 8000000 | tf_op jit(solution)/shard_map/attend/pallas_call | solution.py:100
  63.8 6.4 %collective-permute-done.13 = bf16[1,2,2,96,384]{4,3,2,1,0:T(8,128)(2,1)S(1)} collective-permute-done((bf16[1,2,2,96,384]{4,3,2,1,0:T(8,128)(2,1)S(1)}, bf16[1,2,2,96,384]{4,3,2,1,0:T(8,128)(2,1)S(1)}, u32[]{:S(2)}, u32[]{:S(2)}) %collective-permute-start.13) | collective-permute-done | bytes 294944 | tf_op jit(solution)/shard_map/ppermute | solution.py:46
  77.5 6.4 %collective-permute-done.16.got = bf16[128,1536]{1,0:T(8,128)(2,1)S(1)} collective-permute-done((bf16[128,1536]{1,0:T(8,128)(2,1)S(1)}, bf16[128,1536]{1,0:T(8,128)(2,1)S(1)}, u32[]{:S(2)}, u32[]{:S(2)}) %collective-permute-start.16) | collective-permute-done | bytes 393248 | tf_op jit(solution)/shard_map/ppermute | solution.py:46
  87.9 16.6 %collective-permute-done.18 = bf16[2,2,2,96,384]{4,3,2,1,0:T(8,128)(2,1)S(1)} collective-permute-done((bf16[2,2,2,96,384]{4,3,2,1,0:T(8,128)(2,1)S(1)}, bf16[2,2,2,96,384]{4,3,2,1,0:T(8,128)(2,1)S(1)}, u32[]{:S(2)}, u32[]{:S(2)}) %collective-permute-start.18) | collective-permute-done | bytes 589856 | tf_op jit(solution)/shard_map/ppermute | solution.py:46
  104.8 4.2 %collective-permute-done.21.refs_2_ = bf16[128,1536]{1,0:T(8,128)(2,1)S(1)} collective-permute-done((bf16[128,1536]{1,0:T(8,128)(2,1)S(1)}, bf16[128,1536]{1,0:T(8,128)(2,1)S(1)}, u32[]{:S(2)}, u32[]{:S(2)}) %collective-permute-start.21) | collective-permute-done | bytes 393248 | tf_op jit(solution)/shard_map/ppermute | solution.py:46
  109.0 10.8 %collective-permute-done.20 = bf16[1,2,2,96,384]{4,3,2,1,0:T(8,128)(2,1)S(1)} collective-permute-done((bf16[1,2,2,96,384]{4,3,2,1,0:T(8,128)(2,1)S(1)}, bf16[1,2,2,96,384]{4,3,2,1,0:T(8,128)(2,1)S(1)}, u32[]{:S(2)}, u32[]{:S(2)}) %collective-permute-start.20) | collective-permute-done | bytes 294944 | tf_op jit(solution)/shard_map/ppermute | solution.py:46
  131.0 2.9 %back.2 = (f32[2,128,1536]{2,1,0:T(8,128)S(1)}, bf16[2,128,1536]{2,1,0:T(8,128)(2,1)S(1)}) custom-call(s32[14]{0:T(128)S(1)} %copy-done, bf16[512,256]{1,0:T(8,128)(2,1)S(1)} %get-tuple-element.362.refs_5_.refs_0_, bf16[512,256]{1,0:T(8,128)(2,1)S(1)} %get-tuple-element.381.refs_1_.refs_5_, bf16[512,256]{1,0:T(8,128)(2,1)S(1)} %get-tuple-element.403.refs_2_.refs_5_, ...), custom_call_target="tpu_custom_call" | custom-call | flops 2000000000 | bytes 8000000 | tf_op jit(solution)/shard_map/back/pallas_call | solution.py:100
  144.2 4.0 %collective-permute-done.27 = bf16[128,1536]{1,0:T(8,128)(2,1)S(1)} collective-permute-done((bf16[128,1536]{1,0:T(8,128)(2,1)S(1)}, bf16[128,1536]{1,0:T(8,128)(2,1)S(1)}, u32[]{:S(2)}, u32[]{:S(2)}) %collective-permute-start.27) | collective-permute-done | bytes 393248 | tf_op jit(solution)/shard_map/ppermute | solution.py:46
  153.6 8.8 %collective-permute-done.31 = bf16[1,768,384]{2,1,0:T(8,128)(2,1)S(1)} collective-permute-done((bf16[1,768,384]{2,1,0:T(8,128)(2,1)S(1)}, bf16[1,768,384]{2,1,0:T(8,128)(2,1)S(1)}, u32[]{:S(2)}, u32[]{:S(2)}) %collective-permute-start.31) | collective-permute-done | bytes 589856 | tf_op jit(solution)/shard_map/ppermute | solution.py:46
  167.8 9.8 %collective-permute-done.33.d_far = bf16[128,1536]{1,0:T(8,128)(2,1)S(1)} collective-permute-done((bf16[128,1536]{1,0:T(8,128)(2,1)S(1)}, bf16[128,1536]{1,0:T(8,128)(2,1)S(1)}, u32[]{:S(2)}, u32[]{:S(2)}) %collective-permute-start.33) | collective-permute-done | bytes 393248 | tf_op jit(solution)/shard_map/ppermute | solution.py:46
  177.6 4.4 %attend_back.1 = (bf16[256,192]{1,0:T(8,128)(2,1)S(1)}, f32[2,128,384]{2,1,0:T(8,128)S(1)}, bf16[2,128,384]{2,1,0:T(8,128)(2,1)S(1)}, f32[8,128]{1,0:T(8,128)S(1)}) custom-call(s32[14]{0:T(128)S(1)} %copy-done, bf16[512,576]{1,0:T(8,128)(2,1)S(1)} %get-tuple-element.305.qkv, f32[3,256,512]{2,1,0:T(8,128)S(1)} %get-tuple-element.306.probs_in, ...), custom_call_target="tpu_custom_call" | custom-call | flops 2000000000 | bytes 8000000 | tf_op jit(solution)/shard_map/attend_back/pallas_call | solution.py:100
  185.9 3.3 %collective-permute-done.37 = bf16[1,768,384]{2,1,0:T(8,128)(2,1)S(1)} collective-permute-done((bf16[1,768,384]{2,1,0:T(8,128)(2,1)S(1)}, bf16[1,768,384]{2,1,0:T(8,128)(2,1)S(1)}, u32[]{:S(2)}, u32[]{:S(2)}) %collective-permute-start.37) | collective-permute-done | bytes 589856 | tf_op jit(solution)/shard_map/ppermute | solution.py:46
  194.7 2.8 %collective-permute-start.41 = (bf16[384,384]{1,0:T(8,128)(2,1)S(1)}, bf16[384,384]{1,0:T(8,128)(2,1)S(1)}, u32[]{:S(2)}, u32[]{:S(2)}) collective-permute-start(bf16[384,384]{1,0:T(8,128)(2,1)S(1)} %bitcast.107), channel_id=1, source_target_pairs={{16,0},{0,16},{17,1},{1,17},{18,2},{2,18},{19,3},{3,19},{20,4},{4,... | collective-permute-start | bytes 884744 | tf_op jit(solution)/shard_map/ppermute | solution.py:46
  198.1 7.2 %collective-permute-done.42 = bf16[1,768,384]{2,1,0:T(8,128)(2,1)S(1)} collective-permute-done((bf16[1,768,384]{2,1,0:T(8,128)(2,1)S(1)}, bf16[1,768,384]{2,1,0:T(8,128)(2,1)S(1)}, u32[]{:S(2)}, u32[]{:S(2)}) %collective-permute-start.42) | collective-permute-done | bytes 589856 | tf_op jit(solution)/shard_map/ppermute | solution.py:46
  206.1 7.4 %collective-permute-done.41 = bf16[384,384]{1,0:T(8,128)(2,1)S(1)} collective-permute-done((bf16[384,384]{1,0:T(8,128)(2,1)S(1)}, bf16[384,384]{1,0:T(8,128)(2,1)S(1)}, u32[]{:S(2)}, u32[]{:S(2)}) %collective-permute-start.41) | collective-permute-done | bytes 294944 | tf_op jit(solution)/shard_map/ppermute | solution.py:46
  220.4 4.9 %collective-permute-done.50.got = bf16[2,192,384]{2,1,0:T(8,128)(2,1)S(1)} collective-permute-done((bf16[2,192,384]{2,1,0:T(8,128)(2,1)S(1)}, bf16[2,192,384]{2,1,0:T(8,128)(2,1)S(1)}, u32[]{:S(2)}, u32[]{:S(2)}) %collective-permute-start.50) | collective-permute-done | bytes 294944 | tf_op jit(solution)/shard_map/ppermute | solution.py:46
  225.9 9.2 %collective-permute-done.43.refs_0_ = bf16[208,768]{1,0:T(8,128)(2,1)S(1)} collective-permute-done((bf16[208,768]{1,0:T(8,128)(2,1)S(1)}, bf16[208,768]{1,0:T(8,128)(2,1)S(1)}, u32[]{:S(2)}, u32[]{:S(2)}) %collective-permute-start.43) | collective-permute-done | bytes 319520 | tf_op jit(solution)/shard_map/ppermute | solution.py:46
  238.7 4.7 %collective-permute-done.46.refs_1_ = bf16[3,2,96,384]{3,2,1,0:T(8,128)(2,1)S(1)} collective-permute-done((bf16[3,2,96,384]{3,2,1,0:T(8,128)(2,1)S(1)}, bf16[3,2,96,384]{3,2,1,0:T(8,128)(2,1)S(1)}, u32[]{:S(2)}, u32[]{:S(2)}) %collective-permute-start.46) | collective-permute-done | bytes 442400 | tf_op jit(solution)/shard_map/ppermute | solution.py:46
  (159 shorter events, 100.0 us)
Async XLA Ops:
  12.6 18.6 %collective-permute-start.2 = (bf16[2,4,96,384]{3,2,1,0:T(8,128)(2,1)S(1)}, bf16[2,4,96,384]{3,2,1,0:T(8,128)(2,1)S(1)}, u32[]{:S(2)}, u32[]{:S(2)}) collective-permute-start(bf16[2,4,96,384]{3,2,1,0:T(8,128)(2,1)S(1)} %get-tuple-element.283), channel_id=1, source_target_pairs={{2,0},{0,2},{3,1},{1,3},{6,4},{4,6},{7,5},{5,7},{10,8},{8,10},{11,... | collective-permute-start | bytes 1769480 | tf_op jit(solution)/shard_map/ppermute | solution.py:46
  12.7 18.0 %collective-permute-start.1 = (bf16[2,104,768]{2,1,0:T(8,128)(2,1)S(1)}, bf16[2,104,768]{2,1,0:T(8,128)(2,1)S(1)}, u32[]{:S(2)}, u32[]{:S(2)}) collective-permute-start(bf16[2,104,768]{2,1,0:T(8,128)(2,1)S(1)} %place.3.own), channel_id=1, source_target_pairs={{16,0},{0,16},{17,1},{1,17},{18,2},{2,18},{19,3},{3,19},{20,4},{4,... | collective-permute-start | bytes 958472 | tf_op jit(solution)/shard_map/ppermute | solution.py:46
  15.6 16.9 %collective-permute-start.4 = (bf16[128,1536]{1,0:T(8,128)(2,1)S(1)}, bf16[128,1536]{1,0:T(8,128)(2,1)S(1)}, u32[]{:S(2)}, u32[]{:S(2)}) collective-permute-start(bf16[128,1536]{1,0:T(8,128)(2,1)S(1)} %bitcast.93), channel_id=1, source_target_pairs={{8,0},{0,8},{9,1},{1,9},{10,2},{2,10},{11,3},{3,11},{12,4},{4,12},... | collective-permute-start | bytes 1179656 | tf_op jit(solution)/shard_map/ppermute | solution.py:46
  33.9 17.4 %collective-permute-start.5 = (bf16[2,2,104,768]{3,2,1,0:T(8,128)(2,1)S(1)}, bf16[2,2,104,768]{3,2,1,0:T(8,128)(2,1)S(1)}, u32[]{:S(2)}, u32[]{:S(2)}) collective-permute-start(bf16[2,2,104,768]{3,2,1,0:T(8,128)(2,1)S(1)} %place.4.own), channel_id=1, source_target_pairs={{8,0},{0,8},{9,1},{1,9},{10,2},{2,10},{11,3},{3,11},{12,4},{4,12},... | collective-permute-start | bytes 1916936 | tf_op jit(solution)/shard_map/ppermute | solution.py:46
  52.0 18.9 %collective-permute-start.12 = (bf16[3,2,96,384]{3,2,1,0:T(8,128)(2,1)S(1)}, bf16[3,2,96,384]{3,2,1,0:T(8,128)(2,1)S(1)}, u32[]{:S(2)}, u32[]{:S(2)}) collective-permute-start(bf16[3,2,96,384]{3,2,1,0:T(8,128)(2,1)S(1)} %get-tuple-element.312), channel_id=1, source_target_pairs={{8,0},{0,8},{9,1},{1,9},{10,2},{2,10},{11,3},{3,11},{12,4},{4,12},... | collective-permute-start | bytes 1327112 | tf_op jit(solution)/shard_map/ppermute | solution.py:46
  53.8 16.4 %collective-permute-start.13 = (bf16[1,2,2,96,384]{4,3,2,1,0:T(8,128)(2,1)S(1)}, bf16[1,2,2,96,384]{4,3,2,1,0:T(8,128)(2,1)S(1)}, u32[]{:S(2)}, u32[]{:S(2)}) collective-permute-start(bf16[1,2,2,96,384]{4,3,2,1,0:T(8,128)(2,1)S(1)} %bitcast.72), channel_id=1, source_target_pairs={{16,0},{0,16},{17,1},{1,17},{18,2},{2,18},{19,3},{3,19},{20,4},{4,... | collective-permute-start | bytes 884744 | tf_op jit(solution)/shard_map/ppermute | solution.py:46
  75.6 28.8 %collective-permute-start.19 = (bf16[3,384,384]{2,1,0:T(8,128)(2,1)S(1)}, bf16[3,384,384]{2,1,0:T(8,128)(2,1)S(1)}, u32[]{:S(2)}, u32[]{:S(2)}) collective-permute-start(bf16[3,384,384]{2,1,0:T(8,128)(2,1)S(1)} %bitcast.55), channel_id=1, source_target_pairs={{4,0},{0,4},{5,1},{1,5},{6,2},{2,6},{7,3},{3,7},{12,8},{8,12},{13,... | collective-permute-start | bytes 2654216 | tf_op jit(solution)/shard_map/ppermute | solution.py:46
  76.8 27.7 %collective-permute-start.18 = (bf16[2,2,2,96,384]{4,3,2,1,0:T(8,128)(2,1)S(1)}, bf16[2,2,2,96,384]{4,3,2,1,0:T(8,128)(2,1)S(1)}, u32[]{:S(2)}, u32[]{:S(2)}) collective-permute-start(bf16[2,2,2,96,384]{4,3,2,1,0:T(8,128)(2,1)S(1)} %get-tuple-element.333), channel_id=1, source_target_pairs={{16,0},{0,16},{17,1},{1,17},{18,2},{2,18},{19,3},{3,19},{20,4},{4,... | collective-permute-start | bytes 1769480 | tf_op jit(solution)/shard_map/ppermute | solution.py:46
  85.1 19.4 %collective-permute-start.17 = (bf16[128,1536]{1,0:T(8,128)(2,1)S(1)}, bf16[128,1536]{1,0:T(8,128)(2,1)S(1)}, u32[]{:S(2)}, u32[]{:S(2)}) collective-permute-start(bf16[128,1536]{1,0:T(8,128)(2,1)S(1)} %get-tuple-element.365.refs_0_), channel_id=1, source_target_pairs={{2,0},{0,2},{3,1},{1,3},{6,4},{4,6},{7,5},{5,7},{10,8},{8,10},{11,... | collective-permute-start | bytes 1179656 | tf_op jit(solution)/shard_map/ppermute | solution.py:46
  85.2 23.8 %collective-permute-start.21 = (bf16[128,1536]{1,0:T(8,128)(2,1)S(1)}, bf16[128,1536]{1,0:T(8,128)(2,1)S(1)}, u32[]{:S(2)}, u32[]{:S(2)}) collective-permute-start(bf16[128,1536]{1,0:T(8,128)(2,1)S(1)} %get-tuple-element.365.refs_0_), channel_id=1, source_target_pairs={{8,0},{0,8},{9,1},{1,9},{10,2},{2,10},{11,3},{3,11},{12,4},{4,12},... | collective-permute-start | bytes 1179656 | tf_op jit(solution)/shard_map/ppermute | solution.py:46
  86.4 18.5 %collective-permute-start.22 = (bf16[1,384,384]{2,1,0:T(8,128)(2,1)S(1)}, bf16[1,384,384]{2,1,0:T(8,128)(2,1)S(1)}, u32[]{:S(2)}, u32[]{:S(2)}) collective-permute-start(bf16[1,384,384]{2,1,0:T(8,128)(2,1)S(1)} %bitcast.77), channel_id=1, source_target_pairs={{4,0},{0,4},{5,1},{1,5},{6,2},{2,6},{7,3},{3,7},{12,8},{8,12},{13,... | collective-permute-start | bytes 884744 | tf_op jit(solution)/shard_map/ppermute | solution.py:46
  104.5 18.8 %collective-permute-start.24 = (bf16[2,384,384]{2,1,0:T(8,128)(2,1)S(1)}, bf16[2,384,384]{2,1,0:T(8,128)(2,1)S(1)}, u32[]{:S(2)}, u32[]{:S(2)}) collective-permute-start(bf16[2,384,384]{2,1,0:T(8,128)(2,1)S(1)} %bitcast.65), channel_id=1, source_target_pairs={{4,0},{0,4},{5,1},{1,5},{6,2},{2,6},{7,3},{3,7},{12,8},{8,12},{13,... | collective-permute-start | bytes 1769480 | tf_op jit(solution)/shard_map/ppermute | solution.py:46
  139.7 22.7 %collective-permute-start.31 = (bf16[1,768,384]{2,1,0:T(8,128)(2,1)S(1)}, bf16[1,768,384]{2,1,0:T(8,128)(2,1)S(1)}, u32[]{:S(2)}, u32[]{:S(2)}) collective-permute-start(bf16[1,768,384]{2,1,0:T(8,128)(2,1)S(1)} %get-tuple-element.428), channel_id=1, source_target_pairs={{4,0},{0,4},{5,1},{1,5},{6,2},{2,6},{7,3},{3,7},{12,8},{8,12},{13,... | collective-permute-start | bytes 1769480 | tf_op jit(solution)/shard_map/ppermute | solution.py:46
  151.5 16.3 %collective-permute-start.34 = (bf16[128,1536]{1,0:T(8,128)(2,1)S(1)}, bf16[128,1536]{1,0:T(8,128)(2,1)S(1)}, u32[]{:S(2)}, u32[]{:S(2)}) collective-permute-start(bf16[128,1536]{1,0:T(8,128)(2,1)S(1)} %get-tuple-element.437), channel_id=1, source_target_pairs={{8,0},{0,8},{9,1},{1,9},{10,2},{2,10},{11,3},{3,11},{12,4},{4,12},... | collective-permute-start | bytes 1179656 | tf_op jit(solution)/shard_map/ppermute | solution.py:46
  167.0 22.2 %collective-permute-start.37 = (bf16[1,768,384]{2,1,0:T(8,128)(2,1)S(1)}, bf16[1,768,384]{2,1,0:T(8,128)(2,1)S(1)}, u32[]{:S(2)}, u32[]{:S(2)}) collective-permute-start(bf16[1,768,384]{2,1,0:T(8,128)(2,1)S(1)} %get-tuple-element.456), channel_id=1, source_target_pairs={{4,0},{0,4},{5,1},{1,5},{6,2},{2,6},{7,3},{3,7},{12,8},{8,12},{13,... | collective-permute-start | bytes 1769480 | tf_op jit(solution)/shard_map/ppermute | solution.py:46
  192.9 23.1 %collective-permute-start.39 = (bf16[400,768]{1,0:T(8,128)(2,1)S(1)}, bf16[400,768]{1,0:T(8,128)(2,1)S(1)}, u32[]{:S(2)}, u32[]{:S(2)}) collective-permute-start(bf16[400,768]{1,0:T(8,128)(2,1)S(1)} %bitcast.87), channel_id=1, source_target_pairs={{8,0},{0,8},{9,1},{1,9},{10,2},{2,10},{11,3},{3,11},{12,4},{4,12},... | collective-permute-start | bytes 1843208 | tf_op jit(solution)/shard_map/ppermute | solution.py:46
  193.1 20.4 %collective-permute-start.40 = (bf16[128,1536]{1,0:T(8,128)(2,1)S(1)}, bf16[128,1536]{1,0:T(8,128)(2,1)S(1)}, u32[]{:S(2)}, u32[]{:S(2)}) collective-permute-start(bf16[128,1536]{1,0:T(8,128)(2,1)S(1)} %add_convert_fusion.1.own), channel_id=1, source_target_pairs={{1,0},{0,1},{3,2},{2,3},{5,4},{4,5},{7,6},{6,7},{9,8},{8,9},{11,10... | collective-permute-start | bytes 1179656 | tf_op jit(solution)/shard_map/ppermute | solution.py:46
  194.7 18.8 %collective-permute-start.41 = (bf16[384,384]{1,0:T(8,128)(2,1)S(1)}, bf16[384,384]{1,0:T(8,128)(2,1)S(1)}, u32[]{:S(2)}, u32[]{:S(2)}) collective-permute-start(bf16[384,384]{1,0:T(8,128)(2,1)S(1)} %bitcast.107), channel_id=1, source_target_pairs={{16,0},{0,16},{17,1},{1,17},{18,2},{2,18},{19,3},{3,19},{20,4},{4,... | collective-permute-start | bytes 884744 | tf_op jit(solution)/shard_map/ppermute | solution.py:46
  197.4 38.4 %collective-permute-start.44 = (bf16[128,1536]{1,0:T(8,128)(2,1)S(1)}, bf16[128,1536]{1,0:T(8,128)(2,1)S(1)}, u32[]{:S(2)}, u32[]{:S(2)}) collective-permute-start(bf16[128,1536]{1,0:T(8,128)(2,1)S(1)} %get-tuple-element.493), channel_id=1, source_target_pairs={{4,0},{0,4},{5,1},{1,5},{6,2},{2,6},{7,3},{3,7},{12,8},{8,12},{13,... | collective-permute-start | bytes 1179656 | tf_op jit(solution)/shard_map/ppermute | solution.py:46
  206.0 19.2 %collective-permute-start.50 = (bf16[2,192,384]{2,1,0:T(8,128)(2,1)S(1)}, bf16[2,192,384]{2,1,0:T(8,128)(2,1)S(1)}, u32[]{:S(2)}, u32[]{:S(2)}) collective-permute-start(bf16[2,192,384]{2,1,0:T(8,128)(2,1)S(1)} %get-tuple-element.511), channel_id=1, source_target_pairs={{8,0},{0,8},{9,1},{1,9},{10,2},{2,10},{11,3},{3,11},{12,4},{4,12},... | collective-permute-start | bytes 884744 | tf_op jit(solution)/shard_map/ppermute | solution.py:46
  216.7 18.4 %collective-permute-start.43 = (bf16[208,768]{1,0:T(8,128)(2,1)S(1)}, bf16[208,768]{1,0:T(8,128)(2,1)S(1)}, u32[]{:S(2)}, u32[]{:S(2)}) collective-permute-start(bf16[208,768]{1,0:T(8,128)(2,1)S(1)} %bitcast.102), channel_id=1, source_target_pairs={{16,0},{0,16},{17,1},{1,17},{18,2},{2,18},{19,3},{3,19},{20,4},{4,... | collective-permute-start | bytes 958472 | tf_op jit(solution)/shard_map/ppermute | solution.py:46
  219.9 23.5 %collective-permute-start.46 = (bf16[3,2,96,384]{3,2,1,0:T(8,128)(2,1)S(1)}, bf16[3,2,96,384]{3,2,1,0:T(8,128)(2,1)S(1)}, u32[]{:S(2)}, u32[]{:S(2)}) collective-permute-start(bf16[3,2,96,384]{3,2,1,0:T(8,128)(2,1)S(1)} %get-tuple-element.504), channel_id=1, source_target_pairs={{8,0},{0,8},{9,1},{1,9},{10,2},{2,10},{11,3},{3,11},{12,4},{4,12},... | collective-permute-start | bytes 1327112 | tf_op jit(solution)/shard_map/ppermute | solution.py:46
  220.3 26.4 %collective-permute-start.47 = (bf16[3,96,384]{2,1,0:T(8,128)(2,1)S(1)}, bf16[3,96,384]{2,1,0:T(8,128)(2,1)S(1)}, u32[]{:S(2)}, u32[]{:S(2)}) collective-permute-start(bf16[3,96,384]{2,1,0:T(8,128)(2,1)S(1)} %get-tuple-element.505), channel_id=1, source_target_pairs={{2,0},{0,2},{3,1},{1,3},{6,4},{4,6},{7,5},{5,7},{10,8},{8,10},{11,... | collective-permute-start | bytes 663560 | tf_op jit(solution)/shard_map/ppermute | solution.py:46
  225.8 19.8 %collective-permute-start.51 = (bf16[2,192,384]{2,1,0:T(8,128)(2,1)S(1)}, bf16[2,192,384]{2,1,0:T(8,128)(2,1)S(1)}, u32[]{:S(2)}, u32[]{:S(2)}) collective-permute-start(bf16[2,192,384]{2,1,0:T(8,128)(2,1)S(1)} %bitcast.106), channel_id=1, source_target_pairs={{16,0},{0,16},{17,1},{1,17},{18,2},{2,18},{19,3},{3,19},{20,4},{4,... | collective-permute-start | bytes 884744 | tf_op jit(solution)/shard_map/ppermute | solution.py:46
  (44 other events, 346.7 us)

commit v4 on v3

--- a/solution.py
+++ b/solution.py
@@ -68,6 +68,9 @@
         return values
 
 
+costs = {"attn_final": 200, "last_z": 40, "place": 200}
+
+
 def runs_of(dims, order, inverse):
     index = np.arange(int(np.prod(dims))).reshape(dims).transpose(order).reshape(-1)
     if inverse:
@@ -93,6 +96,7 @@
 
 
 def call(body, name, here, arrays, outs, scratch=(), raw=0, **static):
+    cost = costs.get(name, 100)
     space = pl.BlockSpec(memory_space=pltpu.VMEM)
     spaces = [pl.BlockSpec(memory_space=pltpu.HBM)] * raw + [space] * (len(arrays) - raw)
     need = sum(int(np.prod(s.shape)) * jnp.dtype(s.dtype).itemsize for s in scratch[: len(scratch) - bool(raw)])
@@ -104,7 +108,9 @@
         out_specs=tuple(space for _ in outs),
         scratch_shapes=scratch,
         compiler_params=pltpu.CompilerParams(vmem_limit_bytes=(56 << 20) if raw else need),
-        cost_estimate=pl.CostEstimate(flops=2_000_000_000, bytes_accessed=8_000_000, transcendentals=0),
+        cost_estimate=pl.CostEstimate(
+            flops=20_000_000 * cost, bytes_accessed=80_000 * cost, transcendentals=0
+        ),
         name=name,
     )(here, *arrays)
 

time: 254 us -> 254 us (level)
  no operation moved by 1% of the time
where the time goes in v4:
time: 254 us; the launch traced here: 253 us
  waiting for transfers between devices  145 us (57%)
  Pallas kernels  58.9 us (23%)
  starting transfers between devices  45.6 us (18%)
    ppermute x55, waiting for transfers between devices, fetch(): lax.ppermute(value, axis, [((i + step) % size, i) for i in range(size)])  145 us
    pallas_call x40, Pallas kernels, call(): pl.pallas_call(functools.partial(body, **static), out_shape=tuple((jax.Sh...  58.9 us
    ppermute x55, starting transfers between devices, fetch(): lax.ppermute(value, axis, [((i + step) % size, i) for i in range(size)])  45.6 us
  transfers between devices with their start and end apart: 55, of which 34 were waited for; matrix products, arithmetic and copies ran while one was open for 0% of the time, Pallas kernels for 20%

profile of v4, /device:TPU:0, one launch (start us, length us, event | category | flops | bytes accessed | tf_op | source)
XLA Modules:
  0.0 253.5 jit_solution(12208394103312346030)
XLA Ops:
  4.7 3.0 %collective-permute-start = (bf16[104,768]{1,0:T(8,128)(2,1)}, bf16[104,768]{1,0:T(8,128)(2,1)S(1)}, u32[]{:S(2)}, u32[]{:S(2)}) collective-permute-start(bf16[104,768]{1,0:T(8,128)(2,1)} %get-tuple-element.274), channel_id=1, source_target_pairs={{4,0},{0,4},{5,1},{1,5},{6,2},{2,6},{7,3},{3,7},{12,8},{8,12},{13,... | collective-permute-start | bytes 479240 | tf_op jit(solution)/shard_map/ppermute | solution.py:46
  8.7 3.3 %collective-permute-done.got = bf16[104,768]{1,0:T(8,128)(2,1)S(1)} collective-permute-done((bf16[104,768]{1,0:T(8,128)(2,1)}, bf16[104,768]{1,0:T(8,128)(2,1)S(1)}, u32[]{:S(2)}, u32[]{:S(2)}) %collective-permute-start) | collective-permute-done | bytes 159776 | tf_op jit(solution)/shard_map/ppermute | solution.py:46
  12.6 2.9 %collective-permute-start.1 = (bf16[2,104,768]{2,1,0:T(8,128)(2,1)S(1)}, bf16[2,104,768]{2,1,0:T(8,128)(2,1)S(1)}, u32[]{:S(2)}, u32[]{:S(2)}) collective-permute-start(bf16[2,104,768]{2,1,0:T(8,128)(2,1)S(1)} %place.3.own), channel_id=1, source_target_pairs={{16,0},{0,16},{17,1},{1,17},{18,2},{2,18},{19,3},{3,19},{20,4},{4,... | collective-permute-start | bytes 958472 | tf_op jit(solution)/shard_map/ppermute | solution.py:46
  18.6 10.7 %collective-permute-done.1.got = bf16[2,104,768]{2,1,0:T(8,128)(2,1)S(1)} collective-permute-done((bf16[2,104,768]{2,1,0:T(8,128)(2,1)S(1)}, bf16[2,104,768]{2,1,0:T(8,128)(2,1)S(1)}, u32[]{:S(2)}, u32[]{:S(2)}) %collective-permute-start.1) | collective-permute-done | bytes 319520 | tf_op jit(solution)/shard_map/ppermute | solution.py:46
  35.4 4.2 %collective-permute-done.6.got = bf16[1,2,96,384]{3,2,1,0:T(8,128)(2,1)S(1)} collective-permute-done((bf16[1,2,96,384]{3,2,1,0:T(8,128)(2,1)S(1)}, bf16[1,2,96,384]{3,2,1,0:T(8,128)(2,1)S(1)}, u32[]{:S(2)}, u32[]{:S(2)}) %collective-permute-start.6) | collective-permute-done | bytes 147488 | tf_op jit(solution)/shard_map/ppermute | solution.py:46
  43.9 8.1 %collective-permute-done.5.got = bf16[2,2,104,768]{3,2,1,0:T(8,128)(2,1)S(1)} collective-permute-done((bf16[2,2,104,768]{3,2,1,0:T(8,128)(2,1)S(1)}, bf16[2,2,104,768]{3,2,1,0:T(8,128)(2,1)S(1)}, u32[]{:S(2)}, u32[]{:S(2)}) %collective-permute-start.5) | collective-permute-done | bytes 639008 | tf_op jit(solution)/shard_map/ppermute | solution.py:46
  57.2 5.4 %attend.1 = (bf16[512,576]{1,0:T(8,128)(2,1)S(1)}, f32[3,256,512]{2,1,0:T(8,128)S(1)}, bf16[256,192]{1,0:T(8,128)(2,1)S(1)}, f32[128,1536]{1,0:T(8,128)S(1)}, bf...) custom-call(s32[14]{0:T(128)S(1)} %copy-done, ...), custom_call_target="tpu_custom_call" | custom-call | flops 2000000000 | bytes 8000000 | tf_op jit(solution)/shard_map/attend/pallas_call | solution.py:104
  63.1 6.3 %collective-permute-done.13 = bf16[1,2,2,96,384]{4,3,2,1,0:T(8,128)(2,1)S(1)} collective-permute-done((bf16[1,2,2,96,384]{4,3,2,1,0:T(8,128)(2,1)S(1)}, bf16[1,2,2,96,384]{4,3,2,1,0:T(8,128)(2,1)S(1)}, u32[]{:S(2)}, u32[]{:S(2)}) %collective-permute-start.13) | collective-permute-done | bytes 294944 | tf_op jit(solution)/shard_map/ppermute | solution.py:46
  76.7 6.6 %collective-permute-done.16.got = bf16[128,1536]{1,0:T(8,128)(2,1)S(1)} collective-permute-done((bf16[128,1536]{1,0:T(8,128)(2,1)S(1)}, bf16[128,1536]{1,0:T(8,128)(2,1)S(1)}, u32[]{:S(2)}, u32[]{:S(2)}) %collective-permute-start.16) | collective-permute-done | bytes 393248 | tf_op jit(solution)/shard_map/ppermute | solution.py:46
  87.2 16.6 %collective-permute-done.18 = bf16[2,2,2,96,384]{4,3,2,1,0:T(8,128)(2,1)S(1)} collective-permute-done((bf16[2,2,2,96,384]{4,3,2,1,0:T(8,128)(2,1)S(1)}, bf16[2,2,2,96,384]{4,3,2,1,0:T(8,128)(2,1)S(1)}, u32[]{:S(2)}, u32[]{:S(2)}) %collective-permute-start.18) | collective-permute-done | bytes 589856 | tf_op jit(solution)/shard_map/ppermute | solution.py:46
  104.1 4.2 %collective-permute-done.21.refs_2_ = bf16[128,1536]{1,0:T(8,128)(2,1)S(1)} collective-permute-done((bf16[128,1536]{1,0:T(8,128)(2,1)S(1)}, bf16[128,1536]{1,0:T(8,128)(2,1)S(1)}, u32[]{:S(2)}, u32[]{:S(2)}) %collective-permute-start.21) | collective-permute-done | bytes 393248 | tf_op jit(solution)/shard_map/ppermute | solution.py:46
  108.3 10.7 %collective-permute-done.20 = bf16[1,2,2,96,384]{4,3,2,1,0:T(8,128)(2,1)S(1)} collective-permute-done((bf16[1,2,2,96,384]{4,3,2,1,0:T(8,128)(2,1)S(1)}, bf16[1,2,2,96,384]{4,3,2,1,0:T(8,128)(2,1)S(1)}, u32[]{:S(2)}, u32[]{:S(2)}) %collective-permute-start.20) | collective-permute-done | bytes 294944 | tf_op jit(solution)/shard_map/ppermute | solution.py:46
  130.2 2.9 %back.2 = (f32[2,128,1536]{2,1,0:T(8,128)S(1)}, bf16[2,128,1536]{2,1,0:T(8,128)(2,1)S(1)}) custom-call(s32[14]{0:T(128)S(1)} %copy-done, bf16[512,256]{1,0:T(8,128)(2,1)S(1)} %get-tuple-element.362.refs_5_.refs_0_, bf16[512,256]{1,0:T(8,128)(2,1)S(1)} %get-tuple-element.381.refs_1_.refs_5_, bf16[512,256]{1,0:T(8,128)(2,1)S(1)} %get-tuple-element.403.refs_2_.refs_5_, ...), custom_call_target="tpu_custom_call" | custom-call | flops 2000000000 | bytes 8000000 | tf_op jit(solution)/shard_map/back/pallas_call | solution.py:104
  143.4 4.0 %collective-permute-done.27 = bf16[128,1536]{1,0:T(8,128)(2,1)S(1)} collective-permute-done((bf16[128,1536]{1,0:T(8,128)(2,1)S(1)}, bf16[128,1536]{1,0:T(8,128)(2,1)S(1)}, u32[]{:S(2)}, u32[]{:S(2)}) %collective-permute-start.27) | collective-permute-done | bytes 393248 | tf_op jit(solution)/shard_map/ppermute | solution.py:46
  152.9 8.7 %collective-permute-done.31 = bf16[1,768,384]{2,1,0:T(8,128)(2,1)S(1)} collective-permute-done((bf16[1,768,384]{2,1,0:T(8,128)(2,1)S(1)}, bf16[1,768,384]{2,1,0:T(8,128)(2,1)S(1)}, u32[]{:S(2)}, u32[]{:S(2)}) %collective-permute-start.31) | collective-permute-done | bytes 589856 | tf_op jit(solution)/shard_map/ppermute | solution.py:46
  167.1 9.7 %collective-permute-done.33.d_far = bf16[128,1536]{1,0:T(8,128)(2,1)S(1)} collective-permute-done((bf16[128,1536]{1,0:T(8,128)(2,1)S(1)}, bf16[128,1536]{1,0:T(8,128)(2,1)S(1)}, u32[]{:S(2)}, u32[]{:S(2)}) %collective-permute-start.33) | collective-permute-done | bytes 393248 | tf_op jit(solution)/shard_map/ppermute | solution.py:46
  176.8 4.4 %attend_back.1 = (bf16[256,192]{1,0:T(8,128)(2,1)S(1)}, f32[2,128,384]{2,1,0:T(8,128)S(1)}, bf16[2,128,384]{2,1,0:T(8,128)(2,1)S(1)}, f32[8,128]{1,0:T(8,128)S(1)}) custom-call(s32[14]{0:T(128)S(1)} %copy-done, bf16[512,576]{1,0:T(8,128)(2,1)S(1)} %get-tuple-element.305.qkv, f32[3,256,512]{2,1,0:T(8,128)S(1)} %get-tuple-element.306.probs_in, ...), custom_call_target="tpu_custom_call" | custom-call | flops 2000000000 | bytes 8000000 | tf_op jit(solution)/shard_map/attend_back/pallas_call | solution.py:104
  185.1 3.3 %collective-permute-done.37 = bf16[1,768,384]{2,1,0:T(8,128)(2,1)S(1)} collective-permute-done((bf16[1,768,384]{2,1,0:T(8,128)(2,1)S(1)}, bf16[1,768,384]{2,1,0:T(8,128)(2,1)S(1)}, u32[]{:S(2)}, u32[]{:S(2)}) %collective-permute-start.37) | collective-permute-done | bytes 589856 | tf_op jit(solution)/shard_map/ppermute | solution.py:46
  193.9 2.7 %collective-permute-start.41 = (bf16[384,384]{1,0:T(8,128)(2,1)S(1)}, bf16[384,384]{1,0:T(8,128)(2,1)S(1)}, u32[]{:S(2)}, u32[]{:S(2)}) collective-permute-start(bf16[384,384]{1,0:T(8,128)(2,1)S(1)} %bitcast.108), channel_id=1, source_target_pairs={{16,0},{0,16},{17,1},{1,17},{18,2},{2,18},{19,3},{3,19},{20,4},{4,... | collective-permute-start | bytes 884744 | tf_op jit(solution)/shard_map/ppermute | solution.py:46
  196.6 7.6 %collective-permute-done.42 = bf16[1,768,384]{2,1,0:T(8,128)(2,1)S(1)} collective-permute-done((bf16[1,768,384]{2,1,0:T(8,128)(2,1)S(1)}, bf16[1,768,384]{2,1,0:T(8,128)(2,1)S(1)}, u32[]{:S(2)}, u32[]{:S(2)}) %collective-permute-start.42) | collective-permute-done | bytes 589856 | tf_op jit(solution)/shard_map/ppermute | solution.py:46
  204.9 7.8 %collective-permute-done.41 = bf16[384,384]{1,0:T(8,128)(2,1)S(1)} collective-permute-done((bf16[384,384]{1,0:T(8,128)(2,1)S(1)}, bf16[384,384]{1,0:T(8,128)(2,1)S(1)}, u32[]{:S(2)}, u32[]{:S(2)}) %collective-permute-start.41) | collective-permute-done | bytes 294944 | tf_op jit(solution)/shard_map/ppermute | solution.py:46
  220.7 3.7 %collective-permute-done.50.got = bf16[2,192,384]{2,1,0:T(8,128)(2,1)S(1)} collective-permute-done((bf16[2,192,384]{2,1,0:T(8,128)(2,1)S(1)}, bf16[2,192,384]{2,1,0:T(8,128)(2,1)S(1)}, u32[]{:S(2)}, u32[]{:S(2)}) %collective-permute-start.50) | collective-permute-done | bytes 294944 | tf_op jit(solution)/shard_map/ppermute | solution.py:46
  225.1 9.2 %collective-permute-done.43.refs_0_ = bf16[208,768]{1,0:T(8,128)(2,1)S(1)} collective-permute-done((bf16[208,768]{1,0:T(8,128)(2,1)S(1)}, bf16[208,768]{1,0:T(8,128)(2,1)S(1)}, u32[]{:S(2)}, u32[]{:S(2)}) %collective-permute-start.43) | collective-permute-done | bytes 319520 | tf_op jit(solution)/shard_map/ppermute | solution.py:46
  237.9 4.6 %collective-permute-done.46.refs_1_ = bf16[3,2,96,384]{3,2,1,0:T(8,128)(2,1)S(1)} collective-permute-done((bf16[3,2,96,384]{3,2,1,0:T(8,128)(2,1)S(1)}, bf16[3,2,96,384]{3,2,1,0:T(8,128)(2,1)S(1)}, u32[]{:S(2)}, u32[]{:S(2)}) %collective-permute-start.46) | collective-permute-done | bytes 442400 | tf_op jit(solution)/shard_map/ppermute | solution.py:46
  (159 shorter events, 100.9 us)
Async XLA Ops:
  12.6 16.6 %collective-permute-start.1 = (bf16[2,104,768]{2,1,0:T(8,128)(2,1)S(1)}, bf16[2,104,768]{2,1,0:T(8,128)(2,1)S(1)}, u32[]{:S(2)}, u32[]{:S(2)}) collective-permute-start(bf16[2,104,768]{2,1,0:T(8,128)(2,1)S(1)} %place.3.own), channel_id=1, source_target_pairs={{16,0},{0,16},{17,1},{1,17},{18,2},{2,18},{19,3},{3,19},{20,4},{4,... | collective-permute-start | bytes 958472 | tf_op jit(solution)/shard_map/ppermute | solution.py:46
  15.5 17.4 %collective-permute-start.4 = (bf16[128,1536]{1,0:T(8,128)(2,1)S(1)}, bf16[128,1536]{1,0:T(8,128)(2,1)S(1)}, u32[]{:S(2)}, u32[]{:S(2)}) collective-permute-start(bf16[128,1536]{1,0:T(8,128)(2,1)S(1)} %bitcast.93), channel_id=1, source_target_pairs={{8,0},{0,8},{9,1},{1,9},{10,2},{2,10},{11,3},{3,11},{12,4},{4,12},... | collective-permute-start | bytes 1179656 | tf_op jit(solution)/shard_map/ppermute | solution.py:46
  32.9 19.2 %collective-permute-start.5 = (bf16[2,2,104,768]{3,2,1,0:T(8,128)(2,1)S(1)}, bf16[2,2,104,768]{3,2,1,0:T(8,128)(2,1)S(1)}, u32[]{:S(2)}, u32[]{:S(2)}) collective-permute-start(bf16[2,2,104,768]{3,2,1,0:T(8,128)(2,1)S(1)} %place.4.own), channel_id=1, source_target_pairs={{8,0},{0,8},{9,1},{1,9},{10,2},{2,10},{11,3},{3,11},{12,4},{4,12},... | collective-permute-start | bytes 1916936 | tf_op jit(solution)/shard_map/ppermute | solution.py:46
  52.8 18.9 %collective-permute-start.12 = (bf16[3,2,96,384]{3,2,1,0:T(8,128)(2,1)S(1)}, bf16[3,2,96,384]{3,2,1,0:T(8,128)(2,1)S(1)}, u32[]{:S(2)}, u32[]{:S(2)}) collective-permute-start(bf16[3,2,96,384]{3,2,1,0:T(8,128)(2,1)S(1)} %get-tuple-element.312), channel_id=1, source_target_pairs={{8,0},{0,8},{9,1},{1,9},{10,2},{2,10},{11,3},{3,11},{12,4},{4,12},... | collective-permute-start | bytes 1327112 | tf_op jit(solution)/shard_map/ppermute | solution.py:46
  53.1 16.4 %collective-permute-start.13 = (bf16[1,2,2,96,384]{4,3,2,1,0:T(8,128)(2,1)S(1)}, bf16[1,2,2,96,384]{4,3,2,1,0:T(8,128)(2,1)S(1)}, u32[]{:S(2)}, u32[]{:S(2)}) collective-permute-start(bf16[1,2,2,96,384]{4,3,2,1,0:T(8,128)(2,1)S(1)} %bitcast.72), channel_id=1, source_target_pairs={{16,0},{0,16},{17,1},{1,17},{18,2},{2,18},{19,3},{3,19},{20,4},{4,... | collective-permute-start | bytes 884744 | tf_op jit(solution)/shard_map/ppermute | solution.py:46
  74.9 28.8 %collective-permute-start.19 = (bf16[3,384,384]{2,1,0:T(8,128)(2,1)S(1)}, bf16[3,384,384]{2,1,0:T(8,128)(2,1)S(1)}, u32[]{:S(2)}, u32[]{:S(2)}) collective-permute-start(bf16[3,384,384]{2,1,0:T(8,128)(2,1)S(1)} %bitcast.55), channel_id=1, source_target_pairs={{4,0},{0,4},{5,1},{1,5},{6,2},{2,6},{7,3},{3,7},{12,8},{8,12},{13,... | collective-permute-start | bytes 2654216 | tf_op jit(solution)/shard_map/ppermute | solution.py:46
  76.1 27.7 %collective-permute-start.18 = (bf16[2,2,2,96,384]{4,3,2,1,0:T(8,128)(2,1)S(1)}, bf16[2,2,2,96,384]{4,3,2,1,0:T(8,128)(2,1)S(1)}, u32[]{:S(2)}, u32[]{:S(2)}) collective-permute-start(bf16[2,2,2,96,384]{4,3,2,1,0:T(8,128)(2,1)S(1)} %get-tuple-element.333), channel_id=1, source_target_pairs={{16,0},{0,16},{17,1},{1,17},{18,2},{2,18},{19,3},{3,19},{20,4},{4,... | collective-permute-start | bytes 1769480 | tf_op jit(solution)/shard_map/ppermute | solution.py:46
  84.4 19.4 %collective-permute-start.17 = (bf16[128,1536]{1,0:T(8,128)(2,1)S(1)}, bf16[128,1536]{1,0:T(8,128)(2,1)S(1)}, u32[]{:S(2)}, u32[]{:S(2)}) collective-permute-start(bf16[128,1536]{1,0:T(8,128)(2,1)S(1)} %get-tuple-element.365.refs_0_), channel_id=1, source_target_pairs={{2,0},{0,2},{3,1},{1,3},{6,4},{4,6},{7,5},{5,7},{10,8},{8,10},{11,... | collective-permute-start | bytes 1179656 | tf_op jit(solution)/shard_map/ppermute | solution.py:46
  84.5 23.8 %collective-permute-start.21 = (bf16[128,1536]{1,0:T(8,128)(2,1)S(1)}, bf16[128,1536]{1,0:T(8,128)(2,1)S(1)}, u32[]{:S(2)}, u32[]{:S(2)}) collective-permute-start(bf16[128,1536]{1,0:T(8,128)(2,1)S(1)} %get-tuple-element.365.refs_0_), channel_id=1, source_target_pairs={{8,0},{0,8},{9,1},{1,9},{10,2},{2,10},{11,3},{3,11},{12,4},{4,12},... | collective-permute-start | bytes 1179656 | tf_op jit(solution)/shard_map/ppermute | solution.py:46
  85.7 18.5 %collective-permute-start.22 = (bf16[1,384,384]{2,1,0:T(8,128)(2,1)S(1)}, bf16[1,384,384]{2,1,0:T(8,128)(2,1)S(1)}, u32[]{:S(2)}, u32[]{:S(2)}) collective-permute-start(bf16[1,384,384]{2,1,0:T(8,128)(2,1)S(1)} %bitcast.77), channel_id=1, source_target_pairs={{4,0},{0,4},{5,1},{1,5},{6,2},{2,6},{7,3},{3,7},{12,8},{8,12},{13,... | collective-permute-start | bytes 884744 | tf_op jit(solution)/shard_map/ppermute | solution.py:46
  103.8 18.7 %collective-permute-start.24 = (bf16[2,384,384]{2,1,0:T(8,128)(2,1)S(1)}, bf16[2,384,384]{2,1,0:T(8,128)(2,1)S(1)}, u32[]{:S(2)}, u32[]{:S(2)}) collective-permute-start(bf16[2,384,384]{2,1,0:T(8,128)(2,1)S(1)} %bitcast.65), channel_id=1, source_target_pairs={{4,0},{0,4},{5,1},{1,5},{6,2},{2,6},{7,3},{3,7},{12,8},{8,12},{13,... | collective-permute-start | bytes 1769480 | tf_op jit(solution)/shard_map/ppermute | solution.py:46
  133.2 16.2 %collective-permute-start.29 = (bf16[1,768,384]{2,1,0:T(8,128)(2,1)S(1)}, bf16[1,768,384]{2,1,0:T(8,128)(2,1)S(1)}, u32[]{:S(2)}, u32[]{:S(2)}) collective-permute-start(bf16[1,768,384]{2,1,0:T(8,128)(2,1)S(1)} %get-tuple-element.417), channel_id=1, source_target_pairs={{4,0},{0,4},{5,1},{1,5},{6,2},{2,6},{7,3},{3,7},{12,8},{8,12},{13,... | collective-permute-start | bytes 1769480 | tf_op jit(solution)/shard_map/ppermute | solution.py:46
  138.8 22.7 %collective-permute-start.31 = (bf16[1,768,384]{2,1,0:T(8,128)(2,1)S(1)}, bf16[1,768,384]{2,1,0:T(8,128)(2,1)S(1)}, u32[]{:S(2)}, u32[]{:S(2)}) collective-permute-start(bf16[1,768,384]{2,1,0:T(8,128)(2,1)S(1)} %get-tuple-element.428), channel_id=1, source_target_pairs={{4,0},{0,4},{5,1},{1,5},{6,2},{2,6},{7,3},{3,7},{12,8},{8,12},{13,... | collective-permute-start | bytes 1769480 | tf_op jit(solution)/shard_map/ppermute | solution.py:46
  150.6 16.5 %collective-permute-start.34 = (bf16[128,1536]{1,0:T(8,128)(2,1)S(1)}, bf16[128,1536]{1,0:T(8,128)(2,1)S(1)}, u32[]{:S(2)}, u32[]{:S(2)}) collective-permute-start(bf16[128,1536]{1,0:T(8,128)(2,1)S(1)} %get-tuple-element.437), channel_id=1, source_target_pairs={{8,0},{0,8},{9,1},{1,9},{10,2},{2,10},{11,3},{3,11},{12,4},{4,12},... | collective-permute-start | bytes 1179656 | tf_op jit(solution)/shard_map/ppermute | solution.py:46
  166.2 22.2 %collective-permute-start.37 = (bf16[1,768,384]{2,1,0:T(8,128)(2,1)S(1)}, bf16[1,768,384]{2,1,0:T(8,128)(2,1)S(1)}, u32[]{:S(2)}, u32[]{:S(2)}) collective-permute-start(bf16[1,768,384]{2,1,0:T(8,128)(2,1)S(1)} %get-tuple-element.456), channel_id=1, source_target_pairs={{4,0},{0,4},{5,1},{1,5},{6,2},{2,6},{7,3},{3,7},{12,8},{8,12},{13,... | collective-permute-start | bytes 1769480 | tf_op jit(solution)/shard_map/ppermute | solution.py:46
  192.2 23.1 %collective-permute-start.39 = (bf16[400,768]{1,0:T(8,128)(2,1)S(1)}, bf16[400,768]{1,0:T(8,128)(2,1)S(1)}, u32[]{:S(2)}, u32[]{:S(2)}) collective-permute-start(bf16[400,768]{1,0:T(8,128)(2,1)S(1)} %bitcast.87), channel_id=1, source_target_pairs={{8,0},{0,8},{9,1},{1,9},{10,2},{2,10},{11,3},{3,11},{12,4},{4,12},... | collective-permute-start | bytes 1843208 | tf_op jit(solution)/shard_map/ppermute | solution.py:46
  192.3 20.4 %collective-permute-start.40 = (bf16[128,1536]{1,0:T(8,128)(2,1)S(1)}, bf16[128,1536]{1,0:T(8,128)(2,1)S(1)}, u32[]{:S(2)}, u32[]{:S(2)}) collective-permute-start(bf16[128,1536]{1,0:T(8,128)(2,1)S(1)} %add_convert_fusion.1.own), channel_id=1, source_target_pairs={{1,0},{0,1},{3,2},{2,3},{5,4},{4,5},{7,6},{6,7},{9,8},{8,9},{11,10... | collective-permute-start | bytes 1179656 | tf_op jit(solution)/shard_map/ppermute | solution.py:46
  193.9 18.9 %collective-permute-start.41 = (bf16[384,384]{1,0:T(8,128)(2,1)S(1)}, bf16[384,384]{1,0:T(8,128)(2,1)S(1)}, u32[]{:S(2)}, u32[]{:S(2)}) collective-permute-start(bf16[384,384]{1,0:T(8,128)(2,1)S(1)} %bitcast.108), channel_id=1, source_target_pairs={{16,0},{0,16},{17,1},{1,17},{18,2},{2,18},{19,3},{3,19},{20,4},{4,... | collective-permute-start | bytes 884744 | tf_op jit(solution)/shard_map/ppermute | solution.py:46
  204.9 19.5 %collective-permute-start.50 = (bf16[2,192,384]{2,1,0:T(8,128)(2,1)S(1)}, bf16[2,192,384]{2,1,0:T(8,128)(2,1)S(1)}, u32[]{:S(2)}, u32[]{:S(2)}) collective-permute-start(bf16[2,192,384]{2,1,0:T(8,128)(2,1)S(1)} %get-tuple-element.511), channel_id=1, source_target_pairs={{8,0},{0,8},{9,1},{1,9},{10,2},{2,10},{11,3},{3,11},{12,4},{4,12},... | collective-permute-start | bytes 884744 | tf_op jit(solution)/shard_map/ppermute | solution.py:46
  215.9 18.4 %collective-permute-start.43 = (bf16[208,768]{1,0:T(8,128)(2,1)S(1)}, bf16[208,768]{1,0:T(8,128)(2,1)S(1)}, u32[]{:S(2)}, u32[]{:S(2)}) collective-permute-start(bf16[208,768]{1,0:T(8,128)(2,1)S(1)} %bitcast.102), channel_id=1, source_target_pairs={{16,0},{0,16},{17,1},{1,17},{18,2},{2,18},{19,3},{3,19},{20,4},{4,... | collective-permute-start | bytes 958472 | tf_op jit(solution)/shard_map/ppermute | solution.py:46
  218.4 16.6 %collective-permute-start.44 = (bf16[128,1536]{1,0:T(8,128)(2,1)S(1)}, bf16[128,1536]{1,0:T(8,128)(2,1)S(1)}, u32[]{:S(2)}, u32[]{:S(2)}) collective-permute-start(bf16[128,1536]{1,0:T(8,128)(2,1)S(1)} %get-tuple-element.493), channel_id=1, source_target_pairs={{4,0},{0,4},{5,1},{1,5},{6,2},{2,6},{7,3},{3,7},{12,8},{8,12},{13,... | collective-permute-start | bytes 1179656 | tf_op jit(solution)/shard_map/ppermute | solution.py:46
  220.5 22.0 %collective-permute-start.46 = (bf16[3,2,96,384]{3,2,1,0:T(8,128)(2,1)S(1)}, bf16[3,2,96,384]{3,2,1,0:T(8,128)(2,1)S(1)}, u32[]{:S(2)}, u32[]{:S(2)}) collective-permute-start(bf16[3,2,96,384]{3,2,1,0:T(8,128)(2,1)S(1)} %get-tuple-element.504), channel_id=1, source_target_pairs={{8,0},{0,8},{9,1},{1,9},{10,2},{2,10},{11,3},{3,11},{12,4},{4,12},... | collective-permute-start | bytes 1327112 | tf_op jit(solution)/shard_map/ppermute | solution.py:46
  220.6 25.4 %collective-permute-start.47 = (bf16[3,96,384]{2,1,0:T(8,128)(2,1)S(1)}, bf16[3,96,384]{2,1,0:T(8,128)(2,1)S(1)}, u32[]{:S(2)}, u32[]{:S(2)}) collective-permute-start(bf16[3,96,384]{2,1,0:T(8,128)(2,1)S(1)} %get-tuple-element.505), channel_id=1, source_target_pairs={{2,0},{0,2},{3,1},{1,3},{6,4},{4,6},{7,5},{5,7},{10,8},{8,10},{11,... | collective-permute-start | bytes 663560 | tf_op jit(solution)/shard_map/ppermute | solution.py:46
  225.0 19.8 %collective-permute-start.51 = (bf16[2,192,384]{2,1,0:T(8,128)(2,1)S(1)}, bf16[2,192,384]{2,1,0:T(8,128)(2,1)S(1)}, u32[]{:S(2)}, u32[]{:S(2)}) collective-permute-start(bf16[2,192,384]{2,1,0:T(8,128)(2,1)S(1)} %bitcast.106), channel_id=1, source_target_pairs={{16,0},{0,16},{17,1},{1,17},{18,2},{2,18},{19,3},{3,19},{20,4},{4,... | collective-permute-start | bytes 884744 | tf_op jit(solution)/shard_map/ppermute | solution.py:46
  (44 other events, 343.0 us)

commit v5 on v4

--- a/solution.py
+++ b/solution.py
@@ -68,7 +68,7 @@
         return values
 
 
-costs = {"attn_final": 200, "last_z": 40, "place": 200}
+costs = {"attn_final": 200, "back": 200, "last_z": 40, "mixed": 40, "place": 200}
 
 
 def runs_of(dims, order, inverse):

time: 254 us -> 254 us (level)
  no operation moved by 1% of the time
where the time goes in v5:
time: 254 us; the launch traced here: 253 us
  waiting for transfers between devices  146 us (57%)
  Pallas kernels  58.9 us (23%)
  starting transfers between devices  45.5 us (18%)
    ppermute x55, waiting for transfers between devices, fetch(): lax.ppermute(value, axis, [((i + step) % size, i) for i in range(size)])  146 us
    pallas_call x40, Pallas kernels, call(): pl.pallas_call(functools.partial(body, **static), out_shape=tuple((jax.Sh...  58.9 us
    ppermute x55, starting transfers between devices, fetch(): lax.ppermute(value, axis, [((i + step) % size, i) for i in range(size)])  45.5 us
  transfers between devices with their start and end apart: 55, of which 34 were waited for; matrix products, arithmetic and copies ran while one was open for 0% of the time, Pallas kernels for 20%

profile of v5, /device:TPU:0, one launch (start us, length us, event | category | flops | bytes accessed | tf_op | source)
XLA Modules:
  0.0 253.5 jit_solution(14016018314303872541)
XLA Ops:
  4.7 3.0 %collective-permute-start = (bf16[104,768]{1,0:T(8,128)(2,1)}, bf16[104,768]{1,0:T(8,128)(2,1)S(1)}, u32[]{:S(2)}, u32[]{:S(2)}) collective-permute-start(bf16[104,768]{1,0:T(8,128)(2,1)} %get-tuple-element.274), channel_id=1, source_target_pairs={{4,0},{0,4},{5,1},{1,5},{6,2},{2,6},{7,3},{3,7},{12,8},{8,12},{13,... | collective-permute-start | bytes 479240 | tf_op jit(solution)/shard_map/ppermute | solution.py:46
  8.7 3.3 %collective-permute-done.got = bf16[104,768]{1,0:T(8,128)(2,1)S(1)} collective-permute-done((bf16[104,768]{1,0:T(8,128)(2,1)}, bf16[104,768]{1,0:T(8,128)(2,1)S(1)}, u32[]{:S(2)}, u32[]{:S(2)}) %collective-permute-start) | collective-permute-done | bytes 159776 | tf_op jit(solution)/shard_map/ppermute | solution.py:46
  12.6 2.9 %collective-permute-start.1 = (bf16[2,104,768]{2,1,0:T(8,128)(2,1)S(1)}, bf16[2,104,768]{2,1,0:T(8,128)(2,1)S(1)}, u32[]{:S(2)}, u32[]{:S(2)}) collective-permute-start(bf16[2,104,768]{2,1,0:T(8,128)(2,1)S(1)} %place.3.own), channel_id=1, source_target_pairs={{16,0},{0,16},{17,1},{1,17},{18,2},{2,18},{19,3},{3,19},{20,4},{4,... | collective-permute-start | bytes 958472 | tf_op jit(solution)/shard_map/ppermute | solution.py:46
  18.6 10.7 %collective-permute-done.1.got = bf16[2,104,768]{2,1,0:T(8,128)(2,1)S(1)} collective-permute-done((bf16[2,104,768]{2,1,0:T(8,128)(2,1)S(1)}, bf16[2,104,768]{2,1,0:T(8,128)(2,1)S(1)}, u32[]{:S(2)}, u32[]{:S(2)}) %collective-permute-start.1) | collective-permute-done | bytes 319520 | tf_op jit(solution)/shard_map/ppermute | solution.py:46
  35.4 4.2 %collective-permute-done.6.got = bf16[1,2,96,384]{3,2,1,0:T(8,128)(2,1)S(1)} collective-permute-done((bf16[1,2,96,384]{3,2,1,0:T(8,128)(2,1)S(1)}, bf16[1,2,96,384]{3,2,1,0:T(8,128)(2,1)S(1)}, u32[]{:S(2)}, u32[]{:S(2)}) %collective-permute-start.6) | collective-permute-done | bytes 147488 | tf_op jit(solution)/shard_map/ppermute | solution.py:46
  43.9 8.1 %collective-permute-done.5.got = bf16[2,2,104,768]{3,2,1,0:T(8,128)(2,1)S(1)} collective-permute-done((bf16[2,2,104,768]{3,2,1,0:T(8,128)(2,1)S(1)}, bf16[2,2,104,768]{3,2,1,0:T(8,128)(2,1)S(1)}, u32[]{:S(2)}, u32[]{:S(2)}) %collective-permute-start.5) | collective-permute-done | bytes 639008 | tf_op jit(solution)/shard_map/ppermute | solution.py:46
  57.2 5.4 %attend.1 = (bf16[512,576]{1,0:T(8,128)(2,1)S(1)}, f32[3,256,512]{2,1,0:T(8,128)S(1)}, bf16[256,192]{1,0:T(8,128)(2,1)S(1)}, f32[128,1536]{1,0:T(8,128)S(1)}, bf...) custom-call(s32[14]{0:T(128)S(1)} %copy-done, ...), custom_call_target="tpu_custom_call" | custom-call | flops 2000000000 | bytes 8000000 | tf_op jit(solution)/shard_map/attend/pallas_call | solution.py:104
  63.1 6.3 %collective-permute-done.13 = bf16[1,2,2,96,384]{4,3,2,1,0:T(8,128)(2,1)S(1)} collective-permute-done((bf16[1,2,2,96,384]{4,3,2,1,0:T(8,128)(2,1)S(1)}, bf16[1,2,2,96,384]{4,3,2,1,0:T(8,128)(2,1)S(1)}, u32[]{:S(2)}, u32[]{:S(2)}) %collective-permute-start.13) | collective-permute-done | bytes 294944 | tf_op jit(solution)/shard_map/ppermute | solution.py:46
  76.7 6.6 %collective-permute-done.16.got = bf16[128,1536]{1,0:T(8,128)(2,1)S(1)} collective-permute-done((bf16[128,1536]{1,0:T(8,128)(2,1)S(1)}, bf16[128,1536]{1,0:T(8,128)(2,1)S(1)}, u32[]{:S(2)}, u32[]{:S(2)}) %collective-permute-start.16) | collective-permute-done | bytes 393248 | tf_op jit(solution)/shard_map/ppermute | solution.py:46
  87.2 16.6 %collective-permute-done.18 = bf16[2,2,2,96,384]{4,3,2,1,0:T(8,128)(2,1)S(1)} collective-permute-done((bf16[2,2,2,96,384]{4,3,2,1,0:T(8,128)(2,1)S(1)}, bf16[2,2,2,96,384]{4,3,2,1,0:T(8,128)(2,1)S(1)}, u32[]{:S(2)}, u32[]{:S(2)}) %collective-permute-start.18) | collective-permute-done | bytes 589856 | tf_op jit(solution)/shard_map/ppermute | solution.py:46
  104.1 4.2 %collective-permute-done.21.refs_2_ = bf16[128,1536]{1,0:T(8,128)(2,1)S(1)} collective-permute-done((bf16[128,1536]{1,0:T(8,128)(2,1)S(1)}, bf16[128,1536]{1,0:T(8,128)(2,1)S(1)}, u32[]{:S(2)}, u32[]{:S(2)}) %collective-permute-start.21) | collective-permute-done | bytes 393248 | tf_op jit(solution)/shard_map/ppermute | solution.py:46
  108.3 10.7 %collective-permute-done.20 = bf16[1,2,2,96,384]{4,3,2,1,0:T(8,128)(2,1)S(1)} collective-permute-done((bf16[1,2,2,96,384]{4,3,2,1,0:T(8,128)(2,1)S(1)}, bf16[1,2,2,96,384]{4,3,2,1,0:T(8,128)(2,1)S(1)}, u32[]{:S(2)}, u32[]{:S(2)}) %collective-permute-start.20) | collective-permute-done | bytes 294944 | tf_op jit(solution)/shard_map/ppermute | solution.py:46
  130.2 2.9 %back.2 = (f32[2,128,1536]{2,1,0:T(8,128)S(1)}, bf16[2,128,1536]{2,1,0:T(8,128)(2,1)S(1)}) custom-call(s32[14]{0:T(128)S(1)} %copy-done, bf16[512,256]{1,0:T(8,128)(2,1)S(1)} %get-tuple-element.362.refs_5_.refs_0_, bf16[512,256]{1,0:T(8,128)(2,1)S(1)} %get-tuple-element.381.refs_1_.refs_5_, bf16[512,256]{1,0:T(8,128)(2,1)S(1)} %get-tuple-element.403.refs_2_.refs_5_, ...), custom_call_target="tpu_custom_call" | custom-call | flops 4000000000 | bytes 16000000 | tf_op jit(solution)/shard_map/back/pallas_call | solution.py:104
  143.4 4.0 %collective-permute-done.27 = bf16[128,1536]{1,0:T(8,128)(2,1)S(1)} collective-permute-done((bf16[128,1536]{1,0:T(8,128)(2,1)S(1)}, bf16[128,1536]{1,0:T(8,128)(2,1)S(1)}, u32[]{:S(2)}, u32[]{:S(2)}) %collective-permute-start.27) | collective-permute-done | bytes 393248 | tf_op jit(solution)/shard_map/ppermute | solution.py:46
  152.9 8.7 %collective-permute-done.31 = bf16[1,768,384]{2,1,0:T(8,128)(2,1)S(1)} collective-permute-done((bf16[1,768,384]{2,1,0:T(8,128)(2,1)S(1)}, bf16[1,768,384]{2,1,0:T(8,128)(2,1)S(1)}, u32[]{:S(2)}, u32[]{:S(2)}) %collective-permute-start.31) | collective-permute-done | bytes 589856 | tf_op jit(solution)/shard_map/ppermute | solution.py:46
  167.1 9.7 %collective-permute-done.33.d_far = bf16[128,1536]{1,0:T(8,128)(2,1)S(1)} collective-permute-done((bf16[128,1536]{1,0:T(8,128)(2,1)S(1)}, bf16[128,1536]{1,0:T(8,128)(2,1)S(1)}, u32[]{:S(2)}, u32[]{:S(2)}) %collective-permute-start.33) | collective-permute-done | bytes 393248 | tf_op jit(solution)/shard_map/ppermute | solution.py:46
  176.8 4.5 %attend_back.1 = (bf16[256,192]{1,0:T(8,128)(2,1)S(1)}, f32[2,128,384]{2,1,0:T(8,128)S(1)}, bf16[2,128,384]{2,1,0:T(8,128)(2,1)S(1)}, f32[8,128]{1,0:T(8,128)S(1)}) custom-call(s32[14]{0:T(128)S(1)} %copy-done, bf16[512,576]{1,0:T(8,128)(2,1)S(1)} %get-tuple-element.305.qkv, f32[3,256,512]{2,1,0:T(8,128)S(1)} %get-tuple-element.306.probs_in, ...), custom_call_target="tpu_custom_call" | custom-call | flops 2000000000 | bytes 8000000 | tf_op jit(solution)/shard_map/attend_back/pallas_call | solution.py:104
  185.1 3.3 %collective-permute-done.37 = bf16[1,768,384]{2,1,0:T(8,128)(2,1)S(1)} collective-permute-done((bf16[1,768,384]{2,1,0:T(8,128)(2,1)S(1)}, bf16[1,768,384]{2,1,0:T(8,128)(2,1)S(1)}, u32[]{:S(2)}, u32[]{:S(2)}) %collective-permute-start.37) | collective-permute-done | bytes 589856 | tf_op jit(solution)/shard_map/ppermute | solution.py:46
  193.9 2.7 %collective-permute-start.41 = (bf16[384,384]{1,0:T(8,128)(2,1)S(1)}, bf16[384,384]{1,0:T(8,128)(2,1)S(1)}, u32[]{:S(2)}, u32[]{:S(2)}) collective-permute-start(bf16[384,384]{1,0:T(8,128)(2,1)S(1)} %bitcast.108), channel_id=1, source_target_pairs={{16,0},{0,16},{17,1},{1,17},{18,2},{2,18},{19,3},{3,19},{20,4},{4,... | collective-permute-start | bytes 884744 | tf_op jit(solution)/shard_map/ppermute | solution.py:46
  196.6 7.6 %collective-permute-done.42 = bf16[1,768,384]{2,1,0:T(8,128)(2,1)S(1)} collective-permute-done((bf16[1,768,384]{2,1,0:T(8,128)(2,1)S(1)}, bf16[1,768,384]{2,1,0:T(8,128)(2,1)S(1)}, u32[]{:S(2)}, u32[]{:S(2)}) %collective-permute-start.42) | collective-permute-done | bytes 589856 | tf_op jit(solution)/shard_map/ppermute | solution.py:46
  204.9 7.8 %collective-permute-done.41 = bf16[384,384]{1,0:T(8,128)(2,1)S(1)} collective-permute-done((bf16[384,384]{1,0:T(8,128)(2,1)S(1)}, bf16[384,384]{1,0:T(8,128)(2,1)S(1)}, u32[]{:S(2)}, u32[]{:S(2)}) %collective-permute-start.41) | collective-permute-done | bytes 294944 | tf_op jit(solution)/shard_map/ppermute | solution.py:46
  220.6 3.7 %collective-permute-done.50.got = bf16[2,192,384]{2,1,0:T(8,128)(2,1)S(1)} collective-permute-done((bf16[2,192,384]{2,1,0:T(8,128)(2,1)S(1)}, bf16[2,192,384]{2,1,0:T(8,128)(2,1)S(1)}, u32[]{:S(2)}, u32[]{:S(2)}) %collective-permute-start.50) | collective-permute-done | bytes 294944 | tf_op jit(solution)/shard_map/ppermute | solution.py:46
  225.1 9.3 %collective-permute-done.43.refs_0_ = bf16[208,768]{1,0:T(8,128)(2,1)S(1)} collective-permute-done((bf16[208,768]{1,0:T(8,128)(2,1)S(1)}, bf16[208,768]{1,0:T(8,128)(2,1)S(1)}, u32[]{:S(2)}, u32[]{:S(2)}) %collective-permute-start.43) | collective-permute-done | bytes 319520 | tf_op jit(solution)/shard_map/ppermute | solution.py:46
  237.9 4.7 %collective-permute-done.46.refs_1_ = bf16[3,2,96,384]{3,2,1,0:T(8,128)(2,1)S(1)} collective-permute-done((bf16[3,2,96,384]{3,2,1,0:T(8,128)(2,1)S(1)}, bf16[3,2,96,384]{3,2,1,0:T(8,128)(2,1)S(1)}, u32[]{:S(2)}, u32[]{:S(2)}) %collective-permute-start.46) | collective-permute-done | bytes 442400 | tf_op jit(solution)/shard_map/ppermute | solution.py:46
  (159 shorter events, 100.8 us)
Async XLA Ops:
  12.6 16.6 %collective-permute-start.1 = (bf16[2,104,768]{2,1,0:T(8,128)(2,1)S(1)}, bf16[2,104,768]{2,1,0:T(8,128)(2,1)S(1)}, u32[]{:S(2)}, u32[]{:S(2)}) collective-permute-start(bf16[2,104,768]{2,1,0:T(8,128)(2,1)S(1)} %place.3.own), channel_id=1, source_target_pairs={{16,0},{0,16},{17,1},{1,17},{18,2},{2,18},{19,3},{3,19},{20,4},{4,... | collective-permute-start | bytes 958472 | tf_op jit(solution)/shard_map/ppermute | solution.py:46
  15.5 17.4 %collective-permute-start.4 = (bf16[128,1536]{1,0:T(8,128)(2,1)S(1)}, bf16[128,1536]{1,0:T(8,128)(2,1)S(1)}, u32[]{:S(2)}, u32[]{:S(2)}) collective-permute-start(bf16[128,1536]{1,0:T(8,128)(2,1)S(1)} %bitcast.80), channel_id=1, source_target_pairs={{8,0},{0,8},{9,1},{1,9},{10,2},{2,10},{11,3},{3,11},{12,4},{4,12},... | collective-permute-start | bytes 1179656 | tf_op jit(solution)/shard_map/ppermute | solution.py:46
  32.9 19.2 %collective-permute-start.5 = (bf16[2,2,104,768]{3,2,1,0:T(8,128)(2,1)S(1)}, bf16[2,2,104,768]{3,2,1,0:T(8,128)(2,1)S(1)}, u32[]{:S(2)}, u32[]{:S(2)}) collective-permute-start(bf16[2,2,104,768]{3,2,1,0:T(8,128)(2,1)S(1)} %place.4.own), channel_id=1, source_target_pairs={{8,0},{0,8},{9,1},{1,9},{10,2},{2,10},{11,3},{3,11},{12,4},{4,12},... | collective-permute-start | bytes 1916936 | tf_op jit(solution)/shard_map/ppermute | solution.py:46
  52.8 18.9 %collective-permute-start.12 = (bf16[3,2,96,384]{3,2,1,0:T(8,128)(2,1)S(1)}, bf16[3,2,96,384]{3,2,1,0:T(8,128)(2,1)S(1)}, u32[]{:S(2)}, u32[]{:S(2)}) collective-permute-start(bf16[3,2,96,384]{3,2,1,0:T(8,128)(2,1)S(1)} %get-tuple-element.312), channel_id=1, source_target_pairs={{8,0},{0,8},{9,1},{1,9},{10,2},{2,10},{11,3},{3,11},{12,4},{4,12},... | collective-permute-start | bytes 1327112 | tf_op jit(solution)/shard_map/ppermute | solution.py:46
  53.1 16.4 %collective-permute-start.13 = (bf16[1,2,2,96,384]{4,3,2,1,0:T(8,128)(2,1)S(1)}, bf16[1,2,2,96,384]{4,3,2,1,0:T(8,128)(2,1)S(1)}, u32[]{:S(2)}, u32[]{:S(2)}) collective-permute-start(bf16[1,2,2,96,384]{4,3,2,1,0:T(8,128)(2,1)S(1)} %bitcast.90), channel_id=1, source_target_pairs={{16,0},{0,16},{17,1},{1,17},{18,2},{2,18},{19,3},{3,19},{20,4},{4,... | collective-permute-start | bytes 884744 | tf_op jit(solution)/shard_map/ppermute | solution.py:46
  74.9 28.8 %collective-permute-start.19 = (bf16[3,384,384]{2,1,0:T(8,128)(2,1)S(1)}, bf16[3,384,384]{2,1,0:T(8,128)(2,1)S(1)}, u32[]{:S(2)}, u32[]{:S(2)}) collective-permute-start(bf16[3,384,384]{2,1,0:T(8,128)(2,1)S(1)} %bitcast.57), channel_id=1, source_target_pairs={{4,0},{0,4},{5,1},{1,5},{6,2},{2,6},{7,3},{3,7},{12,8},{8,12},{13,... | collective-permute-start | bytes 2654216 | tf_op jit(solution)/shard_map/ppermute | solution.py:46
  76.1 27.7 %collective-permute-start.18 = (bf16[2,2,2,96,384]{4,3,2,1,0:T(8,128)(2,1)S(1)}, bf16[2,2,2,96,384]{4,3,2,1,0:T(8,128)(2,1)S(1)}, u32[]{:S(2)}, u32[]{:S(2)}) collective-permute-start(bf16[2,2,2,96,384]{4,3,2,1,0:T(8,128)(2,1)S(1)} %get-tuple-element.333), channel_id=1, source_target_pairs={{16,0},{0,16},{17,1},{1,17},{18,2},{2,18},{19,3},{3,19},{20,4},{4,... | collective-permute-start | bytes 1769480 | tf_op jit(solution)/shard_map/ppermute | solution.py:46
  84.4 19.3 %collective-permute-start.17 = (bf16[128,1536]{1,0:T(8,128)(2,1)S(1)}, bf16[128,1536]{1,0:T(8,128)(2,1)S(1)}, u32[]{:S(2)}, u32[]{:S(2)}) collective-permute-start(bf16[128,1536]{1,0:T(8,128)(2,1)S(1)} %get-tuple-element.365.refs_0_), channel_id=1, source_target_pairs={{2,0},{0,2},{3,1},{1,3},{6,4},{4,6},{7,5},{5,7},{10,8},{8,10},{11,... | collective-permute-start | bytes 1179656 | tf_op jit(solution)/shard_map/ppermute | solution.py:46
  84.5 23.8 %collective-permute-start.21 = (bf16[128,1536]{1,0:T(8,128)(2,1)S(1)}, bf16[128,1536]{1,0:T(8,128)(2,1)S(1)}, u32[]{:S(2)}, u32[]{:S(2)}) collective-permute-start(bf16[128,1536]{1,0:T(8,128)(2,1)S(1)} %get-tuple-element.365.refs_0_), channel_id=1, source_target_pairs={{8,0},{0,8},{9,1},{1,9},{10,2},{2,10},{11,3},{3,11},{12,4},{4,12},... | collective-permute-start | bytes 1179656 | tf_op jit(solution)/shard_map/ppermute | solution.py:46
  85.7 18.5 %collective-permute-start.22 = (bf16[1,384,384]{2,1,0:T(8,128)(2,1)S(1)}, bf16[1,384,384]{2,1,0:T(8,128)(2,1)S(1)}, u32[]{:S(2)}, u32[]{:S(2)}) collective-permute-start(bf16[1,384,384]{2,1,0:T(8,128)(2,1)S(1)} %bitcast.95), channel_id=1, source_target_pairs={{4,0},{0,4},{5,1},{1,5},{6,2},{2,6},{7,3},{3,7},{12,8},{8,12},{13,... | collective-permute-start | bytes 884744 | tf_op jit(solution)/shard_map/ppermute | solution.py:46
  103.8 18.7 %collective-permute-start.24 = (bf16[2,384,384]{2,1,0:T(8,128)(2,1)S(1)}, bf16[2,384,384]{2,1,0:T(8,128)(2,1)S(1)}, u32[]{:S(2)}, u32[]{:S(2)}) collective-permute-start(bf16[2,384,384]{2,1,0:T(8,128)(2,1)S(1)} %bitcast.68), channel_id=1, source_target_pairs={{4,0},{0,4},{5,1},{1,5},{6,2},{2,6},{7,3},{3,7},{12,8},{8,12},{13,... | collective-permute-start | bytes 1769480 | tf_op jit(solution)/shard_map/ppermute | solution.py:46
  133.2 16.2 %collective-permute-start.29 = (bf16[1,768,384]{2,1,0:T(8,128)(2,1)S(1)}, bf16[1,768,384]{2,1,0:T(8,128)(2,1)S(1)}, u32[]{:S(2)}, u32[]{:S(2)}) collective-permute-start(bf16[1,768,384]{2,1,0:T(8,128)(2,1)S(1)} %get-tuple-element.417), channel_id=1, source_target_pairs={{4,0},{0,4},{5,1},{1,5},{6,2},{2,6},{7,3},{3,7},{12,8},{8,12},{13,... | collective-permute-start | bytes 1769480 | tf_op jit(solution)/shard_map/ppermute | solution.py:46
  138.8 22.7 %collective-permute-start.31 = (bf16[1,768,384]{2,1,0:T(8,128)(2,1)S(1)}, bf16[1,768,384]{2,1,0:T(8,128)(2,1)S(1)}, u32[]{:S(2)}, u32[]{:S(2)}) collective-permute-start(bf16[1,768,384]{2,1,0:T(8,128)(2,1)S(1)} %get-tuple-element.428), channel_id=1, source_target_pairs={{4,0},{0,4},{5,1},{1,5},{6,2},{2,6},{7,3},{3,7},{12,8},{8,12},{13,... | collective-permute-start | bytes 1769480 | tf_op jit(solution)/shard_map/ppermute | solution.py:46
  150.6 16.5 %collective-permute-start.34 = (bf16[128,1536]{1,0:T(8,128)(2,1)S(1)}, bf16[128,1536]{1,0:T(8,128)(2,1)S(1)}, u32[]{:S(2)}, u32[]{:S(2)}) collective-permute-start(bf16[128,1536]{1,0:T(8,128)(2,1)S(1)} %get-tuple-element.437), channel_id=1, source_target_pairs={{8,0},{0,8},{9,1},{1,9},{10,2},{2,10},{11,3},{3,11},{12,4},{4,12},... | collective-permute-start | bytes 1179656 | tf_op jit(solution)/shard_map/ppermute | solution.py:46
  166.2 22.2 %collective-permute-start.37 = (bf16[1,768,384]{2,1,0:T(8,128)(2,1)S(1)}, bf16[1,768,384]{2,1,0:T(8,128)(2,1)S(1)}, u32[]{:S(2)}, u32[]{:S(2)}) collective-permute-start(bf16[1,768,384]{2,1,0:T(8,128)(2,1)S(1)} %get-tuple-element.456), channel_id=1, source_target_pairs={{4,0},{0,4},{5,1},{1,5},{6,2},{2,6},{7,3},{3,7},{12,8},{8,12},{13,... | collective-permute-start | bytes 1769480 | tf_op jit(solution)/shard_map/ppermute | solution.py:46
  192.1 23.1 %collective-permute-start.39 = (bf16[400,768]{1,0:T(8,128)(2,1)S(1)}, bf16[400,768]{1,0:T(8,128)(2,1)S(1)}, u32[]{:S(2)}, u32[]{:S(2)}) collective-permute-start(bf16[400,768]{1,0:T(8,128)(2,1)S(1)} %bitcast.67), channel_id=1, source_target_pairs={{8,0},{0,8},{9,1},{1,9},{10,2},{2,10},{11,3},{3,11},{12,4},{4,12},... | collective-permute-start | bytes 1843208 | tf_op jit(solution)/shard_map/ppermute | solution.py:46
  192.3 20.4 %collective-permute-start.40 = (bf16[128,1536]{1,0:T(8,128)(2,1)S(1)}, bf16[128,1536]{1,0:T(8,128)(2,1)S(1)}, u32[]{:S(2)}, u32[]{:S(2)}) collective-permute-start(bf16[128,1536]{1,0:T(8,128)(2,1)S(1)} %add_convert_fusion.1.own), channel_id=1, source_target_pairs={{1,0},{0,1},{3,2},{2,3},{5,4},{4,5},{7,6},{6,7},{9,8},{8,9},{11,10... | collective-permute-start | bytes 1179656 | tf_op jit(solution)/shard_map/ppermute | solution.py:46
  193.9 18.8 %collective-permute-start.41 = (bf16[384,384]{1,0:T(8,128)(2,1)S(1)}, bf16[384,384]{1,0:T(8,128)(2,1)S(1)}, u32[]{:S(2)}, u32[]{:S(2)}) collective-permute-start(bf16[384,384]{1,0:T(8,128)(2,1)S(1)} %bitcast.108), channel_id=1, source_target_pairs={{16,0},{0,16},{17,1},{1,17},{18,2},{2,18},{19,3},{3,19},{20,4},{4,... | collective-permute-start | bytes 884744 | tf_op jit(solution)/shard_map/ppermute | solution.py:46
  204.8 19.6 %collective-permute-start.50 = (bf16[2,192,384]{2,1,0:T(8,128)(2,1)S(1)}, bf16[2,192,384]{2,1,0:T(8,128)(2,1)S(1)}, u32[]{:S(2)}, u32[]{:S(2)}) collective-permute-start(bf16[2,192,384]{2,1,0:T(8,128)(2,1)S(1)} %get-tuple-element.511), channel_id=1, source_target_pairs={{8,0},{0,8},{9,1},{1,9},{10,2},{2,10},{11,3},{3,11},{12,4},{4,12},... | collective-permute-start | bytes 884744 | tf_op jit(solution)/shard_map/ppermute | solution.py:46
  215.9 18.4 %collective-permute-start.43 = (bf16[208,768]{1,0:T(8,128)(2,1)S(1)}, bf16[208,768]{1,0:T(8,128)(2,1)S(1)}, u32[]{:S(2)}, u32[]{:S(2)}) collective-permute-start(bf16[208,768]{1,0:T(8,128)(2,1)S(1)} %bitcast.89), channel_id=1, source_target_pairs={{16,0},{0,16},{17,1},{1,17},{18,2},{2,18},{19,3},{3,19},{20,4},{4,... | collective-permute-start | bytes 958472 | tf_op jit(solution)/shard_map/ppermute | solution.py:46
  218.4 16.6 %collective-permute-start.44 = (bf16[128,1536]{1,0:T(8,128)(2,1)S(1)}, bf16[128,1536]{1,0:T(8,128)(2,1)S(1)}, u32[]{:S(2)}, u32[]{:S(2)}) collective-permute-start(bf16[128,1536]{1,0:T(8,128)(2,1)S(1)} %get-tuple-element.493), channel_id=1, source_target_pairs={{4,0},{0,4},{5,1},{1,5},{6,2},{2,6},{7,3},{3,7},{12,8},{8,12},{13,... | collective-permute-start | bytes 1179656 | tf_op jit(solution)/shard_map/ppermute | solution.py:46
  220.5 22.1 %collective-permute-start.46 = (bf16[3,2,96,384]{3,2,1,0:T(8,128)(2,1)S(1)}, bf16[3,2,96,384]{3,2,1,0:T(8,128)(2,1)S(1)}, u32[]{:S(2)}, u32[]{:S(2)}) collective-permute-start(bf16[3,2,96,384]{3,2,1,0:T(8,128)(2,1)S(1)} %get-tuple-element.504), channel_id=1, source_target_pairs={{8,0},{0,8},{9,1},{1,9},{10,2},{2,10},{11,3},{3,11},{12,4},{4,12},... | collective-permute-start | bytes 1327112 | tf_op jit(solution)/shard_map/ppermute | solution.py:46
  220.6 25.4 %collective-permute-start.47 = (bf16[3,96,384]{2,1,0:T(8,128)(2,1)S(1)}, bf16[3,96,384]{2,1,0:T(8,128)(2,1)S(1)}, u32[]{:S(2)}, u32[]{:S(2)}) collective-permute-start(bf16[3,96,384]{2,1,0:T(8,128)(2,1)S(1)} %get-tuple-element.505), channel_id=1, source_target_pairs={{2,0},{0,2},{3,1},{1,3},{6,4},{4,6},{7,5},{5,7},{10,8},{8,10},{11,... | collective-permute-start | bytes 663560 | tf_op jit(solution)/shard_map/ppermute | solution.py:46
  225.0 19.8 %collective-permute-start.51 = (bf16[2,192,384]{2,1,0:T(8,128)(2,1)S(1)}, bf16[2,192,384]{2,1,0:T(8,128)(2,1)S(1)}, u32[]{:S(2)}, u32[]{:S(2)}) collective-permute-start(bf16[2,192,384]{2,1,0:T(8,128)(2,1)S(1)} %bitcast.106), channel_id=1, source_target_pairs={{16,0},{0,16},{17,1},{1,17},{18,2},{2,18},{19,3},{3,19},{20,4},{4,... | collective-permute-start | bytes 884744 | tf_op jit(solution)/shard_map/ppermute | solution.py:46
  (44 other events, 343.1 us)
